TPU v7x, 256 devices: a whole 4x4x8 slice. The times are simulated.
256 devices in a mesh: slab: 16 (over y, z_lo), chan: 16 (over z_hi, x, core).
Axes of the slice: x: 4, y: 4, z: 8 (z_hi: 2, z_lo: 4; z = z_hi * 4 + z_lo), core: 2. Of those that a mesh axis runs over, the one named last changes fastest.
Arguments:
- saved_input: float32 [512, 96, 256], P('chan', 'slab'), may hold values from -6 to 6
- pre_first: float32 [512, 96, 256], P('chan', 'slab'), may hold values from -8 to 8
- pre_second: float32 [512, 96, 256], P('chan', 'slab'), may hold values from -8 to 8
- out_grad: float32 [512, 96, 256], P('chan', 'slab'), may hold values from -12 to 12
- weight_first: float32 [27, 512, 512], P(None, 'chan'), may hold values from -0.0546875 to 0.0546875
- weight_second: float32 [27, 512, 512], P(None, 'chan'), may hold values from -0.0546875 to 0.0546875
Outputs:
- input_grad: float32 [512, 96, 256], P('chan', 'slab')
- grad_weight_first: float32 [27, 512, 512], P(None, 'chan', 'slab')
- grad_weight_second: float32 [27, 512, 512], P(None, 'chan', 'slab')
All inputs are finite; a program needn't handle non-finite values.
Results may differ from a plain program's by a relative error of at most 0.00013.
Values sent between devices are 32-bit elements; how exact they have to be, the bound alone decides.
No kernel may reach another device: no remote copies, remote signals or barrier semaphores. Data moves between devices by JAX's collectives and lax.ppermute only.
A program may use at most 128 MiB of HBM per device.

v0:
```python
import math

import jax
import jax.numpy as jnp
from jax import lax
from jax.experimental import pallas as pl
from jax.experimental.pallas import tpu as pltpu
from jax.sharding import PartitionSpec as P

SIDE = 16
AREA = 256
SLABS = 16
SHIFTS = [(b, c) for b in (-1, 0, 1) for c in (-1, 0, 1)]
F32 = jnp.float32
BF16 = jnp.bfloat16
VM = pl.BlockSpec(memory_space=pltpu.VMEM)
SM = pl.BlockSpec(memory_space=pltpu.SMEM)


def slope_of(values):
    sigma = jax.nn.sigmoid(values)
    return sigma * (1.0 + values * (1.0 - sigma))


def call(kernel, out_shape, scratch, args, n_smem=0, flops=0, name=None):
    many = isinstance(out_shape, list)
    moved = sum(a.size * a.dtype.itemsize for a in args)
    moved += sum(o.size * o.dtype.itemsize for o in (out_shape if many else [out_shape]))
    return pl.pallas_call(
        kernel,
        out_shape=out_shape,
        in_specs=[SM] * n_smem + [VM] * (len(args) - n_smem),
        out_specs=[VM] * len(out_shape) if many else VM,
        scratch_shapes=scratch,
        compiler_params=pltpu.CompilerParams(vmem_limit_bytes=40 << 20),
        cost_estimate=pl.CostEstimate(flops=flops, bytes_accessed=moved, transcendentals=0),
        name=name,
    )(*args)


def shape(*dims, dtype=F32):
    return jax.ShapeDtypeStruct(dims, dtype)


def split(value):
    high = value.astype(BF16)
    return high, (value - high.astype(F32)).astype(BF16)


def moved_cells(plane, row_step, col_step):
    cells = lax.broadcasted_iota(jnp.int32, plane.shape, 1)
    if col_step:
        col = cells % SIDE + col_step
        plane = jnp.where((col >= 0) & (col < SIDE), pltpu.roll(plane, -col_step % AREA, 1), 0.0)
    if row_step:
        row = cells // SIDE + row_step
        plane = jnp.where((row >= 0) & (row < SIDE), pltpu.roll(plane, -row_step * SIDE % AREA, 1), 0.0)
    return plane


def scaled_kernel(pre_ref, grad_ref, out_ref):
    for p in range(out_ref.shape[0]):
        out_ref[p] = grad_ref[:, p, :] * slope_of(pre_ref[:, p, :])


def scaled(pre, grad):
    channels, planes, area = pre.shape
    return call(scaled_kernel, shape(planes, channels, area), [], [pre, grad], name="scaled")


def prepare_kernel(pre_ref, saved_ref, low_ref, high_ref, w1_ref, w2_ref,
                   h_hi, h_lo, x_hi, x_lo, w1_hi, w1_lo, w2_hi, w2_lo, slope_ref, rows):
    planes = slope_ref.shape[0]
    channels = slope_ref.shape[1]
    for n, (own, hi_ref, lo_ref) in enumerate(((pre_ref, h_hi, h_lo), (saved_ref, x_hi, x_lo))):
        rows[0] = low_ref[n]
        rows[planes + 1] = high_ref[n]
        for p in range(planes):
            rows[p + 1] = own[:, p, :]
            if n == 0:
                slope_ref[p] = slope_of(own[:, p, :])

        def one_plane(q, _):
            plane = rows[q]
            if n == 0:
                plane = plane * jax.nn.sigmoid(plane)
            lanes = pl.ds(pl.multiple_of(q * AREA, AREA), AREA)
            for s, (b, c) in enumerate(SHIFTS):
                hi, lo = split(moved_cells(plane, b, c))
                hi_ref[s * channels:(s + 1) * channels, lanes] = hi
                lo_ref[s * channels:(s + 1) * channels, lanes] = lo
            return 0

        lax.fori_loop(0, planes + 2, one_plane, 0)
    for source, hi_ref, lo_ref in ((w2_ref, w2_hi, w2_lo), (w1_ref, w1_hi, w1_lo)):

        def one_tap(t, _):
            at = pl.ds(pl.multiple_of(t * channels, channels), channels)
            hi, lo = split(source[t])
            hi_ref[at, :] = hi
            lo_ref[at, :] = lo
            return 0

        lax.fori_loop(0, source.shape[0], one_tap, 0)


def prepared(pre, saved, low, high, w1, w2):
    channels, planes, area = pre.shape
    taps, _, total = w1.shape
    tall = shape(len(SHIFTS) * channels, (planes + 2) * area, dtype=BF16)
    flat = shape(taps * channels, total, dtype=BF16)
    outs = [tall] * 4 + [flat] * 4 + [shape(planes, channels, area)]
    return call(prepare_kernel, outs, [pltpu.VMEM((planes + 2, channels, area), F32)],
                [pre, saved, low, high, w1, w2], name="prepared")


def gather_blocks(spots, pieces, g_hi, g_lo):
    planes = pieces[0].shape[0]
    for k, piece in enumerate(pieces):
        spot = spots[k]

        def one(p, _):
            lanes = pl.ds(pl.multiple_of(p * AREA, AREA), AREA)
            hi, lo = split(piece[p])
            g_hi[spot, :, lanes] = hi
            g_lo[spot, :, lanes] = lo
            return 0

        lax.fori_loop(0, planes, one, 0, unroll=True)


def data_kernel(n_pieces, spots, *refs):
    pieces, (w_hi, w_lo, own_ref, before_ref, after_ref, g_hi, g_lo, sums) = refs[:n_pieces], refs[n_pieces:]
    planes, channels, _ = own_ref.shape
    total = w_hi.shape[1]
    third = len(SHIFTS) * channels
    gather_blocks(spots, pieces, g_hi, g_lo)
    sums[...] = jnp.zeros_like(sums)

    def one_plane(p, _):
        lanes = pl.ds(pl.multiple_of(p * AREA, AREA), AREA)
        hi = g_hi[:, :, lanes].reshape(total, AREA)
        lo = g_lo[:, :, lanes].reshape(total, AREA)
        for a in range(3):
            w_a = w_hi[a * third:(a + 1) * third, :]
            out = jnp.dot(w_a, hi, preferred_element_type=F32)
            out += jnp.dot(w_a, lo, preferred_element_type=F32)
            out += jnp.dot(w_lo[a * third:(a + 1) * third, :], hi, preferred_element_type=F32)
            sums[p + a] += out
        return 0

    lax.fori_loop(0, planes, one_plane, 0)

    def spread(q):
        total_plane = jnp.zeros((channels, AREA), F32)
        for b in (-1, 0, 1):
            row = jnp.zeros((channels, AREA), F32)
            for c in (-1, 0, 1):
                s = SHIFTS.index((b, c)) * channels
                row += moved_cells(sums[q, s:s + channels, :], 0, -c)
            total_plane += moved_cells(row, -b, 0)
        return total_plane

    before_ref[...] = spread(0)
    after_ref[...] = spread(planes + 1)

    def one_out(p, _):
        own_ref[p] = spread(p + 1)
        return 0

    lax.fori_loop(0, planes, one_out, 0)


def data_gradient(spots, pieces, w_hi, w_lo):
    planes, channels, area = pieces[0].shape
    rows, total = w_hi.shape
    blocks = total // channels
    kernel = lambda *refs: data_kernel(len(pieces), *refs)
    outs = [shape(planes, channels, area), shape(channels, area), shape(channels, area)]
    scratch = [pltpu.VMEM((blocks, channels, planes * area), BF16)] * 2
    scratch += [pltpu.VMEM((planes + 2, rows // 3, area), F32)]
    return call(kernel, outs, scratch, [spots, *pieces, w_hi, w_lo], 1, 6 * rows * total * planes * area,
                name="data_gradient")


def filter_kernel(n_pieces, spots, *refs):
    pieces, (i_hi, i_lo), outs, (g_hi, g_lo) = (
        refs[:n_pieces], refs[n_pieces:n_pieces + 2], refs[n_pieces + 2:-2], refs[-2:])
    planes = pieces[0].shape[0]
    total = g_hi.shape[0] * g_hi.shape[1]
    width = total // len(outs)
    gather_blocks(spots, pieces, g_hi, g_lo)
    for out in outs:
        out[...] = jnp.zeros_like(out)

    def one_plane(p, _):
        lanes = pl.ds(pl.multiple_of(p * AREA, AREA), AREA)
        hi = g_hi[:, :, lanes].reshape(total, AREA)
        lo = g_lo[:, :, lanes].reshape(total, AREA)
        windows = [pl.ds(pl.multiple_of((p + a) * AREA, AREA), AREA) for a in range(3)]
        left_hi = jnp.concatenate([i_hi[:, w] for w in windows], 0)
        left_lo = jnp.concatenate([i_lo[:, w] for w in windows], 0)
        dims = (((1,), (1,)), ((), ()))
        part = lax.dot_general(left_hi, hi, dims, preferred_element_type=F32)
        part += lax.dot_general(left_hi, lo, dims, preferred_element_type=F32)
        part += lax.dot_general(left_lo, hi, dims, preferred_element_type=F32)
        for d, out in enumerate(outs):
            out[...] += part[:, d * width:(d + 1) * width]
        return 0

    lax.fori_loop(0, planes, one_plane, 0)


def filter_gradient(spots, pieces, i_hi, i_lo, parts):
    planes, channels, area = pieces[0].shape
    rows = 3 * i_hi.shape[0]
    total = channels * len(pieces)
    kernel = lambda *refs: filter_kernel(len(pieces), *refs)
    outs = [shape(rows, total // parts)] * parts
    scratch = [pltpu.VMEM((len(pieces), channels, planes * area), BF16)] * 2
    return call(kernel, outs, scratch, [spots, *pieces, i_hi, i_lo], 1, 6 * rows * total * planes * area,
                name="filter_gradient")


def turned_kernel(spots, a, b, c, d, *refs):
    outs, turned = refs[:-1], refs[-1]
    turned[...] = (a[...] + b[...] + c[...] + d[...]).T
    height = outs[0].shape[0]
    for k, out in enumerate(outs):
        out[...] = turned[pl.ds(pl.multiple_of(spots[k] * height, height), height), :]


def turned_sum(spots, parts):
    rows, width = parts[0].shape
    return call(turned_kernel, [shape(width // 4, rows)] * 4, [pltpu.VMEM((width, rows), F32)],
                [spots, *parts], 1, name="turned_sum")


def last_kernel(scale, a, b, c, d, out):
    out[...] = ((a[...] + b[...] + c[...] + d[...]) * scale).T


def last_sum(parts, scale):
    height, rows = parts[0].shape
    return call(lambda *refs: last_kernel(scale, *refs), shape(rows, height), [], parts, name="last_sum")


def first_kernel(own, before, after, slope, out):
    planes = out.shape[0]
    for p in range(planes):
        value = own[p]
        if p == 0:
            value = value + before[...]
        if p == planes - 1:
            value = value + after[...]
        out[p] = value * slope[p]


def input_kernel(own, before, after, out):
    planes = own.shape[0]
    for p in range(planes):
        value = own[p]
        if p == 0:
            value = value + before[...]
        if p == planes - 1:
            value = value + after[...]
        out[:, p, :] = value


FAR = [(i, (i + 8) % 16) for i in range(16)]
TWIN = [(i, i ^ 1) for i in range(16)]
UP = [(i, i + 1) for i in range(SLABS - 1)]
DOWN = [(i + 1, i) for i in range(SLABS - 1)]


def along_x(d):
    return [(i, (i & 9) | ((i + 2 * d) & 6)) for i in range(16)]


def along_y(d):
    return [(i, (i + 4 * d) % 16) for i in range(16)]


def along_z(d):
    return [(i, (i & 12) | ((i + d) & 3)) for i in range(16)]


def send(value, moves, axis="chan"):
    return lax.ppermute(value, axis, moves)


def gathered(own):
    me = lax.axis_index("chan")
    far = send(own, FAR)
    pieces, ids = [own, far], [me, me ^ 8]
    for value, shard in ((own, me), (far, me ^ 8)):
        for d in (1, 3, 2):
            pieces.append(send(value, along_x(d)))
            ids.append((shard & 9) | ((shard - 2 * d) & 6))
    pieces += [send(piece, TWIN) for piece in pieces]
    ids += [shard ^ 1 for shard in ids]
    return pieces, jnp.stack(ids).astype(jnp.int32)


def edges(before, after):
    return send(after, UP, "slab"), send(before, DOWN, "slab")


def owner_sum(parts, spots, scale):
    arrived = [parts[0]] + [send(parts[d], along_y(d), "slab") for d in (2, 1, 3)]
    rows = turned_sum(spots, arrived)
    arrived = [rows[0]] + [send(rows[d], along_z(d), "slab") for d in (1, 2, 3)]
    return last_sum(arrived, scale)


def per_device(saved_input, pre_first, pre_second, out_grad, weight_first, weight_second):
    channels, planes, area = saved_input.shape
    taps, _, total = weight_first.shape
    scale = 1.0 / math.sqrt(planes * SLABS * area)
    slab = lax.axis_index("slab")
    y_spot = slab // 4
    z_spots = ((slab + jnp.arange(4)) % 4).astype(jnp.int32)

    second_grad = scaled(pre_second, out_grad)
    pieces, ids = gathered(second_grad)
    quarters = (((ids // 4 - y_spot) % 4) * 4 + ids % 4).astype(jnp.int32)

    low = send(jnp.stack([pre_first[:, planes - 1], saved_input[:, planes - 1]]), UP, "slab")
    high = send(jnp.stack([pre_first[:, 0], saved_input[:, 0]]), DOWN, "slab")
    h_hi, h_lo, x_hi, x_lo, w1_hi, w1_lo, w2_hi, w2_lo, slope = prepared(
        pre_first, saved_input, low, high, weight_first, weight_second)

    own, before, after = data_gradient(ids, pieces, w2_hi, w2_lo)
    first_grad = call(first_kernel, shape(planes, channels, area), [],
                      [own, *edges(before, after), slope], name="first_grad")
    second_parts = filter_gradient(quarters, pieces, h_hi, h_lo, 4)

    pieces, ids = gathered(first_grad)
    second_weights = owner_sum(second_parts, z_spots, scale)
    first_parts = filter_gradient(quarters, pieces, x_hi, x_lo, 4)
    first_weights = owner_sum(first_parts, z_spots, scale)
    own, before, after = data_gradient(ids, pieces, w1_hi, w1_lo)
    input_grad = call(input_kernel, shape(channels, planes, area), [], [own, *edges(before, after)], name="input_grad")
    return (input_grad, first_weights.reshape(taps, channels, -1), second_weights.reshape(taps, channels, -1))


def solution(mesh):
    in_specs = (
        P("chan", "slab", None),
        P("chan", "slab", None),
        P("chan", "slab", None),
        P("chan", "slab", None),
        P(None, "chan", None),
        P(None, "chan", None),
    )
    out_specs = (P("chan", "slab", None), P(None, "chan", "slab"), P(None, "chan", "slab"))
    return jax.shard_map(
        per_device, mesh=mesh, in_specs=in_specs, out_specs=out_specs, check_vma=False
    )
```

profile of v0, /device:TPU:8, one launch (start us, length us, event | category | flops | bytes accessed | tf_op | source)
XLA Modules:
  0.0 182.0 jit_solution(18352372137861624240)
XLA Ops:
  1.5 4.0 %collective-permute-start.15 = (f32[2,32,256]{2,1,0:T(8,128)S(1)}, f32[2,32,256]{2,1,0:T(8,128)S(1)}, u32[]{:S(2)}, u32[]{:S(2)}) collective-permute-start(f32[2,32,256]{2,1,0:T(8,128)S(1)} %pad_maximum_fusion), channel_id=1, source_target_pairs={{0,16},{16,32},{32,48},{48,64},{64,80},{80,96},{96,112},{112,128},... | collective-permute-start | bytes 196616 | tf_op jit(solution)/shard_map/ppermute | solution.py:289
  5.5 4.7 %collective-permute-start.16 = (f32[2,32,256]{2,1,0:T(8,128)S(1)}, f32[2,32,256]{2,1,0:T(8,128)S(1)}, u32[]{:S(2)}, u32[]{:S(2)}) collective-permute-start(f32[2,32,256]{2,1,0:T(8,128)S(1)} %pad_maximum_fusion.1), channel_id=1, source_target_pairs={{16,0},{32,16},{48,32},{64,48},{80,64},{96,80},{112,96},{128,112},... | collective-permute-start | bytes 196616 | tf_op jit(solution)/shard_map/ppermute | solution.py:289
  12.7 3.1 %collective-permute-start.3 = (f32[6,32,256]{2,1,0:T(8,128)S(1)}, f32[6,32,256]{2,1,0:T(8,128)S(1)}, u32[]{:S(2)}, u32[]{:S(2)}) collective-permute-start(f32[6,32,256]{2,1,0:T(8,128)S(1)} %scaled.1.refs_1_), channel_id=1, source_target_pairs={{0,4},{1,5},{2,6},{3,7},{4,0},{5,1},{6,2},{7,3},{8,12},{9,13},{10,... | collective-permute-start | bytes 589832 | tf_op jit(solution)/shard_map/ppermute | solution.py:289
  17.0 7.2 %collective-permute-start = (f32[6,32,256]{2,1,0:T(8,128)S(1)}, f32[6,32,256]{2,1,0:T(8,128)}, u32[]{:S(2)}, u32[]{:S(2)}) collective-permute-start(f32[6,32,256]{2,1,0:T(8,128)S(1)} %scaled.1.refs_1_), channel_id=1, source_target_pairs={{0,8},{1,9},{2,10},{3,11},{4,12},{5,13},{6,14},{7,15},{8,0},{9,1},... | collective-permute-start | bytes 589832 | tf_op jit(solution)/shard_map/ppermute | solution.py:289
  27.0 5.3 %collective-permute-done.refs_2_ = f32[6,32,256]{2,1,0:T(8,128)} collective-permute-done((f32[6,32,256]{2,1,0:T(8,128)S(1)}, f32[6,32,256]{2,1,0:T(8,128)}, u32[]{:S(2)}, u32[]{:S(2)}) %collective-permute-start) | collective-permute-done | bytes 196640 | tf_op jit(solution)/shard_map/ppermute | solution.py:289
  41.4 2.7 %collective-permute-done.4.refs_6_ = f32[6,32,256]{2,1,0:T(8,128)} collective-permute-done((f32[6,32,256]{2,1,0:T(8,128)}, f32[6,32,256]{2,1,0:T(8,128)}, u32[]{:S(2)}, u32[]{:S(2)}) %collective-permute-start.4) | collective-permute-done | bytes 196640 | tf_op jit(solution)/shard_map/ppermute | solution.py:289
  46.0 3.9 %prepared.1 = (bf16[288,2048]{1,0:T(8,128)(2,1)S(1)}, bf16[288,2048]{1,0:T(8,128)(2,1)S(1)}, bf16[288,2048]{1,0:T(8,128)(2,1)S(1)}, bf16[288,2048]{1,0:T(8,128)(...) custom-call(f32[32,6,256]{2,1,0:T(8,128)S(1)} %copy.11.pre_ref, ...), custom_call_target="tpu_custom_call" | custom-call | bytes 12517376 | tf_op jit(solution)/shard_map/prepared/pallas_call | solution.py:29
  53.0 9.4 %data_gradient.2 = (f32[6,32,256]{2,1,0:T(8,128)S(1)}, f32[32,256]{1,0:T(8,128)S(1)}, f32[32,256]{1,0:T(8,128)S(1)}) custom-call(s32[16]{0:T(128)S(1)} %stack.90.refs_0_, f32[6,32,256]{2,1,0:T(8,128)S(1)} %scaled.1.refs_1_, f32[6,32,256]{2,1,0:T(8,128)} %collective-permute-done.refs_2_, f32[6,32,256]{2,1,0:T(8,128)} %collective-permute-done.1.refs_3_, ...), custom_call_target="tpu_custom_call" | custom-call | flops 4076863488 | bytes 5177408 | tf_op jit(solution)/shard_map/data_gradient/pallas_call | solution.py:29
  64.4 6.6 %collective-permute-start.18 = (f32[32,256]{1,0:T(8,128)S(1)}, f32[32,256]{1,0:T(8,128)S(1)}, u32[]{:S(2)}, u32[]{:S(2)}) collective-permute-start(f32[32,256]{1,0:T(8,128)S(1)} %get-tuple-element.38), channel_id=1, source_target_pairs={{16,0},{32,16},{48,32},{64,48},{80,64},{96,80},{112,96},{128,112},... | collective-permute-start | bytes 98312 | tf_op jit(solution)/shard_map/ppermute | solution.py:289
  72.6 3.1 %collective-permute-start.19 = (f32[6,32,256]{2,1,0:T(8,128)S(1)}, f32[6,32,256]{2,1,0:T(8,128)}, u32[]{:S(2)}, u32[]{:S(2)}) collective-permute-start(f32[6,32,256]{2,1,0:T(8,128)S(1)} %first_grad.1.refs_1_), channel_id=1, source_target_pairs={{0,8},{1,9},{2,10},{3,11},{4,12},{5,13},{6,14},{7,15},{8,0},{9,1},... | collective-permute-start | bytes 589832 | tf_op jit(solution)/shard_map/ppermute | solution.py:289
  79.1 8.1 %collective-permute-done.19.refs_2_ = f32[6,32,256]{2,1,0:T(8,128)} collective-permute-done((f32[6,32,256]{2,1,0:T(8,128)S(1)}, f32[6,32,256]{2,1,0:T(8,128)}, u32[]{:S(2)}, u32[]{:S(2)}) %collective-permute-start.19) | collective-permute-done | bytes 196640 | tf_op jit(solution)/shard_map/ppermute | solution.py:289
  92.9 2.7 %collective-permute-done.25.refs_8_ = f32[6,32,256]{2,1,0:T(8,128)S(1)} collective-permute-done((f32[6,32,256]{2,1,0:T(8,128)}, f32[6,32,256]{2,1,0:T(8,128)S(1)}, u32[]{:S(2)}, u32[]{:S(2)}) %collective-permute-start.25) | collective-permute-done | bytes 196640 | tf_op jit(solution)/shard_map/ppermute | solution.py:289
  104.9 7.5 %filter_gradient.3 = (f32[864,128]{1,0:T(8,128)S(1)}, f32[864,128]{1,0:T(8,128)S(1)}, f32[864,128]{1,0:T(8,128)S(1)}, f32[864,128]{1,0:T(8,128)S(1)}) custom-call(s32[16]{0:T(128)S(1)} %fusion.refs_0_, f32[6,32,256]{2,1,0:T(8,128)S(1)} %scaled.1.refs_1_, f32[6,32,256]{2,1,0:T(8,128)} %collective-permute-done.refs_2_, ...), custom_call_target="tpu_custom_call" | custom-call | flops 4076863488 | bytes 7274560 | tf_op jit(solution)/shard_map/filter_gradient/pallas_call | solution.py:29
  112.4 2.9 %collective-permute-start.42 = (f32[864,128]{1,0:T(8,128)S(1)}, f32[864,128]{1,0:T(8,128)S(1)}, u32[]{:S(2)}, u32[]{:S(2)}) collective-permute-start(f32[864,128]{1,0:T(8,128)S(1)} %get-tuple-element.58), channel_id=1, source_target_pairs={{0,128},{16,144},{32,160},{48,176},{64,192},{80,208},{96,224},{112... | collective-permute-start | bytes 1327112 | tf_op jit(solution)/shard_map/ppermute | solution.py:289
  117.7 6.8 %filter_gradient.2 = (f32[864,128]{1,0:T(8,128)S(1)}, f32[864,128]{1,0:T(8,128)S(1)}, f32[864,128]{1,0:T(8,128)S(1)}, f32[864,128]{1,0:T(8,128)S(1)}) custom-call(s32[16]{0:T(128)S(1)} %fusion.refs_0_, f32[6,32,256]{2,1,0:T(8,128)S(1)} %first_grad.1.refs_1_, f32[6,32,256]{2,1,0:T(8,128)} %collective-permute-done.19.refs_2_, ...), custom_call_target="tpu_custom_call" | custom-call | flops 4076863488 | bytes 7274560 | tf_op jit(solution)/shard_map/filter_gradient/pallas_call | solution.py:29
  129.3 8.7 %collective-permute-done.43.c = f32[864,128]{1,0:T(8,128)S(1)} collective-permute-done((f32[864,128]{1,0:T(8,128)S(1)}, f32[864,128]{1,0:T(8,128)S(1)}, u32[]{:S(2)}, u32[]{:S(2)}) %collective-permute-start.43) | collective-permute-done | bytes 442400 | tf_op jit(solution)/shard_map/ppermute | solution.py:289
  138.9 4.3 %collective-permute-start.46 = (f32[32,864]{1,0:T(8,128)S(1)}, f32[32,864]{1,0:T(8,128)S(1)}, u32[]{:S(2)}, u32[]{:S(2)}) collective-permute-start(f32[32,864]{1,0:T(8,128)S(1)} %get-tuple-element.63), channel_id=1, source_target_pairs={{0,32},{16,48},{32,0},{48,16},{64,96},{80,112},{96,64},{112,80},{1... | collective-permute-start | bytes 331784 | tf_op jit(solution)/shard_map/ppermute | solution.py:289
  143.3 2.8 %collective-permute-done.36.b = f32[864,128]{1,0:T(8,128)S(1)} collective-permute-done((f32[864,128]{1,0:T(8,128)S(1)}, f32[864,128]{1,0:T(8,128)S(1)}, u32[]{:S(2)}, u32[]{:S(2)}) %collective-permute-start.36) | collective-permute-done | bytes 442400 | tf_op jit(solution)/shard_map/ppermute | solution.py:289
  146.0 4.7 %collective-permute-start.47 = (f32[32,864]{1,0:T(8,128)S(1)}, f32[32,864]{1,0:T(8,128)S(1)}, u32[]{:S(2)}, u32[]{:S(2)}) collective-permute-start(f32[32,864]{1,0:T(8,128)S(1)} %get-tuple-element.64), channel_id=1, source_target_pairs={{0,48},{16,0},{32,16},{48,32},{64,112},{80,64},{96,80},{112,96},{1... | collective-permute-start | bytes 331784 | tf_op jit(solution)/shard_map/ppermute | solution.py:289
  150.7 5.9 %collective-permute-done.37.c = f32[864,128]{1,0:T(8,128)S(1)} collective-permute-done((f32[864,128]{1,0:T(8,128)S(1)}, f32[864,128]{1,0:T(8,128)S(1)}, u32[]{:S(2)}, u32[]{:S(2)}) %collective-permute-start.37) | collective-permute-done | bytes 442400 | tf_op jit(solution)/shard_map/ppermute | solution.py:289
  157.5 4.3 %collective-permute-start.40 = (f32[32,864]{1,0:T(8,128)S(1)}, f32[32,864]{1,0:T(8,128)S(1)}, u32[]{:S(2)}, u32[]{:S(2)}) collective-permute-start(f32[32,864]{1,0:T(8,128)S(1)} %get-tuple-element.53), channel_id=1, source_target_pairs={{0,32},{16,48},{32,0},{48,16},{64,96},{80,112},{96,64},{112,80},{1... | collective-permute-start | bytes 331784 | tf_op jit(solution)/shard_map/ppermute | solution.py:289
  161.9 8.1 %data_gradient.3 = (f32[6,32,256]{2,1,0:T(8,128)S(1)}, f32[32,256]{1,0:T(8,128)S(1)}, f32[32,256]{1,0:T(8,128)S(1)}) custom-call(s32[16]{0:T(128)S(1)} %stack.90.refs_0_, f32[6,32,256]{2,1,0:T(8,128)S(1)} %first_grad.1.refs_1_, f32[6,32,256]{2,1,0:T(8,128)} %collective-permute-done.19.refs_2_, f32[6,32,256]{2,1,0:T(8,128)} %collective-permute-done.20.refs_3_, ...), custom_call_target="tpu_custom_call" | custom-call | flops 4076863488 | bytes 5177408 | tf_op jit(solution)/shard_map/data_gradient/pallas_call | solution.py:29
  170.0 3.9 %collective-permute-start.34 = (f32[32,256]{1,0:T(8,128)S(1)}, f32[32,256]{1,0:T(8,128)S(1)}, u32[]{:S(2)}, u32[]{:S(2)}) collective-permute-start(f32[32,256]{1,0:T(8,128)S(1)} %get-tuple-element.43), channel_id=1, source_target_pairs={{0,16},{16,32},{32,48},{48,64},{64,80},{80,96},{96,112},{112,128},... | collective-permute-start | bytes 98312 | tf_op jit(solution)/shard_map/ppermute | solution.py:289
  174.0 4.6 %collective-permute-start.35 = (f32[32,256]{1,0:T(8,128)S(1)}, f32[32,256]{1,0:T(8,128)S(1)}, u32[]{:S(2)}, u32[]{:S(2)}) collective-permute-start(f32[32,256]{1,0:T(8,128)S(1)} %get-tuple-element.44), channel_id=1, source_target_pairs={{16,0},{32,16},{48,32},{64,48},{80,64},{96,80},{112,96},{128,112},... | collective-permute-start | bytes 98312 | tf_op jit(solution)/shard_map/ppermute | solution.py:289
  (165 shorter events, 55.2 us)
Async XLA Ops:
  1.5 22.7 %collective-permute-start.15 = (f32[2,32,256]{2,1,0:T(8,128)S(1)}, f32[2,32,256]{2,1,0:T(8,128)S(1)}, u32[]{:S(2)}, u32[]{:S(2)}) collective-permute-start(f32[2,32,256]{2,1,0:T(8,128)S(1)} %pad_maximum_fusion), channel_id=1, source_target_pairs={{0,16},{16,32},{32,48},{48,64},{64,80},{80,96},{96,112},{112,128},... | collective-permute-start | bytes 196616 | tf_op jit(solution)/shard_map/ppermute | solution.py:289
  5.5 18.7 %collective-permute-start.16 = (f32[2,32,256]{2,1,0:T(8,128)S(1)}, f32[2,32,256]{2,1,0:T(8,128)S(1)}, u32[]{:S(2)}, u32[]{:S(2)}) collective-permute-start(f32[2,32,256]{2,1,0:T(8,128)S(1)} %pad_maximum_fusion.1), channel_id=1, source_target_pairs={{16,0},{32,16},{48,32},{64,48},{80,64},{96,80},{112,96},{128,112},... | collective-permute-start | bytes 196616 | tf_op jit(solution)/shard_map/ppermute | solution.py:289
  17.0 15.3 %collective-permute-start = (f32[6,32,256]{2,1,0:T(8,128)S(1)}, f32[6,32,256]{2,1,0:T(8,128)}, u32[]{:S(2)}, u32[]{:S(2)}) collective-permute-start(f32[6,32,256]{2,1,0:T(8,128)S(1)} %scaled.1.refs_1_), channel_id=1, source_target_pairs={{0,8},{1,9},{2,10},{3,11},{4,12},{5,13},{6,14},{7,15},{8,0},{9,1},... | collective-permute-start | bytes 589832 | tf_op jit(solution)/shard_map/ppermute | solution.py:289
  37.3 15.7 %collective-permute-start.8 = (f32[6,32,256]{2,1,0:T(8,128)}, f32[6,32,256]{2,1,0:T(8,128)}, u32[]{:S(2)}, u32[]{:S(2)}) collective-permute-start(f32[6,32,256]{2,1,0:T(8,128)} %collective-permute-done.refs_2_), channel_id=1, source_target_pairs={{0,1},{1,0},{2,3},{3,2},{4,5},{5,4},{6,7},{7,6},{8,9},{9,8},{10,11... | collective-permute-start | bytes 589832 | tf_op jit(solution)/shard_map/ppermute | solution.py:289
  38.0 15.0 %collective-permute-start.9 = (f32[6,32,256]{2,1,0:T(8,128)}, f32[6,32,256]{2,1,0:T(8,128)}, u32[]{:S(2)}, u32[]{:S(2)}) collective-permute-start(f32[6,32,256]{2,1,0:T(8,128)} %collective-permute-done.1.refs_3_), channel_id=1, source_target_pairs={{0,1},{1,0},{2,3},{3,2},{4,5},{5,4},{6,7},{7,6},{8,9},{9,8},{10,11... | collective-permute-start | bytes 589832 | tf_op jit(solution)/shard_map/ppermute | solution.py:289
  72.6 14.6 %collective-permute-start.19 = (f32[6,32,256]{2,1,0:T(8,128)S(1)}, f32[6,32,256]{2,1,0:T(8,128)}, u32[]{:S(2)}, u32[]{:S(2)}) collective-permute-start(f32[6,32,256]{2,1,0:T(8,128)S(1)} %first_grad.1.refs_1_), channel_id=1, source_target_pairs={{0,8},{1,9},{2,10},{3,11},{4,12},{5,13},{6,14},{7,15},{8,0},{9,1},... | collective-permute-start | bytes 589832 | tf_op jit(solution)/shard_map/ppermute | solution.py:289
  75.7 14.3 %collective-permute-start.22 = (f32[6,32,256]{2,1,0:T(8,128)S(1)}, f32[6,32,256]{2,1,0:T(8,128)S(1)}, u32[]{:S(2)}, u32[]{:S(2)}) collective-permute-start(f32[6,32,256]{2,1,0:T(8,128)S(1)} %first_grad.1.refs_1_), channel_id=1, source_target_pairs={{0,4},{1,5},{2,6},{3,7},{4,0},{5,1},{6,2},{7,3},{8,12},{9,13},{10,... | collective-permute-start | bytes 589832 | tf_op jit(solution)/shard_map/ppermute | solution.py:289
  92.2 23.2 %collective-permute-start.27 = (f32[6,32,256]{2,1,0:T(8,128)}, f32[6,32,256]{2,1,0:T(8,128)S(1)}, u32[]{:S(2)}, u32[]{:S(2)}) collective-permute-start(f32[6,32,256]{2,1,0:T(8,128)} %collective-permute-done.19.refs_2_), channel_id=1, source_target_pairs={{0,1},{1,0},{2,3},{3,2},{4,5},{5,4},{6,7},{7,6},{8,9},{9,8},{10,11... | collective-permute-start | bytes 589832 | tf_op jit(solution)/shard_map/ppermute | solution.py:289
  92.5 19.9 %collective-permute-start.28 = (f32[6,32,256]{2,1,0:T(8,128)}, f32[6,32,256]{2,1,0:T(8,128)S(1)}, u32[]{:S(2)}, u32[]{:S(2)}) collective-permute-start(f32[6,32,256]{2,1,0:T(8,128)} %collective-permute-done.20.refs_3_), channel_id=1, source_target_pairs={{0,1},{1,0},{2,3},{3,2},{4,5},{5,4},{6,7},{7,6},{8,9},{9,8},{10,11... | collective-permute-start | bytes 589832 | tf_op jit(solution)/shard_map/ppermute | solution.py:289
  95.6 20.0 %collective-permute-start.33 = (f32[6,32,256]{2,1,0:T(8,128)S(1)}, f32[6,32,256]{2,1,0:T(8,128)S(1)}, u32[]{:S(2)}, u32[]{:S(2)}) collective-permute-start(f32[6,32,256]{2,1,0:T(8,128)S(1)} %collective-permute-done.25.refs_8_), channel_id=1, source_target_pairs={{0,1},{1,0},{2,3},{3,2},{4,5},{5,4},{6,7},{7,6},{8,9},{9,8},{10,11... | collective-permute-start | bytes 589832 | tf_op jit(solution)/shard_map/ppermute | solution.py:289
  96.6 21.1 %collective-permute-start.32 = (f32[6,32,256]{2,1,0:T(8,128)S(1)}, f32[6,32,256]{2,1,0:T(8,128)S(1)}, u32[]{:S(2)}, u32[]{:S(2)}) collective-permute-start(f32[6,32,256]{2,1,0:T(8,128)S(1)} %collective-permute-done.24.refs_7_), channel_id=1, source_target_pairs={{0,1},{1,0},{2,3},{3,2},{4,5},{5,4},{6,7},{7,6},{8,9},{9,8},{10,11... | collective-permute-start | bytes 589832 | tf_op jit(solution)/shard_map/ppermute | solution.py:289
  97.7 20.0 %collective-permute-start.31 = (f32[6,32,256]{2,1,0:T(8,128)S(1)}, f32[6,32,256]{2,1,0:T(8,128)S(1)}, u32[]{:S(2)}, u32[]{:S(2)}) collective-permute-start(f32[6,32,256]{2,1,0:T(8,128)S(1)} %collective-permute-done.23.refs_6_), channel_id=1, source_target_pairs={{0,1},{1,0},{2,3},{3,2},{4,5},{5,4},{6,7},{7,6},{8,9},{9,8},{10,11... | collective-permute-start | bytes 589832 | tf_op jit(solution)/shard_map/ppermute | solution.py:289
  112.4 16.8 %collective-permute-start.42 = (f32[864,128]{1,0:T(8,128)S(1)}, f32[864,128]{1,0:T(8,128)S(1)}, u32[]{:S(2)}, u32[]{:S(2)}) collective-permute-start(f32[864,128]{1,0:T(8,128)S(1)} %get-tuple-element.58), channel_id=1, source_target_pairs={{0,128},{16,144},{32,160},{48,176},{64,192},{80,208},{96,224},{112... | collective-permute-start | bytes 1327112 | tf_op jit(solution)/shard_map/ppermute | solution.py:289
  115.4 22.7 %collective-permute-start.43 = (f32[864,128]{1,0:T(8,128)S(1)}, f32[864,128]{1,0:T(8,128)S(1)}, u32[]{:S(2)}, u32[]{:S(2)}) collective-permute-start(f32[864,128]{1,0:T(8,128)S(1)} %get-tuple-element.59), channel_id=1, source_target_pairs={{0,64},{16,80},{32,96},{48,112},{64,128},{80,144},{96,160},{112,17... | collective-permute-start | bytes 1327112 | tf_op jit(solution)/shard_map/ppermute | solution.py:289
  115.6 22.4 %collective-permute-start.44 = (f32[864,128]{1,0:T(8,128)S(1)}, f32[864,128]{1,0:T(8,128)S(1)}, u32[]{:S(2)}, u32[]{:S(2)}) collective-permute-start(f32[864,128]{1,0:T(8,128)S(1)} %get-tuple-element.60), channel_id=1, source_target_pairs={{0,192},{16,208},{32,224},{48,240},{64,0},{80,16},{96,32},{112,48}... | collective-permute-start | bytes 1327112 | tf_op jit(solution)/shard_map/ppermute | solution.py:289
  124.6 21.5 %collective-permute-start.36 = (f32[864,128]{1,0:T(8,128)S(1)}, f32[864,128]{1,0:T(8,128)S(1)}, u32[]{:S(2)}, u32[]{:S(2)}) collective-permute-start(f32[864,128]{1,0:T(8,128)S(1)} %get-tuple-element.48), channel_id=1, source_target_pairs={{0,128},{16,144},{32,160},{48,176},{64,192},{80,208},{96,224},{112... | collective-permute-start | bytes 1327112 | tf_op jit(solution)/shard_map/ppermute | solution.py:289
  126.7 30.0 %collective-permute-start.37 = (f32[864,128]{1,0:T(8,128)S(1)}, f32[864,128]{1,0:T(8,128)S(1)}, u32[]{:S(2)}, u32[]{:S(2)}) collective-permute-start(f32[864,128]{1,0:T(8,128)S(1)} %get-tuple-element.49), channel_id=1, source_target_pairs={{0,64},{16,80},{32,96},{48,112},{64,128},{80,144},{96,160},{112,17... | collective-permute-start | bytes 1327112 | tf_op jit(solution)/shard_map/ppermute | solution.py:289
  129.3 27.4 %collective-permute-start.38 = (f32[864,128]{1,0:T(8,128)S(1)}, f32[864,128]{1,0:T(8,128)S(1)}, u32[]{:S(2)}, u32[]{:S(2)}) collective-permute-start(f32[864,128]{1,0:T(8,128)S(1)} %get-tuple-element.50), channel_id=1, source_target_pairs={{0,192},{16,208},{32,224},{48,240},{64,0},{80,16},{96,32},{112,48}... | collective-permute-start | bytes 1327112 | tf_op jit(solution)/shard_map/ppermute | solution.py:289
  138.8 23.0 %collective-permute-start.45 = (f32[32,864]{1,0:T(8,128)S(1)}, f32[32,864]{1,0:T(8,128)S(1)}, u32[]{:S(2)}, u32[]{:S(2)}) collective-permute-start(f32[32,864]{1,0:T(8,128)S(1)} %get-tuple-element.62), channel_id=1, source_target_pairs={{0,16},{16,32},{32,48},{48,0},{64,80},{80,96},{96,112},{112,64},{1... | collective-permute-start | bytes 331784 | tf_op jit(solution)/shard_map/ppermute | solution.py:289
  138.9 31.1 %collective-permute-start.46 = (f32[32,864]{1,0:T(8,128)S(1)}, f32[32,864]{1,0:T(8,128)S(1)}, u32[]{:S(2)}, u32[]{:S(2)}) collective-permute-start(f32[32,864]{1,0:T(8,128)S(1)} %get-tuple-element.63), channel_id=1, source_target_pairs={{0,32},{16,48},{32,0},{48,16},{64,96},{80,112},{96,64},{112,80},{1... | collective-permute-start | bytes 331784 | tf_op jit(solution)/shard_map/ppermute | solution.py:289
  146.0 27.9 %collective-permute-start.47 = (f32[32,864]{1,0:T(8,128)S(1)}, f32[32,864]{1,0:T(8,128)S(1)}, u32[]{:S(2)}, u32[]{:S(2)}) collective-permute-start(f32[32,864]{1,0:T(8,128)S(1)} %get-tuple-element.64), channel_id=1, source_target_pairs={{0,48},{16,0},{32,16},{48,32},{64,112},{80,64},{96,80},{112,96},{1... | collective-permute-start | bytes 331784 | tf_op jit(solution)/shard_map/ppermute | solution.py:289
  157.4 23.5 %collective-permute-start.39 = (f32[32,864]{1,0:T(8,128)S(1)}, f32[32,864]{1,0:T(8,128)S(1)}, u32[]{:S(2)}, u32[]{:S(2)}) collective-permute-start(f32[32,864]{1,0:T(8,128)S(1)} %get-tuple-element.52), channel_id=1, source_target_pairs={{0,16},{16,32},{32,48},{48,0},{64,80},{80,96},{96,112},{112,64},{1... | collective-permute-start | bytes 331784 | tf_op jit(solution)/shard_map/ppermute | solution.py:289
  157.5 23.5 %collective-permute-start.40 = (f32[32,864]{1,0:T(8,128)S(1)}, f32[32,864]{1,0:T(8,128)S(1)}, u32[]{:S(2)}, u32[]{:S(2)}) collective-permute-start(f32[32,864]{1,0:T(8,128)S(1)} %get-tuple-element.53), channel_id=1, source_target_pairs={{0,32},{16,48},{32,0},{48,16},{64,96},{80,112},{96,64},{112,80},{1... | collective-permute-start | bytes 331784 | tf_op jit(solution)/shard_map/ppermute | solution.py:289
  161.9 19.1 %collective-permute-start.41 = (f32[32,864]{1,0:T(8,128)S(1)}, f32[32,864]{1,0:T(8,128)S(1)}, u32[]{:S(2)}, u32[]{:S(2)}) collective-permute-start(f32[32,864]{1,0:T(8,128)S(1)} %get-tuple-element.54), channel_id=1, source_target_pairs={{0,48},{16,0},{32,16},{48,32},{64,112},{80,64},{96,80},{112,96},{1... | collective-permute-start | bytes 331784 | tf_op jit(solution)/shard_map/ppermute | solution.py:289
  (59 other events, 498.0 us)
where the time goes:
time: 183 us; the launch traced here: 182 us
  starting transfers between devices  76.3 us (42%)
  waiting for transfers between devices  43.5 us (24%)
  Pallas kernels  39.7 us (22%)
  local copies, waits for them, and re-layouts  21.3 us (12%)
    ppermute x48, starting transfers between devices, send(): return lax.ppermute(value, axis, moves)  76.3 us
    ppermute x48, waiting for transfers between devices, send(): return lax.ppermute(value, axis, moves)  43.5 us
    pallas_call x12, Pallas kernels, call(): pl.pallas_call(kernel, out_shape=out_shape, in_specs=[SM] * n_smem + [VM]...  39.7 us
    unnamed x75, local copies, waits for them, and re-layouts  20.3 us
  transfers between devices with their start and end apart: 48, of which 14 were waited for; matrix products, arithmetic and copies ran while one was open for 2% of the time, Pallas kernels for 16%

commit v1 on v0

v1 whole, which is shorter than its diff:
```python
import math

import jax
import jax.numpy as jnp
from jax import lax
from jax.experimental import pallas as pl
from jax.experimental.pallas import tpu as pltpu
from jax.sharding import PartitionSpec as P

SIDE = 16
AREA = 256
SLABS = 16
SHIFTS = [(b, c) for b in (-1, 0, 1) for c in (-1, 0, 1)]
F32 = jnp.float32
BF16 = jnp.bfloat16
VM = pl.BlockSpec(memory_space=pltpu.VMEM)
SM = pl.BlockSpec(memory_space=pltpu.SMEM)


def slope_of(values):
    sigma = jax.nn.sigmoid(values)
    return sigma * (1.0 + values * (1.0 - sigma))


def call(kernel, out_shape, scratch, args, n_smem=0, flops=0, name=None, fetched=()):
    many = isinstance(out_shape, list)
    moved = sum(a.size * a.dtype.itemsize for a in (*args, *fetched))
    moved += sum(o.size * o.dtype.itemsize for o in (out_shape if many else [out_shape]))
    n, m = len(args), len(fetched)

    def whole(*refs):
        sources, rest = refs[n:n + m], refs[n + m:]
        rest, targets, sems = rest[:len(rest) - m - 1], rest[len(rest) - m - 1:-1], rest[-1]
        copies = [(pltpu.make_async_copy(s, t, sems.at[k]), t) for k, (s, t) in enumerate(zip(sources, targets))]
        for copy, _ in copies:
            copy.start()
        kernel(copies, *refs[:n], *rest)

    if fetched:
        scratch = [*scratch, *(pltpu.VMEM(f.shape, f.dtype) for f in fetched), pltpu.SemaphoreType.DMA((m,))]
    return pl.pallas_call(
        whole if fetched else kernel,
        out_shape=out_shape,
        in_specs=[SM] * n_smem + [VM] * (n - n_smem) + [pl.BlockSpec(memory_space=pltpu.HBM)] * m,
        out_specs=[VM] * len(out_shape) if many else VM,
        scratch_shapes=scratch,
        compiler_params=pltpu.CompilerParams(vmem_limit_bytes=16 << 20),
        cost_estimate=pl.CostEstimate(flops=flops, bytes_accessed=moved, transcendentals=0),
        name=name,
    )(*args, *fetched)


def arrived(copies):
    for copy, _ in copies:
        copy.wait()
    return [target for _, target in copies]


def shape(*dims, dtype=F32):
    return jax.ShapeDtypeStruct(dims, dtype)


def split(value):
    high = value.astype(BF16)
    return high, (value - high.astype(F32)).astype(BF16)


def moved_cells(plane, row_step, col_step):
    cells = lax.broadcasted_iota(jnp.int32, plane.shape, 1)
    if col_step:
        col = cells % SIDE + col_step
        plane = jnp.where((col >= 0) & (col < SIDE), pltpu.roll(plane, -col_step % AREA, 1), 0.0)
    if row_step:
        row = cells // SIDE + row_step
        plane = jnp.where((row >= 0) & (row < SIDE), pltpu.roll(plane, -row_step * SIDE % AREA, 1), 0.0)
    return plane


def scaled_kernel(pre_ref, grad_ref, out_ref):
    out_ref[...] = grad_ref[...] * slope_of(pre_ref[...])


def scaled(pre, grad):
    return call(scaled_kernel, shape(*pre.shape), [], [pre, grad], name="scaled")


def weights_kernel(copies, turn, pre_ref, *outs):
    slope_ref = outs[-1]
    slope_ref[...] = slope_of(pre_ref[...])
    for n, copy in enumerate(copies):
        source, = arrived([copy])
        taps, channels, total = source.shape
        width = total // 4
        for a in range(3):
            hi_ref, lo_ref = outs[6 * n + 2 * a:6 * n + 2 * a + 2]

            def one_tap(t, _):
                at = pl.ds(pl.multiple_of(t * channels, channels), channels)
                for d in range(4):
                    lanes = pl.ds(pl.multiple_of(turn[d] * width, width), width)
                    hi, lo = split(source[t + a * (taps // 3), :, lanes])
                    hi_ref[at, d * width:(d + 1) * width] = hi
                    lo_ref[at, d * width:(d + 1) * width] = lo
                return 0

            lax.fori_loop(0, taps // 3, one_tap, 0)


def weight_halves(turn, pre, w1, w2):
    taps, channels, total = w1.shape
    flat = shape(taps // 3 * channels, total, dtype=BF16)
    *halves, slope = call(weights_kernel, [flat] * 12 + [shape(*pre.shape)], [], [turn, pre], 1,
                          name="weight_halves", fetched=[w2, w1])
    return halves[:6], halves[6:], slope


def inputs_kernel(pre_ref, saved_ref, low_ref, high_ref, h_hi, h_lo, x_hi, x_lo, rows):
    planes, channels, _ = pre_ref.shape
    for n, (own, hi_ref, lo_ref) in enumerate(((pre_ref, h_hi, h_lo), (saved_ref, x_hi, x_lo))):
        rows[0] = low_ref[n + 1]
        rows[planes + 1] = high_ref[n + 1]
        rows[1:planes + 1] = own[...]

        def one_plane(q, _):
            plane = rows[q]
            if n == 0:
                plane = plane * jax.nn.sigmoid(plane)
            lanes = pl.ds(pl.multiple_of(q * AREA, AREA), AREA)
            for s, (b, c) in enumerate(SHIFTS):
                hi, lo = split(moved_cells(plane, b, c))
                hi_ref[s * channels:(s + 1) * channels, lanes] = hi
                lo_ref[s * channels:(s + 1) * channels, lanes] = lo
            return 0

        lax.fori_loop(0, planes + 2, one_plane, 0)


def input_halves(pre, saved, low, high):
    planes, channels, area = pre.shape
    tall = shape(len(SHIFTS) * channels, (planes + 2) * area, dtype=BF16)
    return call(inputs_kernel, [tall] * 4, [pltpu.VMEM((planes + 2, channels, area), F32)],
                [pre, saved, low, high], name="input_halves")


def gather_blocks(spots, pieces, g_hi, g_lo):
    planes = pieces[0].shape[0]
    k = 0
    for piece in pieces:
        for first in range(0, piece.shape[0], planes):
            spot = spots[k]
            k += 1
            for p in range(planes):
                hi, lo = split(piece[first + p])
                g_hi[spot, :, p * AREA:(p + 1) * AREA] = hi
                g_lo[spot, :, p * AREA:(p + 1) * AREA] = lo


def spread(sums):
    channels = sums.shape[0] // len(SHIFTS)
    total = jnp.zeros((channels, AREA), F32)
    for b in (-1, 0, 1):
        row = jnp.zeros((channels, AREA), F32)
        for c in (-1, 0, 1):
            s = SHIFTS.index((b, c)) * channels
            row += moved_cells(sums[s:s + channels, :], 0, -c)
        total += moved_cells(row, -b, 0)
    return total


def three_products(w_hi, w_lo, hi, lo):
    out = jnp.dot(w_hi, hi, preferred_element_type=F32)
    out += jnp.dot(w_hi, lo, preferred_element_type=F32)
    return out + jnp.dot(w_lo, hi, preferred_element_type=F32)


def plane_of(g_ref, p):
    lanes = pl.ds(pl.multiple_of(p * AREA, AREA), AREA)
    return g_ref[:, :, lanes].reshape(g_ref.shape[0] * g_ref.shape[1], AREA)


def outer_part(g_hi, g_lo, copies, before_ref, behind_ref, edge_refs=()):
    last = g_hi.shape[2] // AREA - 1
    w_refs = arrived(copies)
    for p, w_hi, w_lo, out in ((0, *w_refs[:2], before_ref), (last, *w_refs[2:], behind_ref)):
        out[0] = spread(three_products(w_hi[...], w_lo[...], plane_of(g_hi, p), plane_of(g_lo, p)))
        for n, edge in enumerate(edge_refs):
            out[n + 1] = edge[p]


def inner_part(copies, g_hi, g_lo, own_ref, sums):
    planes = own_ref.shape[0]
    third = sums.shape[1]
    for n, a in enumerate((1, 0, 2)):
        w_hi, w_lo = arrived(copies[2 * n:2 * n + 2])

        def one_plane(p, _):
            out = three_products(w_hi[...], w_lo[...], plane_of(g_hi, p), plane_of(g_lo, p))
            if a == 1:
                sums[p] = out
            else:
                sums[p + a - 1] += out
            return 0

        lax.fori_loop(max(0, 1 - a), planes - max(0, a - 1), one_plane, 0)

    def one_out(p, _):
        own_ref[p] = spread(sums[p])
        return 0

    lax.fori_loop(0, planes, one_out, 0)


def filter_part(g_hi, g_lo, i_hi, i_lo, outs):
    total = g_hi.shape[0] * g_hi.shape[1]
    planes = g_hi.shape[2] // AREA
    width = total // len(outs)
    for out in outs:
        out[...] = jnp.zeros_like(out)

    def one_plane(p, _):
        lanes = pl.ds(pl.multiple_of(p * AREA, AREA), AREA)
        hi = g_hi[:, :, lanes].reshape(total, AREA)
        lo = g_lo[:, :, lanes].reshape(total, AREA)
        windows = [pl.ds(pl.multiple_of((p + a) * AREA, AREA), AREA) for a in range(3)]
        left_hi = jnp.concatenate([i_hi[:, w] for w in windows], 0)
        left_lo = jnp.concatenate([i_lo[:, w] for w in windows], 0)
        dims = (((1,), (1,)), ((), ()))
        part = lax.dot_general(left_hi, hi, dims, preferred_element_type=F32)
        part += lax.dot_general(left_hi, lo, dims, preferred_element_type=F32)
        part += lax.dot_general(left_lo, hi, dims, preferred_element_type=F32)
        for d, out in enumerate(outs):
            out[...] += part[:, d * width:(d + 1) * width]
        return 0

    lax.fori_loop(0, planes, one_plane, 0)


def first_use(body, spots, pieces, others, outs, flops, name, fetched):
    planes, channels, area = pieces[0].shape
    n, m = len(pieces), len(pieces) + len(others)
    shards = sum(piece.shape[0] for piece in pieces) // planes
    halves = [shape(shards, channels, planes * area, dtype=BF16)] * 2

    def kernel(copies, spots, *refs):
        g_hi, g_lo = refs[m:m + 2]
        gather_blocks(spots, refs[:n], g_hi, g_lo)
        body(g_hi, g_lo, copies, *refs[n:m], *refs[m + 2:])

    g_hi, g_lo, *rest = call(kernel, halves + outs, [], [spots, *pieces, *others], 1, flops, name, fetched)
    return (g_hi, g_lo), rest


def inner(halves, weights, planes, flops, name):
    third = weights[0].shape[0]
    channels = third // len(SHIFTS)
    return call(inner_part, shape(planes, channels, AREA), [pltpu.VMEM((planes, third, AREA), F32)], list(halves),
                0, flops, name, [*weights[2:4], *weights[:2], *weights[4:]])


def turned_kernel(spots, a, b, c, d, *refs):
    outs, turned = refs[:-1], refs[-1]
    turned[...] = (a[...] + b[...] + c[...] + d[...]).T
    height = outs[0].shape[0]
    for k, out in enumerate(outs):
        out[...] = turned[pl.ds(pl.multiple_of(spots[k] * height, height), height), :]


def turned_sum(spots, parts):
    rows, width = parts[0].shape
    return call(turned_kernel, [shape(width // 4, rows)] * 4, [pltpu.VMEM((width, rows), F32)],
                [spots, *parts], 1, name="turned_sum")


def last_kernel(scale, a, b, c, d, out):
    out[...] = ((a[...] + b[...] + c[...] + d[...]) * scale).T


def last_sum(parts, scale):
    height, rows = parts[0].shape
    return call(lambda *refs: last_kernel(scale, *refs), shape(rows, height), [], parts, name="last_sum")


def first_kernel(own, before, after, slope, out):
    planes = out.shape[0]
    for p in range(planes):
        value = own[p]
        if p == 0:
            value = value + before[0]
        if p == planes - 1:
            value = value + after[0]
        out[p] = value * slope[p]


def input_kernel(own, before, after, out):
    planes = own.shape[0]
    for p in range(planes):
        value = own[p]
        if p == 0:
            value = value + before[0]
        if p == planes - 1:
            value = value + after[0]
        out[p] = value


FAR = [(i, (i + 8) % 16) for i in range(16)]
TWIN = [(i, i ^ 1) for i in range(16)]
UP = [(i, i + 1) for i in range(SLABS - 1)]
DOWN = [(i + 1, i) for i in range(SLABS - 1)]


def along_x(d):
    return [(i, (i & 9) | ((i + 2 * d) & 6)) for i in range(16)]


def along_y(d):
    return [(i, (i + 4 * d) % 16) for i in range(16)]


def along_z(d):
    return [(i, (i & 12) | ((i + d) & 3)) for i in range(16)]


def send(value, moves, axis="chan"):
    return lax.ppermute(value, axis, moves)


def after(value, done):
    return lax.optimization_barrier((value, *done))[0]


def shard_ids():
    me = lax.axis_index("chan")
    row, far_row = ([s] + [(s & 9) | ((s - 2 * d) & 6) for d in (1, 3, 2)] for s in (me, me ^ 8))
    ids = row + far_row
    return jnp.stack(ids + [i ^ 1 for i in ids]).astype(jnp.int32)


def gathered(own, soon, late):
    far = send(own, FAR)
    near = [own] + [send(own, along_x(d)) for d in (1, 3, 2)]
    far = after(far, [*near, *soon])
    near_twin = send(jnp.concatenate(near, 0), TWIN)
    wide = [far] + [send(far, along_x(d)) for d in (1, 3, 2)]
    result, done = late(far)
    wide_twin = send(after(jnp.concatenate(wide, 0), done), TWIN)
    return [*near, *wide, near_twin, wide_twin], result


def edges(before, after):
    return send(after, UP, "slab"), send(before, DOWN, "slab")


def row_sum(parts):
    return [parts[0]] + [send(parts[d], along_y(d), "slab") for d in (2, 1, 3)]


def owner_sum(parts, spots, scale):
    rows = turned_sum(spots, parts)
    return last_sum([rows[0]] + [send(rows[d], along_z(d), "slab") for d in (1, 2, 3)], scale)


def per_device(saved_input, pre_first, pre_second, out_grad, weight_first, weight_second):
    saved, pre1, pre2, grad = (jnp.transpose(v, (1, 0, 2)) for v in (saved_input, pre_first, pre_second, out_grad))
    planes, channels, area = saved.shape
    taps, _, total = weight_first.shape
    rows = taps * channels
    flops = 6 * rows * total * planes * area
    scale = 1.0 / math.sqrt(planes * SLABS * area)
    slab = lax.axis_index("slab")
    turn = ((slab // 4 + jnp.arange(4)) % 4).astype(jnp.int32)
    z_spots = ((slab + jnp.arange(4)) % 4).astype(jnp.int32)
    ids = shard_ids()
    spots = (((ids // 4 - slab // 4) % 4) * 4 + ids % 4).astype(jnp.int32)
    quarters = [shape(rows, total // 4)] * 4
    second_grad = scaled(pre2, grad)
    w2, w1, slope = weight_halves(turn, pre1, weight_first, weight_second)
    pieces, _ = gathered(second_grad, [*w1, *w2, slope], lambda far: ((), []))

    halves, (before, behind) = first_use(
        lambda g_hi, g_lo, copies, pre, saved, *outs: outer_part(g_hi, g_lo, copies, *outs, (pre, saved)),
        spots, pieces, [pre1, saved], [shape(3, channels, area)] * 2, flops // 9, "second_outer", [*w2[:2], *w2[4:]])
    before, behind = edges(before, behind)
    own = inner(halves, w2, planes, flops, "second_inner")
    first_grad = call(first_kernel, shape(planes, channels, area), [], [own, before, behind, slope], name="first_grad")
    h_hi, h_lo, x_hi, x_lo = input_halves(pre1, saved, before, behind)

    second_parts = call(lambda g_hi, g_lo, i_hi, i_lo, *outs: filter_part(g_hi, g_lo, i_hi, i_lo, outs),
                        quarters, [], [*halves, h_hi, h_lo], 0, flops, "second_filter")

    def second_sum(far):
        rows = row_sum(lax.optimization_barrier((*second_parts, far))[:4])
        return rows, rows[1:3]

    pieces, second_rows = gathered(first_grad, second_parts, second_sum)
    halves, first_parts = first_use(
        lambda g_hi, g_lo, copies, *outs: filter_part(g_hi, g_lo, *arrived(copies), outs),
        spots, pieces, [], quarters, flops, "first_filter", [x_hi, x_lo])
    first_rows = row_sum(first_parts)
    second_rows = lax.optimization_barrier((*second_rows, first_parts[0]))[:4]
    second_weights = owner_sum(second_rows, z_spots, scale)

    before, behind = call(lambda copies, g_hi, g_lo, *outs: outer_part(g_hi, g_lo, copies, *outs),
                          [shape(1, channels, area)] * 2, [], list(halves), 0, flops // 9, "first_outer",
                          [*w1[:2], *w1[4:]])
    before, behind = edges(before, behind)
    own = inner(halves, w1, planes, flops, "first_inner")
    input_grad = call(input_kernel, shape(planes, channels, area), [], [own, before, behind], name="input_grad")
    first_weights = owner_sum(first_rows, z_spots, scale)
    return (jnp.transpose(input_grad, (1, 0, 2)), first_weights.reshape(taps, channels, -1),
            second_weights.reshape(taps, channels, -1))


def solution(mesh):
    in_specs = (
        P("chan", "slab", None),
        P("chan", "slab", None),
        P("chan", "slab", None),
        P("chan", "slab", None),
        P(None, "chan", None),
        P(None, "chan", None),
    )
    out_specs = (P("chan", "slab", None), P(None, "chan", "slab"), P(None, "chan", "slab"))
    return jax.shard_map(
        per_device, mesh=mesh, in_specs=in_specs, out_specs=out_specs, check_vma=False
    )
```

time: 183 us -> 148 us (0.81)
  starting transfers between devices: 76.3 us -> 50.2 us
  local copies, waits for them, and re-layouts: 21.3 us -> 11.2 us
  waiting for transfers between devices: 43.5 us -> 40.8 us
  other arithmetic: 0.04 us -> 2.11 us
    ppermute x48 -> x34, starting transfers between devices: 76.3 us -> 50.2 us  [send(): return lax.ppermute(value, axis, moves)]
    unnamed x75 -> x70, local copies, waits for them, and re-layouts: 20.3 us -> 11.1 us
    ppermute x48 -> x34, waiting for transfers between devices: 43.5 us -> 40.8 us  [send(): return lax.ppermute(value, axis, moves)]
    concatenate x0 -> x4, other arithmetic: none -> 2.07 us  [the longest x2 1.05 us: gathered(): near_twin = send(jnp.concatenate(near, 0), TWIN)]
    pallas_call x12 -> x15, Pallas kernels: 39.7 us -> 40.9 us  [call(): pl.pallas_call(whole if fetched else kernel, out_shape=out_shape, in_spec...]
  transfers between devices with their start and end apart: 48 -> 34, of which waited for: 14 -> 14; matrix products, arithmetic and copies ran while one was open for 2% -> 2% of each run, Pallas kernels for 16% -> 26%
where the time goes in v1:
time: 148 us; the launch traced here: 147 us
  starting transfers between devices  50.2 us (34%)
  Pallas kernels  40.9 us (28%)
  waiting for transfers between devices  40.8 us (28%)
  local copies, waits for them, and re-layouts  11.2 us (8%)
  other arithmetic  2.11 us (1%)
    ppermute x34, starting transfers between devices, send(): return lax.ppermute(value, axis, moves)  50.2 us
    pallas_call x15, Pallas kernels, call(): pl.pallas_call(whole if fetched else kernel, out_shape=out_shape, in_spec...  40.9 us
    ppermute x34, waiting for transfers between devices, send(): return lax.ppermute(value, axis, moves)  40.8 us
    unnamed x70, local copies, waits for them, and re-layouts  11.1 us
  transfers between devices with their start and end apart: 34, of which 14 were waited for; matrix products, arithmetic and copies ran while one was open for 2% of the time, Pallas kernels for 26%

profile of v1, /device:TPU:8, one launch (start us, length us, event | category | flops | bytes accessed | tf_op | source)
XLA Modules:
  0.0 146.6 jit_solution(4985005537328791454)
XLA Ops:
  2.5 7.3 %collective-permute-start.3 = (f32[6,32,256]{2,1,0:T(8,128)S(1)}, f32[6,32,256]{2,1,0:T(8,128)S(1)}, u32[]{:S(2)}, u32[]{:S(2)}) collective-permute-start(f32[6,32,256]{2,1,0:T(8,128)S(1)} %scaled.1.refs_1_), channel_id=1, source_target_pairs={{0,8},{1,9},{2,10},{3,11},{4,12},{5,13},{6,14},{7,15},{8,0},{9,1},... | collective-permute-start | bytes 589832 | tf_op jit(solution)/shard_map/ppermute | solution.py:324
  9.8 3.0 %collective-permute-start.2 = (f32[6,32,256]{2,1,0:T(8,128)S(1)}, f32[6,32,256]{2,1,0:T(8,128)S(1)}, u32[]{:S(2)}, u32[]{:S(2)}) collective-permute-start(f32[6,32,256]{2,1,0:T(8,128)S(1)} %scaled.1.refs_1_), channel_id=1, source_target_pairs={{0,4},{1,5},{2,6},{3,7},{4,0},{5,1},{6,2},{7,3},{8,12},{9,13},{10,... | collective-permute-start | bytes 589832 | tf_op jit(solution)/shard_map/ppermute | solution.py:324
  18.8 2.4 %weight_halves.1 = (bf16[288,512]{1,0:T(8,128)(2,1)S(1)}, bf16[288,512]{1,0:T(8,128)(2,1)S(1)}, bf16[288,512]{1,0:T(8,128)(2,1)S(1)}, bf16[288,512]{1,0:T(8,128)...) custom-call(s32[4]{0:T(128)S(1)} %and_select_fusion.1.refs_0_, ...), custom_call_target="tpu_custom_call" | custom-call | bytes 7471120 | tf_op jit(solution)/shard_map/weight_halves/pallas_call | solution.py:41
  22.8 2.1 %collective-permute-start.6 = (f32[6,32,256]{2,1,0:T(8,128)S(1)}, f32[6,32,256]{2,1,0:T(8,128)S(1)}, u32[]{:S(2)}, u32[]{:S(2)}) collective-permute-start(f32[6,32,256]{2,1,0:T(8,128)S(1)} %collective-permute-done.3.refs_5_), channel_id=1, source_target_pairs={{0,4},{1,5},{2,6},{3,7},{4,0},{5,1},{6,2},{7,3},{8,12},{9,13},{10,... | collective-permute-start | bytes 589832 | tf_op jit(solution)/shard_map/ppermute | solution.py:324
  27.9 4.2 %collective-permute-done.6.refs_8_ = f32[6,32,256]{2,1,0:T(8,128)S(1)} collective-permute-done((f32[6,32,256]{2,1,0:T(8,128)S(1)}, f32[6,32,256]{2,1,0:T(8,128)S(1)}, u32[]{:S(2)}, u32[]{:S(2)}) %collective-permute-start.6) | collective-permute-done | bytes 196640 | tf_op jit(solution)/shard_map/ppermute | solution.py:324
  32.1 2.5 %collective-permute-done.5.refs_7_ = f32[6,32,256]{2,1,0:T(8,128)S(1)} collective-permute-done((f32[6,32,256]{2,1,0:T(8,128)S(1)}, f32[6,32,256]{2,1,0:T(8,128)S(1)}, u32[]{:S(2)}, u32[]{:S(2)}) %collective-permute-start.5) | collective-permute-done | bytes 196640 | tf_op jit(solution)/shard_map/ppermute | solution.py:324
  36.3 2.3 %collective-permute-done.8.refs_10_ = f32[24,32,256]{2,1,0:T(8,128)S(1)} collective-permute-done((f32[24,32,256]{2,1,0:T(8,128)}, f32[24,32,256]{2,1,0:T(8,128)S(1)}, u32[]{:S(2)}, u32[]{:S(2)}) %collective-permute-start.8) | collective-permute-done | bytes 786464 | tf_op jit(solution)/shard_map/ppermute | solution.py:324
  44.5 2.9 %collective-permute-start.9 = (f32[3,32,256]{2,1,0:T(8,128)S(1)}, f32[3,32,256]{2,1,0:T(8,128)S(1)}, u32[]{:S(2)}, u32[]{:S(2)}) collective-permute-start(f32[3,32,256]{2,1,0:T(8,128)S(1)} %get-tuple-element.71), channel_id=1, source_target_pairs={{0,16},{16,32},{32,48},{48,64},{64,80},{80,96},{96,112},{112,128},... | collective-permute-start | bytes 294920 | tf_op jit(solution)/shard_map/ppermute | solution.py:324
  47.4 5.6 %collective-permute-start.10 = (f32[3,32,256]{2,1,0:T(8,128)S(1)}, f32[3,32,256]{2,1,0:T(8,128)S(1)}, u32[]{:S(2)}, u32[]{:S(2)}) collective-permute-start(f32[3,32,256]{2,1,0:T(8,128)S(1)} %get-tuple-element.72), channel_id=1, source_target_pairs={{16,0},{32,16},{48,32},{64,48},{80,64},{96,80},{112,96},{128,112},... | collective-permute-start | bytes 294920 | tf_op jit(solution)/shard_map/ppermute | solution.py:324
  53.1 7.9 %second_inner.1.own = f32[6,32,256]{2,1,0:T(8,128)S(1)} custom-call(bf16[16,32,1536]{2,1,0:T(8,128)(2,1)S(1)} %get-tuple-element.69.refs_0_.g_hi, bf16[16,32,1536]{2,1,0:T(8,128)(2,1)S(1)} %get-tuple-element.70.refs_1_.g_lo, bf16[288,512]{1,0:T(8,128)(2,1)S(1)} %copy-done.32, bf16[288,512]{1,0:T(8,128)(2,1)S(1)} %copy-done.34, ...), custom_call_target="tpu_custom_call" | custom-call | flops 4076863488 | bytes 5111808 | tf_op jit(solution)/shard_map/second_inner/pallas_call | solution.py:41
  62.0 2.1 %collective-permute-start.13 = (f32[6,32,256]{2,1,0:T(8,128)S(1)}, f32[6,32,256]{2,1,0:T(8,128)S(1)}, u32[]{:S(2)}, u32[]{:S(2)}) collective-permute-start(f32[6,32,256]{2,1,0:T(8,128)S(1)} %first_grad.1.refs_1_), channel_id=1, source_target_pairs={{0,4},{1,5},{2,6},{3,7},{4,0},{5,1},{6,2},{7,3},{8,12},{9,13},{10,... | collective-permute-start | bytes 589832 | tf_op jit(solution)/shard_map/ppermute | solution.py:324
  66.1 3.0 %input_halves.1 = (bf16[288,2048]{1,0:T(8,128)(2,1)S(1)}, bf16[288,2048]{1,0:T(8,128)(2,1)S(1)}, bf16[288,2048]{1,0:T(8,128)(2,1)S(1)}, bf16[288,2048]{1,0:T(8,128)(2,1)S(1)}) custom-call(f32[6,32,256]{2,1,0:T(8,128)S(1)} %bitcast.25, f32[6,32,256]{2,1,0:T(8,128)S(1)} %bitcast.27, f32[3,32,256]{2,1,0:T(8,128)S(1)} %collective-permute-done.9.before.low_ref, ...), custom_call_target="tpu_custom_call" | custom-call | bytes 5308416 | tf_op jit(solution)/shard_map/input_halves/pallas_call | solution.py:41
  69.1 5.5 %second_filter.1 = (f32[864,128]{1,0:T(8,128)S(1)}, f32[864,128]{1,0:T(8,128)S(1)}, f32[864,128]{1,0:T(8,128)S(1)}, f32[864,128]{1,0:T(8,128)S(1)}) custom-call(bf16[16,32,1536]{2,1,0:T(8,128)(2,1)S(1)} %get-tuple-element.69.refs_0_.g_hi, bf16[16,32,1536]{2,1,0:T(8,128)(2,1)S(1)} %get-tuple-element.70.refs_1_.g_lo, ...), custom_call_target="tpu_custom_call" | custom-call | flops 4076863488 | bytes 7274496 | tf_op jit(solution)/shard_map/second_filter/pallas_call | solution.py:41
  74.6 2.4 %collective-permute-start.19 = (f32[864,128]{1,0:T(8,128)S(1)}, f32[864,128]{1,0:T(8,128)S(1)}, u32[]{:S(2)}, u32[]{:S(2)}) collective-permute-start(f32[864,128]{1,0:T(8,128)S(1)} %get-tuple-element.80), channel_id=1, source_target_pairs={{0,128},{16,144},{32,160},{48,176},{64,192},{80,208},{96,224},{112... | collective-permute-start | bytes 1327112 | tf_op jit(solution)/shard_map/ppermute | solution.py:324
  80.5 5.2 %collective-permute-done.17.refs_8_ = f32[6,32,256]{2,1,0:T(8,128)S(1)} collective-permute-done((f32[6,32,256]{2,1,0:T(8,128)S(1)}, f32[6,32,256]{2,1,0:T(8,128)S(1)}, u32[]{:S(2)}, u32[]{:S(2)}) %collective-permute-start.17) | collective-permute-done | bytes 196640 | tf_op jit(solution)/shard_map/ppermute | solution.py:324
  88.7 7.7 %collective-permute-done.20.c = f32[864,128]{1,0:T(8,128)S(1)} collective-permute-done((f32[864,128]{1,0:T(8,128)S(1)}, f32[864,128]{1,0:T(8,128)S(1)}, u32[]{:S(2)}, u32[]{:S(2)}) %collective-permute-start.20) | collective-permute-done | bytes 442400 | tf_op jit(solution)/shard_map/ppermute | solution.py:324
  96.6 2.0 %collective-permute-done.21.refs_10_ = f32[24,32,256]{2,1,0:T(8,128)S(1)} collective-permute-done((f32[24,32,256]{2,1,0:T(8,128)S(1)}, f32[24,32,256]{2,1,0:T(8,128)S(1)}, u32[]{:S(2)}, u32[]{:S(2)}) %collective-permute-start.21) | collective-permute-done | bytes 786464 | tf_op jit(solution)/shard_map/ppermute | solution.py:324
  98.7 6.8 %first_filter.1 = (bf16[16,32,1536]{2,1,0:T(8,128)(2,1)S(1)}, bf16[16,32,1536]{2,1,0:T(8,128)(2,1)S(1)}, f32[864,128]{1,0:T(8,128)S(1)}, f32[864,128]{1,0:T(8,12...) custom-call(s32[16]{0:T(128)S(1)} %fusion.refs_0_, f32[6,32,256]{2,1,0:T(8,128)S(1)} %first_grad.1.refs_1_, ...), custom_call_target="tpu_custom_call" | custom-call | flops 4076863488 | bytes 10420288 | tf_op jit(solution)/shard_map/first_filter/pallas_call | solution.py:41
  111.0 2.8 %collective-permute-start.22 = (f32[1,32,256]{2,1,0:T(8,128)S(1)}, f32[1,32,256]{2,1,0:T(8,128)S(1)}, u32[]{:S(2)}, u32[]{:S(2)}) collective-permute-start(f32[1,32,256]{2,1,0:T(8,128)S(1)} %get-tuple-element.87), channel_id=1, source_target_pairs={{0,16},{16,32},{32,48},{48,64},{64,80},{80,96},{96,112},{112,128},... | collective-permute-start | bytes 98312 | tf_op jit(solution)/shard_map/ppermute | solution.py:324
  113.8 6.4 %collective-permute-done.24.b = f32[864,128]{1,0:T(8,128)S(1)} collective-permute-done((f32[864,128]{1,0:T(8,128)S(1)}, f32[864,128]{1,0:T(8,128)S(1)}, u32[]{:S(2)}, u32[]{:S(2)}) %collective-permute-start.24) | collective-permute-done | bytes 442400 | tf_op jit(solution)/shard_map/ppermute | solution.py:324
  120.2 2.5 %collective-permute-start.23 = (f32[1,32,256]{2,1,0:T(8,128)S(1)}, f32[1,32,256]{2,1,0:T(8,128)S(1)}, u32[]{:S(2)}, u32[]{:S(2)}) collective-permute-start(f32[1,32,256]{2,1,0:T(8,128)S(1)} %get-tuple-element.88), channel_id=1, source_target_pairs={{16,0},{32,16},{48,32},{64,48},{80,64},{96,80},{112,96},{128,112},... | collective-permute-start | bytes 98312 | tf_op jit(solution)/shard_map/ppermute | solution.py:324
  122.7 6.0 %collective-permute-done.25.c = f32[864,128]{1,0:T(8,128)S(1)} collective-permute-done((f32[864,128]{1,0:T(8,128)S(1)}, f32[864,128]{1,0:T(8,128)S(1)}, u32[]{:S(2)}, u32[]{:S(2)}) %collective-permute-start.25) | collective-permute-done | bytes 442400 | tf_op jit(solution)/shard_map/ppermute | solution.py:324
  131.8 2.8 %collective-permute-start.28 = (f32[32,864]{1,0:T(8,128)S(1)}, f32[32,864]{1,0:T(8,128)S(1)}, u32[]{:S(2)}, u32[]{:S(2)}) collective-permute-start(f32[32,864]{1,0:T(8,128)S(1)} %get-tuple-element.95), channel_id=1, source_target_pairs={{0,32},{16,48},{32,0},{48,16},{64,96},{80,112},{96,64},{112,80},{1... | collective-permute-start | bytes 331784 | tf_op jit(solution)/shard_map/ppermute | solution.py:324
  135.5 7.9 %first_inner.1.own = f32[6,32,256]{2,1,0:T(8,128)S(1)} custom-call(bf16[16,32,1536]{2,1,0:T(8,128)(2,1)S(1)} %get-tuple-element.85.refs_0_, bf16[16,32,1536]{2,1,0:T(8,128)(2,1)S(1)} %get-tuple-element.86.refs_1_, bf16[288,512]{1,0:T(8,128)(2,1)S(1)} %copy-done.28, bf16[288,512]{1,0:T(8,128)(2,1)S(1)} %copy-done.30, bf16[288,512]{1,0:T(8,128)(2,1)S(1)} %copy-done.6, ...), custom_call_target="tpu_custom_call" | custom-call | flops 4076863488 | bytes 5111808 | tf_op jit(solution)/shard_map/first_inner/pallas_call | solution.py:41
  (137 shorter events, 41.7 us)
Async XLA Ops:
  2.5 20.2 %collective-permute-start.3 = (f32[6,32,256]{2,1,0:T(8,128)S(1)}, f32[6,32,256]{2,1,0:T(8,128)S(1)}, u32[]{:S(2)}, u32[]{:S(2)}) collective-permute-start(f32[6,32,256]{2,1,0:T(8,128)S(1)} %scaled.1.refs_1_), channel_id=1, source_target_pairs={{0,8},{1,9},{2,10},{3,11},{4,12},{5,13},{6,14},{7,15},{8,0},{9,1},... | collective-permute-start | bytes 589832 | tf_op jit(solution)/shard_map/ppermute | solution.py:324
  9.8 12.9 %collective-permute-start.2 = (f32[6,32,256]{2,1,0:T(8,128)S(1)}, f32[6,32,256]{2,1,0:T(8,128)S(1)}, u32[]{:S(2)}, u32[]{:S(2)}) collective-permute-start(f32[6,32,256]{2,1,0:T(8,128)S(1)} %scaled.1.refs_1_), channel_id=1, source_target_pairs={{0,4},{1,5},{2,6},{3,7},{4,0},{5,1},{6,2},{7,3},{8,12},{9,13},{10,... | collective-permute-start | bytes 589832 | tf_op jit(solution)/shard_map/ppermute | solution.py:324
  12.8 9.9 %collective-permute-start.1 = (f32[6,32,256]{2,1,0:T(8,128)S(1)}, f32[6,32,256]{2,1,0:T(8,128)S(1)}, u32[]{:S(2)}, u32[]{:S(2)}) collective-permute-start(f32[6,32,256]{2,1,0:T(8,128)S(1)} %scaled.1.refs_1_), channel_id=1, source_target_pairs={{0,6},{1,7},{2,0},{3,1},{4,2},{5,3},{6,4},{7,5},{8,14},{9,15},{10,... | collective-permute-start | bytes 589832 | tf_op jit(solution)/shard_map/ppermute | solution.py:324
  24.9 9.7 %collective-permute-start.5 = (f32[6,32,256]{2,1,0:T(8,128)S(1)}, f32[6,32,256]{2,1,0:T(8,128)S(1)}, u32[]{:S(2)}, u32[]{:S(2)}) collective-permute-start(f32[6,32,256]{2,1,0:T(8,128)S(1)} %collective-permute-done.3.refs_5_), channel_id=1, source_target_pairs={{0,6},{1,7},{2,0},{3,1},{4,2},{5,3},{6,4},{7,5},{8,14},{9,15},{10,... | collective-permute-start | bytes 589832 | tf_op jit(solution)/shard_map/ppermute | solution.py:324
  44.5 16.6 %collective-permute-start.9 = (f32[3,32,256]{2,1,0:T(8,128)S(1)}, f32[3,32,256]{2,1,0:T(8,128)S(1)}, u32[]{:S(2)}, u32[]{:S(2)}) collective-permute-start(f32[3,32,256]{2,1,0:T(8,128)S(1)} %get-tuple-element.71), channel_id=1, source_target_pairs={{0,16},{16,32},{32,48},{48,64},{64,80},{80,96},{96,112},{112,128},... | collective-permute-start | bytes 294920 | tf_op jit(solution)/shard_map/ppermute | solution.py:324
  47.4 13.6 %collective-permute-start.10 = (f32[3,32,256]{2,1,0:T(8,128)S(1)}, f32[3,32,256]{2,1,0:T(8,128)S(1)}, u32[]{:S(2)}, u32[]{:S(2)}) collective-permute-start(f32[3,32,256]{2,1,0:T(8,128)S(1)} %get-tuple-element.72), channel_id=1, source_target_pairs={{16,0},{32,16},{48,32},{64,48},{80,64},{96,80},{112,96},{128,112},... | collective-permute-start | bytes 294920 | tf_op jit(solution)/shard_map/ppermute | solution.py:324
  61.1 13.4 %collective-permute-start.14 = (f32[6,32,256]{2,1,0:T(8,128)S(1)}, f32[6,32,256]{2,1,0:T(8,128)S(1)}, u32[]{:S(2)}, u32[]{:S(2)}) collective-permute-start(f32[6,32,256]{2,1,0:T(8,128)S(1)} %first_grad.1.refs_1_), channel_id=1, source_target_pairs={{0,8},{1,9},{2,10},{3,11},{4,12},{5,13},{6,14},{7,15},{8,0},{9,1},... | collective-permute-start | bytes 589832 | tf_op jit(solution)/shard_map/ppermute | solution.py:324
  62.0 12.6 %collective-permute-start.13 = (f32[6,32,256]{2,1,0:T(8,128)S(1)}, f32[6,32,256]{2,1,0:T(8,128)S(1)}, u32[]{:S(2)}, u32[]{:S(2)}) collective-permute-start(f32[6,32,256]{2,1,0:T(8,128)S(1)} %first_grad.1.refs_1_), channel_id=1, source_target_pairs={{0,4},{1,5},{2,6},{3,7},{4,0},{5,1},{6,2},{7,3},{8,12},{9,13},{10,... | collective-permute-start | bytes 589832 | tf_op jit(solution)/shard_map/ppermute | solution.py:324
  64.1 10.5 %collective-permute-start.12 = (f32[6,32,256]{2,1,0:T(8,128)S(1)}, f32[6,32,256]{2,1,0:T(8,128)S(1)}, u32[]{:S(2)}, u32[]{:S(2)}) collective-permute-start(f32[6,32,256]{2,1,0:T(8,128)S(1)} %first_grad.1.refs_1_), channel_id=1, source_target_pairs={{0,6},{1,7},{2,0},{3,1},{4,2},{5,3},{6,4},{7,5},{8,14},{9,15},{10,... | collective-permute-start | bytes 589832 | tf_op jit(solution)/shard_map/ppermute | solution.py:324
  74.6 14.0 %collective-permute-start.19 = (f32[864,128]{1,0:T(8,128)S(1)}, f32[864,128]{1,0:T(8,128)S(1)}, u32[]{:S(2)}, u32[]{:S(2)}) collective-permute-start(f32[864,128]{1,0:T(8,128)S(1)} %get-tuple-element.80), channel_id=1, source_target_pairs={{0,128},{16,144},{32,160},{48,176},{64,192},{80,208},{96,224},{112... | collective-permute-start | bytes 1327112 | tf_op jit(solution)/shard_map/ppermute | solution.py:324
  77.0 19.4 %collective-permute-start.20 = (f32[864,128]{1,0:T(8,128)S(1)}, f32[864,128]{1,0:T(8,128)S(1)}, u32[]{:S(2)}, u32[]{:S(2)}) collective-permute-start(f32[864,128]{1,0:T(8,128)S(1)} %get-tuple-element.81), channel_id=1, source_target_pairs={{0,64},{16,80},{32,96},{48,112},{64,128},{80,144},{96,160},{112,17... | collective-permute-start | bytes 1327112 | tf_op jit(solution)/shard_map/ppermute | solution.py:324
  85.7 10.9 %collective-permute-start.18 = (f32[24,32,256]{2,1,0:T(8,128)S(1)}, f32[24,32,256]{2,1,0:T(8,128)S(1)}, u32[]{:S(2)}, u32[]{:S(2)}) collective-permute-start(f32[24,32,256]{2,1,0:T(8,128)S(1)} %pad_maximum_fusion.2), channel_id=1, source_target_pairs={{0,1},{1,0},{2,3},{3,2},{4,5},{5,4},{6,7},{7,6},{8,9},{9,8},{10,11... | collective-permute-start | bytes 2359304 | tf_op jit(solution)/shard_map/ppermute | solution.py:324
  96.4 12.6 %collective-permute-start.30 = (f32[864,128]{1,0:T(8,128)S(1)}, f32[864,128]{1,0:T(8,128)S(1)}, u32[]{:S(2)}, u32[]{:S(2)}) collective-permute-start(f32[864,128]{1,0:T(8,128)S(1)} %get-tuple-element.98), channel_id=1, source_target_pairs={{0,192},{16,208},{32,224},{48,240},{64,0},{80,16},{96,32},{112,48}... | collective-permute-start | bytes 1327112 | tf_op jit(solution)/shard_map/ppermute | solution.py:324
  105.5 14.6 %collective-permute-start.24 = (f32[864,128]{1,0:T(8,128)S(1)}, f32[864,128]{1,0:T(8,128)S(1)}, u32[]{:S(2)}, u32[]{:S(2)}) collective-permute-start(f32[864,128]{1,0:T(8,128)S(1)} %get-tuple-element.90), channel_id=1, source_target_pairs={{0,128},{16,144},{32,160},{48,176},{64,192},{80,208},{96,224},{112... | collective-permute-start | bytes 1327112 | tf_op jit(solution)/shard_map/ppermute | solution.py:324
  105.6 23.1 %collective-permute-start.25 = (f32[864,128]{1,0:T(8,128)S(1)}, f32[864,128]{1,0:T(8,128)S(1)}, u32[]{:S(2)}, u32[]{:S(2)}) collective-permute-start(f32[864,128]{1,0:T(8,128)S(1)} %get-tuple-element.91), channel_id=1, source_target_pairs={{0,64},{16,80},{32,96},{48,112},{64,128},{80,144},{96,160},{112,17... | collective-permute-start | bytes 1327112 | tf_op jit(solution)/shard_map/ppermute | solution.py:324
  107.3 21.5 %collective-permute-start.26 = (f32[864,128]{1,0:T(8,128)S(1)}, f32[864,128]{1,0:T(8,128)S(1)}, u32[]{:S(2)}, u32[]{:S(2)}) collective-permute-start(f32[864,128]{1,0:T(8,128)S(1)} %get-tuple-element.92), channel_id=1, source_target_pairs={{0,192},{16,208},{32,224},{48,240},{64,0},{80,16},{96,32},{112,48}... | collective-permute-start | bytes 1327112 | tf_op jit(solution)/shard_map/ppermute | solution.py:324
  109.7 24.9 %collective-permute-start.31 = (f32[32,864]{1,0:T(8,128)S(1)}, f32[32,864]{1,0:T(8,128)S(1)}, u32[]{:S(2)}, u32[]{:S(2)}) collective-permute-start(f32[32,864]{1,0:T(8,128)S(1)} %get-tuple-element.104), channel_id=1, source_target_pairs={{0,16},{16,32},{32,48},{48,0},{64,80},{80,96},{96,112},{112,64},{1... | collective-permute-start | bytes 331784 | tf_op jit(solution)/shard_map/ppermute | solution.py:324
  111.0 19.7 %collective-permute-start.22 = (f32[1,32,256]{2,1,0:T(8,128)S(1)}, f32[1,32,256]{2,1,0:T(8,128)S(1)}, u32[]{:S(2)}, u32[]{:S(2)}) collective-permute-start(f32[1,32,256]{2,1,0:T(8,128)S(1)} %get-tuple-element.87), channel_id=1, source_target_pairs={{0,16},{16,32},{32,48},{48,64},{64,80},{80,96},{96,112},{112,128},... | collective-permute-start | bytes 98312 | tf_op jit(solution)/shard_map/ppermute | solution.py:324
  120.2 11.6 %collective-permute-start.23 = (f32[1,32,256]{2,1,0:T(8,128)S(1)}, f32[1,32,256]{2,1,0:T(8,128)S(1)}, u32[]{:S(2)}, u32[]{:S(2)}) collective-permute-start(f32[1,32,256]{2,1,0:T(8,128)S(1)} %get-tuple-element.88), channel_id=1, source_target_pairs={{16,0},{32,16},{48,32},{64,48},{80,64},{96,80},{112,96},{128,112},... | collective-permute-start | bytes 98312 | tf_op jit(solution)/shard_map/ppermute | solution.py:324
  128.8 15.4 %collective-permute-start.32 = (f32[32,864]{1,0:T(8,128)S(1)}, f32[32,864]{1,0:T(8,128)S(1)}, u32[]{:S(2)}, u32[]{:S(2)}) collective-permute-start(f32[32,864]{1,0:T(8,128)S(1)} %get-tuple-element.105), channel_id=1, source_target_pairs={{0,32},{16,48},{32,0},{48,16},{64,96},{80,112},{96,64},{112,80},{1... | collective-permute-start | bytes 331784 | tf_op jit(solution)/shard_map/ppermute | solution.py:324
  128.8 15.3 %collective-permute-start.33 = (f32[32,864]{1,0:T(8,128)S(1)}, f32[32,864]{1,0:T(8,128)S(1)}, u32[]{:S(2)}, u32[]{:S(2)}) collective-permute-start(f32[32,864]{1,0:T(8,128)S(1)} %get-tuple-element.106), channel_id=1, source_target_pairs={{0,48},{16,0},{32,16},{48,32},{64,112},{80,64},{96,80},{112,96},{1... | collective-permute-start | bytes 331784 | tf_op jit(solution)/shard_map/ppermute | solution.py:324
  130.7 14.5 %collective-permute-start.27 = (f32[32,864]{1,0:T(8,128)S(1)}, f32[32,864]{1,0:T(8,128)S(1)}, u32[]{:S(2)}, u32[]{:S(2)}) collective-permute-start(f32[32,864]{1,0:T(8,128)S(1)} %get-tuple-element.94), channel_id=1, source_target_pairs={{0,16},{16,32},{32,48},{48,0},{64,80},{80,96},{96,112},{112,64},{1... | collective-permute-start | bytes 331784 | tf_op jit(solution)/shard_map/ppermute | solution.py:324
  131.8 13.9 %collective-permute-start.28 = (f32[32,864]{1,0:T(8,128)S(1)}, f32[32,864]{1,0:T(8,128)S(1)}, u32[]{:S(2)}, u32[]{:S(2)}) collective-permute-start(f32[32,864]{1,0:T(8,128)S(1)} %get-tuple-element.95), channel_id=1, source_target_pairs={{0,32},{16,48},{32,0},{48,16},{64,96},{80,112},{96,64},{112,80},{1... | collective-permute-start | bytes 331784 | tf_op jit(solution)/shard_map/ppermute | solution.py:324
  134.6 11.0 %collective-permute-start.29 = (f32[32,864]{1,0:T(8,128)S(1)}, f32[32,864]{1,0:T(8,128)S(1)}, u32[]{:S(2)}, u32[]{:S(2)}) collective-permute-start(f32[32,864]{1,0:T(8,128)S(1)} %get-tuple-element.96), channel_id=1, source_target_pairs={{0,48},{16,0},{32,16},{48,32},{64,112},{80,64},{96,80},{112,96},{1... | collective-permute-start | bytes 331784 | tf_op jit(solution)/shard_map/ppermute | solution.py:324
  (45 other events, 381.5 us)

commit v2 on v1

--- a/solution.py
+++ b/solution.py
@@ -22,7 +22,7 @@
     return sigma * (1.0 + values * (1.0 - sigma))
 
 
-def call(kernel, out_shape, scratch, args, n_smem=0, flops=0, name=None, fetched=()):
+def call(kernel, out_shape, scratch, args, n_smem=0, flops=0, name=None, fetched=(), vmem=16):
     many = isinstance(out_shape, list)
     moved = sum(a.size * a.dtype.itemsize for a in (*args, *fetched))
     moved += sum(o.size * o.dtype.itemsize for o in (out_shape if many else [out_shape]))
@@ -44,7 +44,7 @@
         in_specs=[SM] * n_smem + [VM] * (n - n_smem) + [pl.BlockSpec(memory_space=pltpu.HBM)] * m,
         out_specs=[VM] * len(out_shape) if many else VM,
         scratch_shapes=scratch,
-        compiler_params=pltpu.CompilerParams(vmem_limit_bytes=16 << 20),
+        compiler_params=pltpu.CompilerParams(vmem_limit_bytes=vmem << 20),
         cost_estimate=pl.CostEstimate(flops=flops, bytes_accessed=moved, transcendentals=0),
         name=name,
     )(*args, *fetched)
@@ -76,70 +76,70 @@
     return plane
 
 
-def scaled_kernel(pre_ref, grad_ref, out_ref):
-    out_ref[...] = grad_ref[...] * slope_of(pre_ref[...])
-
-
-def scaled(pre, grad):
-    return call(scaled_kernel, shape(*pre.shape), [], [pre, grad], name="scaled")
-
-
-def weights_kernel(copies, turn, pre_ref, *outs):
-    slope_ref = outs[-1]
-    slope_ref[...] = slope_of(pre_ref[...])
-    for n, copy in enumerate(copies):
-        source, = arrived([copy])
-        taps, channels, total = source.shape
-        width = total // 4
-        for a in range(3):
-            hi_ref, lo_ref = outs[6 * n + 2 * a:6 * n + 2 * a + 2]
-
-            def one_tap(t, _):
-                at = pl.ds(pl.multiple_of(t * channels, channels), channels)
-                for d in range(4):
-                    lanes = pl.ds(pl.multiple_of(turn[d] * width, width), width)
-                    hi, lo = split(source[t + a * (taps // 3), :, lanes])
-                    hi_ref[at, d * width:(d + 1) * width] = hi
-                    lo_ref[at, d * width:(d + 1) * width] = lo
-                return 0
-
-            lax.fori_loop(0, taps // 3, one_tap, 0)
-
-
-def weight_halves(turn, pre, w1, w2):
-    taps, channels, total = w1.shape
+def weights_kernel(turn, source, *outs):
+    taps, channels, total = source.shape
+    width = total // 4
+    for a in range(3):
+        hi_ref, lo_ref = outs[2 * a:2 * a + 2]
+
+        def one_tap(t, _):
+            at = pl.ds(pl.multiple_of(t * channels, channels), channels)
+            for d in range(4):
+                lanes = pl.ds(pl.multiple_of(turn[d] * width, width), width)
+                hi, lo = split(source[t + a * (taps // 3), :, lanes])
+                hi_ref[at, d * width:(d + 1) * width] = hi
+                lo_ref[at, d * width:(d + 1) * width] = lo
+            return 0
+
+        lax.fori_loop(0, taps // 3, one_tap, 0)
+
+
+def weight_halves(turn, weight, name):
+    taps, channels, total = weight.shape
     flat = shape(taps // 3 * channels, total, dtype=BF16)
-    *halves, slope = call(weights_kernel, [flat] * 12 + [shape(*pre.shape)], [], [turn, pre], 1,
-                          name="weight_halves", fetched=[w2, w1])
-    return halves[:6], halves[6:], slope
-
-
-def inputs_kernel(pre_ref, saved_ref, low_ref, high_ref, h_hi, h_lo, x_hi, x_lo, rows):
-    planes, channels, _ = pre_ref.shape
-    for n, (own, hi_ref, lo_ref) in enumerate(((pre_ref, h_hi, h_lo), (saved_ref, x_hi, x_lo))):
-        rows[0] = low_ref[n + 1]
-        rows[planes + 1] = high_ref[n + 1]
-        rows[1:planes + 1] = own[...]
-
-        def one_plane(q, _):
-            plane = rows[q]
-            if n == 0:
-                plane = plane * jax.nn.sigmoid(plane)
-            lanes = pl.ds(pl.multiple_of(q * AREA, AREA), AREA)
-            for s, (b, c) in enumerate(SHIFTS):
-                hi, lo = split(moved_cells(plane, b, c))
-                hi_ref[s * channels:(s + 1) * channels, lanes] = hi
-                lo_ref[s * channels:(s + 1) * channels, lanes] = lo
-            return 0
-
-        lax.fori_loop(0, planes + 2, one_plane, 0)
-
-
-def input_halves(pre, saved, low, high):
-    planes, channels, area = pre.shape
+    return call(weights_kernel, [flat] * 6, [], [turn, weight], 1, name=name)
+
+
+def second_kernel(turn, source, pre, saved, *outs):
+    *halves, rims, slope = outs
+    for n, p in enumerate((0, slope.shape[0] - 1)):
+        rims[n, 0] = pre[p]
+        rims[n, 1] = saved[p]
+    slope[...] = slope_of(pre[...])
+    weights_kernel(turn, source, *halves)
+
+
+def second_ready(turn, weight, pre, saved):
+    taps, channels, total = weight.shape
+    outs = [shape(taps // 3 * channels, total, dtype=BF16)] * 6 + [shape(2, 2, *pre.shape[1:]), shape(*pre.shape)]
+    return call(second_kernel, outs, [], [turn, weight, pre, saved], 1, name="second_ready")
+
+
+def inputs_kernel(n, own_ref, low_ref, high_ref, hi_ref, lo_ref, rows):
+    planes, channels, _ = own_ref.shape
+    rows[0] = low_ref[n + 1]
+    rows[planes + 1] = high_ref[n + 1]
+    rows[1:planes + 1] = own_ref[...]
+
+    def one_plane(q, _):
+        plane = rows[q]
+        if n == 0:
+            plane = plane * jax.nn.sigmoid(plane)
+        lanes = pl.ds(pl.multiple_of(q * AREA, AREA), AREA)
+        for s, (b, c) in enumerate(SHIFTS):
+            hi, lo = split(moved_cells(plane, b, c))
+            hi_ref[s * channels:(s + 1) * channels, lanes] = hi
+            lo_ref[s * channels:(s + 1) * channels, lanes] = lo
+        return 0
+
+    lax.fori_loop(0, planes + 2, one_plane, 0)
+
+
+def input_halves(n, own, low, high, name):
+    planes, channels, area = own.shape
     tall = shape(len(SHIFTS) * channels, (planes + 2) * area, dtype=BF16)
-    return call(inputs_kernel, [tall] * 4, [pltpu.VMEM((planes + 2, channels, area), F32)],
-                [pre, saved, low, high], name="input_halves")
+    return call(lambda *refs: inputs_kernel(n, *refs), [tall] * 2, [pltpu.VMEM((planes + 2, channels, area), F32)],
+                [own, low, high], name=name)
 
 
 def gather_blocks(spots, pieces, g_hi, g_lo):
@@ -178,20 +178,20 @@
     return g_ref[:, :, lanes].reshape(g_ref.shape[0] * g_ref.shape[1], AREA)
 
 
-def outer_part(g_hi, g_lo, copies, before_ref, behind_ref, edge_refs=()):
+def outer_part(g_hi, g_lo, w_refs, before_ref, behind_ref, rims=None):
     last = g_hi.shape[2] // AREA - 1
-    w_refs = arrived(copies)
     for p, w_hi, w_lo, out in ((0, *w_refs[:2], before_ref), (last, *w_refs[2:], behind_ref)):
         out[0] = spread(three_products(w_hi[...], w_lo[...], plane_of(g_hi, p), plane_of(g_lo, p)))
-        for n, edge in enumerate(edge_refs):
-            out[n + 1] = edge[p]
-
-
-def inner_part(copies, g_hi, g_lo, own_ref, sums):
+        if rims is not None:
+            out[1:] = rims[min(p, 1)]
+
+
+def inner_part(g_hi, g_lo, *refs):
+    weights, (own_ref, sums) = refs[:6], refs[6:]
     planes = own_ref.shape[0]
     third = sums.shape[1]
     for n, a in enumerate((1, 0, 2)):
-        w_hi, w_lo = arrived(copies[2 * n:2 * n + 2])
+        w_hi, w_lo = weights[2 * n:2 * n + 2]
 
         def one_plane(p, _):
             out = three_products(w_hi[...], w_lo[...], plane_of(g_hi, p), plane_of(g_lo, p))
@@ -210,17 +210,17 @@
     lax.fori_loop(0, planes, one_out, 0)
 
 
-def filter_part(g_hi, g_lo, i_hi, i_lo, outs):
-    total = g_hi.shape[0] * g_hi.shape[1]
+def filter_part(g_hi, g_lo, i_hi, i_lo, outs, quarters):
     planes = g_hi.shape[2] // AREA
-    width = total // len(outs)
+    width = outs[0].shape[1]
+    blocks = width // g_hi.shape[1]
     for out in outs:
         out[...] = jnp.zeros_like(out)
 
     def one_plane(p, _):
         lanes = pl.ds(pl.multiple_of(p * AREA, AREA), AREA)
-        hi = g_hi[:, :, lanes].reshape(total, AREA)
-        lo = g_lo[:, :, lanes].reshape(total, AREA)
+        hi, lo = (jnp.concatenate(
+            [g[d * blocks:(d + 1) * blocks, :, lanes].reshape(width, AREA) for d in quarters], 0) for g in (g_hi, g_lo))
         windows = [pl.ds(pl.multiple_of((p + a) * AREA, AREA), AREA) for a in range(3)]
         left_hi = jnp.concatenate([i_hi[:, w] for w in windows], 0)
         left_lo = jnp.concatenate([i_lo[:, w] for w in windows], 0)
@@ -228,33 +228,35 @@
         part = lax.dot_general(left_hi, hi, dims, preferred_element_type=F32)
         part += lax.dot_general(left_hi, lo, dims, preferred_element_type=F32)
         part += lax.dot_general(left_lo, hi, dims, preferred_element_type=F32)
-        for d, out in enumerate(outs):
-            out[...] += part[:, d * width:(d + 1) * width]
+        for n, out in enumerate(outs):
+            out[...] += part[:, n * width:(n + 1) * width]
         return 0
 
     lax.fori_loop(0, planes, one_plane, 0)
 
 
-def first_use(body, spots, pieces, others, outs, flops, name, fetched):
+def first_use(body, spots, pieces, others, outs, flops, name, fetched, vmem=16):
     planes, channels, area = pieces[0].shape
     n, m = len(pieces), len(pieces) + len(others)
     shards = sum(piece.shape[0] for piece in pieces) // planes
     halves = [shape(shards, channels, planes * area, dtype=BF16)] * 2
 
-    def kernel(copies, spots, *refs):
+    def kernel(*refs):
+        copies = refs[0] if fetched else []
+        spots, *refs = refs[1:] if fetched else refs
         g_hi, g_lo = refs[m:m + 2]
         gather_blocks(spots, refs[:n], g_hi, g_lo)
         body(g_hi, g_lo, copies, *refs[n:m], *refs[m + 2:])
 
-    g_hi, g_lo, *rest = call(kernel, halves + outs, [], [spots, *pieces, *others], 1, flops, name, fetched)
+    g_hi, g_lo, *rest = call(kernel, halves + outs, [], [spots, *pieces, *others], 1, flops, name, fetched, vmem)
     return (g_hi, g_lo), rest
 
 
 def inner(halves, weights, planes, flops, name):
     third = weights[0].shape[0]
     channels = third // len(SHIFTS)
-    return call(inner_part, shape(planes, channels, AREA), [pltpu.VMEM((planes, third, AREA), F32)], list(halves),
-                0, flops, name, [*weights[2:4], *weights[:2], *weights[4:]])
+    return call(inner_part, shape(planes, channels, AREA), [pltpu.VMEM((planes, third, AREA), F32)],
+                [*halves, *weights[2:4], *weights[:2], *weights[4:]], 0, flops, name)
 
 
 def turned_kernel(spots, a, b, c, d, *refs):
@@ -338,11 +340,13 @@
 def gathered(own, soon, late):
     far = send(own, FAR)
     near = [own] + [send(own, along_x(d)) for d in (1, 3, 2)]
-    far = after(far, [*near, *soon])
-    near_twin = send(jnp.concatenate(near, 0), TWIN)
+    far = after(far, [*near[1:3], *soon])
     wide = [far] + [send(far, along_x(d)) for d in (1, 3, 2)]
-    result, done = late(far)
-    wide_twin = send(after(jnp.concatenate(wide, 0), done), TWIN)
+    near_all = jnp.concatenate(near, 0)
+    near_twin = send(near_all, TWIN)
+    wide_all = jnp.concatenate(wide, 0)
+    result, done = late(far, near_all, wide_all)
+    wide_twin = send(after(wide_all, done), TWIN)
     return [*near, *wide, near_twin, wide_twin], result
 
 
@@ -350,12 +354,11 @@
     return send(after, UP, "slab"), send(before, DOWN, "slab")
 
 
-def row_sum(parts):
-    return [parts[0]] + [send(parts[d], along_y(d), "slab") for d in (2, 1, 3)]
-
-
-def owner_sum(parts, spots, scale):
-    rows = turned_sum(spots, parts)
+def to_row(part, d):
+    return send(part, along_y(d), "slab")
+
+
+def owner_sum(rows, scale):
     return last_sum([rows[0]] + [send(rows[d], along_z(d), "slab") for d in (1, 2, 3)], scale)
 
 
@@ -371,41 +374,55 @@
     z_spots = ((slab + jnp.arange(4)) % 4).astype(jnp.int32)
     ids = shard_ids()
     spots = (((ids // 4 - slab // 4) % 4) * 4 + ids % 4).astype(jnp.int32)
-    quarters = [shape(rows, total // 4)] * 4
-    second_grad = scaled(pre2, grad)
-    w2, w1, slope = weight_halves(turn, pre1, weight_first, weight_second)
-    pieces, _ = gathered(second_grad, [*w1, *w2, slope], lambda far: ((), []))
+    quarter = shape(rows, total // 4)
+    second_grad = grad * slope_of(pre2)
+    def second_weights_of(_, near, wide):
+        return second_ready(after(turn, [wide]), weight_second, pre1, saved), ()
+
+    pieces, (*w2, rims, slope) = gathered(second_grad, [], second_weights_of)
 
     halves, (before, behind) = first_use(
-        lambda g_hi, g_lo, copies, pre, saved, *outs: outer_part(g_hi, g_lo, copies, *outs, (pre, saved)),
-        spots, pieces, [pre1, saved], [shape(3, channels, area)] * 2, flops // 9, "second_outer", [*w2[:2], *w2[4:]])
+        lambda g_hi, g_lo, _, rims, *refs: outer_part(g_hi, g_lo, refs[:4], *refs[4:], rims),
+        spots, pieces, [rims, *w2[:2], *w2[4:]], [shape(3, channels, area)] * 2, flops // 9, "second_outer", [])
     before, behind = edges(before, behind)
     own = inner(halves, w2, planes, flops, "second_inner")
     first_grad = call(first_kernel, shape(planes, channels, area), [], [own, before, behind, slope], name="first_grad")
-    h_hi, h_lo, x_hi, x_lo = input_halves(pre1, saved, before, behind)
-
-    second_parts = call(lambda g_hi, g_lo, i_hi, i_lo, *outs: filter_part(g_hi, g_lo, i_hi, i_lo, outs),
-                        quarters, [], [*halves, h_hi, h_lo], 0, flops, "second_filter")
-
-    def second_sum(far):
-        rows = row_sum(lax.optimization_barrier((*second_parts, far))[:4])
-        return rows, rows[1:3]
-
-    pieces, second_rows = gathered(first_grad, second_parts, second_sum)
-    halves, first_parts = first_use(
-        lambda g_hi, g_lo, copies, *outs: filter_part(g_hi, g_lo, *arrived(copies), outs),
-        spots, pieces, [], quarters, flops, "first_filter", [x_hi, x_lo])
-    first_rows = row_sum(first_parts)
-    second_rows = lax.optimization_barrier((*second_rows, first_parts[0]))[:4]
-    second_weights = owner_sum(second_rows, z_spots, scale)
-
-    before, behind = call(lambda copies, g_hi, g_lo, *outs: outer_part(g_hi, g_lo, copies, *outs),
-                          [shape(1, channels, area)] * 2, [], list(halves), 0, flops // 9, "first_outer",
-                          [*w1[:2], *w1[4:]])
+    h_hi, h_lo = input_halves(0, pre1, before, behind, "second_input")
+
+    second_parts = call(
+        lambda g_hi, g_lo, i_hi, i_lo, *outs: filter_part(g_hi, g_lo, i_hi, i_lo, outs, range(4)),
+        [quarter] * 4, [], [*halves, h_hi, h_lo], 0, flops, "second_filter")
+
+    def second_sum(far, near, _):
+        parts = lax.optimization_barrier((*second_parts, near))[:4]
+        one, three = to_row(parts[1], 1), to_row(parts[3], 3)
+        two = to_row(after(parts[2], [one, three]), 2)
+        halves = input_halves(1, after(saved, [far]), before, behind, "first_input")
+        return ([parts[0], one, two, three], halves), [one, three, *halves]
+
+    pieces, (second_rows, (x_hi, x_lo)) = gathered(first_grad, second_parts, second_sum)
+    halves, (part_2, part_1) = first_use(
+        lambda g_hi, g_lo, copies, *outs: filter_part(g_hi, g_lo, *arrived(copies), outs, (2, 1)),
+        spots, pieces, [], [quarter] * 2, flops // 2, "first_filter", [x_hi, x_lo])
+    row_2, row_1 = to_row(part_2, 2), to_row(part_1, 1)
+    part_3, part_0 = call(
+        lambda g_hi, g_lo, i_hi, i_lo, *outs: filter_part(g_hi, g_lo, i_hi, i_lo, outs, (3, 0)),
+        [quarter] * 2, [], [*halves, x_hi, x_lo], 0, flops // 2, "first_filter_rest")
+    first_rows = [part_0, row_1, row_2, to_row(part_3, 3)]
+
+    second_rows = lax.optimization_barrier((*second_rows, part_0))[:4]
+    second_rows = turned_sum(z_spots, second_rows)
+    w1 = weight_halves(after(turn, [second_rows[0]]), weight_first, "first_weights")
+    own = inner(halves, w1, planes, flops, "first_inner")
+    first_rows = lax.optimization_barrier((*first_rows, own))[:4]
+    first_rows = turned_sum(z_spots, first_rows)
+    before, behind = call(
+        lambda g_hi, g_lo, *refs: outer_part(g_hi, g_lo, refs[:4], *refs[4:]), [shape(1, channels, area)] * 2, [],
+        [after(halves[0], [first_rows[0]]), halves[1], *w1[:2], *w1[4:]], 0, flops // 9, "first_outer")
+    second_weights = owner_sum(second_rows, scale)
+    first_weights = owner_sum(first_rows, scale)
     before, behind = edges(before, behind)
-    own = inner(halves, w1, planes, flops, "first_inner")
     input_grad = call(input_kernel, shape(planes, channels, area), [], [own, before, behind], name="input_grad")
-    first_weights = owner_sum(first_rows, z_spots, scale)
     return (jnp.transpose(input_grad, (1, 0, 2)), first_weights.reshape(taps, channels, -1),
             second_weights.reshape(taps, channels, -1))
 

time: 148 us -> 138 us (0.932)
  local copies, waits for them, and re-layouts: 11.2 us -> 3.8 us
  waiting for transfers between devices: 40.8 us -> 36.8 us
    unnamed x70 -> x13, local copies, waits for them, and re-layouts: 11.1 us -> 3.03 us
    ppermute x34, waiting for transfers between devices: 40.8 us -> 36.8 us  [send(): return lax.ppermute(value, axis, moves)]
    pallas_call x15 -> x17, Pallas kernels: 40.9 us -> 41.8 us  [call(): pl.pallas_call(whole if fetched else kernel, out_shape=out_shape, in_spec...]
  transfers between devices with their start and end apart: 34 -> 34, of which waited for: 14 -> 12; matrix products, arithmetic and copies ran while one was open for 2% -> 3% of each run, Pallas kernels for 26% -> 28%
where the time goes in v2:
time: 138 us; the launch traced here: 136 us
  starting transfers between devices  50.5 us (37%)
  Pallas kernels  41.8 us (30%)
  waiting for transfers between devices  36.8 us (27%)
  local copies, waits for them, and re-layouts  3.8 us (3%)
  other arithmetic  2.21 us (2%)
    ppermute x34, starting transfers between devices, send(): return lax.ppermute(value, axis, moves)  50.5 us
    pallas_call x17, Pallas kernels, call(): pl.pallas_call(whole if fetched else kernel, out_shape=out_shape, in_spec...  41.8 us
    ppermute x34, waiting for transfers between devices, send(): return lax.ppermute(value, axis, moves)  36.8 us
    unnamed x13, local copies, waits for them, and re-layouts  3.03 us
  transfers between devices with their start and end apart: 34, of which 12 were waited for; matrix products, arithmetic and copies ran while one was open for 3% of the time, Pallas kernels for 28%

profile of v2, /device:TPU:8, one launch (start us, length us, event | category | flops | bytes accessed | tf_op | source)
XLA Modules:
  0.0 136.1 jit_solution(2307704384108450042)
XLA Ops:
  1.8 7.3 %collective-permute-start.3 = (f32[6,32,256]{2,1,0:T(8,128)S(1)}, f32[6,32,256]{2,1,0:T(8,128)S(1)}, u32[]{:S(2)}, u32[]{:S(2)}) collective-permute-start(f32[6,32,256]{2,1,0:T(8,128)S(1)} %fusion.5.refs_1_), channel_id=1, source_target_pairs={{0,8},{1,9},{2,10},{3,11},{4,12},{5,13},{6,14},{7,15},{8,0},{9,1},... | collective-permute-start | bytes 589832 | tf_op jit(solution)/shard_map/ppermute | solution.py:326
  9.0 2.8 %collective-permute-start.1 = (f32[6,32,256]{2,1,0:T(8,128)S(1)}, f32[6,32,256]{2,1,0:T(8,128)S(1)}, u32[]{:S(2)}, u32[]{:S(2)}) collective-permute-start(f32[6,32,256]{2,1,0:T(8,128)S(1)} %fusion.5.refs_1_), channel_id=1, source_target_pairs={{0,6},{1,7},{2,0},{3,1},{4,2},{5,3},{6,4},{7,5},{8,14},{9,15},{10,... | collective-permute-start | bytes 589832 | tf_op jit(solution)/shard_map/ppermute | solution.py:326
  11.8 2.3 %collective-permute-start.2 = (f32[6,32,256]{2,1,0:T(8,128)S(1)}, f32[6,32,256]{2,1,0:T(8,128)S(1)}, u32[]{:S(2)}, u32[]{:S(2)}) collective-permute-start(f32[6,32,256]{2,1,0:T(8,128)S(1)} %fusion.5.refs_1_), channel_id=1, source_target_pairs={{0,4},{1,5},{2,6},{3,7},{4,0},{5,1},{6,2},{7,3},{8,12},{9,13},{10,... | collective-permute-start | bytes 589832 | tf_op jit(solution)/shard_map/ppermute | solution.py:326
  14.1 9.0 %collective-permute-done.1.refs_3_ = f32[6,32,256]{2,1,0:T(8,128)S(1)} collective-permute-done((f32[6,32,256]{2,1,0:T(8,128)S(1)}, f32[6,32,256]{2,1,0:T(8,128)S(1)}, u32[]{:S(2)}, u32[]{:S(2)}) %collective-permute-start.1) | collective-permute-done | bytes 196640 | tf_op jit(solution)/shard_map/ppermute | solution.py:326
  23.1 2.9 %collective-permute-done.refs_2_ = f32[6,32,256]{2,1,0:T(8,128)S(1)} collective-permute-done((f32[6,32,256]{2,1,0:T(8,128)S(1)}, f32[6,32,256]{2,1,0:T(8,128)S(1)}, u32[]{:S(2)}, u32[]{:S(2)}) %collective-permute-start) | collective-permute-done | bytes 196640 | tf_op jit(solution)/shard_map/ppermute | solution.py:326
  29.6 5.6 %collective-permute-done.4.refs_6_ = f32[6,32,256]{2,1,0:T(8,128)S(1)} collective-permute-done((f32[6,32,256]{2,1,0:T(8,128)S(1)}, f32[6,32,256]{2,1,0:T(8,128)S(1)}, u32[]{:S(2)}, u32[]{:S(2)}) %collective-permute-start.4) | collective-permute-done | bytes 196640 | tf_op jit(solution)/shard_map/ppermute | solution.py:326
  39.9 2.6 %second_outer.1 = (bf16[16,32,1536]{2,1,0:T(8,128)(2,1)S(1)}, bf16[16,32,1536]{2,1,0:T(8,128)(2,1)S(1)}, f32[3,32,256]{2,1,0:T(8,128)S(1)}, f32[3,32,256]{2,1,0:T(8,128)S(1)}) custom-call(s32[16]{0:T(128)S(1)} %fusion.6.refs_0_, f32[6,32,256]{2,1,0:T(8,128)S(1)} %fusion.5.refs_1_, f32[6,32,256]{2,1,0:T(8,128)S(1)} %collective-permute-done.refs_2_, ...), custom_call_target="tpu_custom_call" | custom-call | flops 452984832 | bytes 7798848 | tf_op jit(solution)/shard_map/second_outer/pallas_call | solution.py:41
  42.6 2.9 %collective-permute-start.9 = (f32[3,32,256]{2,1,0:T(8,128)S(1)}, f32[3,32,256]{2,1,0:T(8,128)S(1)}, u32[]{:S(2)}, u32[]{:S(2)}) collective-permute-start(f32[3,32,256]{2,1,0:T(8,128)S(1)} %get-tuple-element.76), channel_id=1, source_target_pairs={{0,16},{16,32},{32,48},{48,64},{64,80},{80,96},{96,112},{112,128},... | collective-permute-start | bytes 294920 | tf_op jit(solution)/shard_map/ppermute | solution.py:326
  45.5 5.6 %collective-permute-start.10 = (f32[3,32,256]{2,1,0:T(8,128)S(1)}, f32[3,32,256]{2,1,0:T(8,128)S(1)}, u32[]{:S(2)}, u32[]{:S(2)}) collective-permute-start(f32[3,32,256]{2,1,0:T(8,128)S(1)} %get-tuple-element.77), channel_id=1, source_target_pairs={{16,0},{32,16},{48,32},{64,48},{80,64},{96,80},{112,96},{128,112},... | collective-permute-start | bytes 294920 | tf_op jit(solution)/shard_map/ppermute | solution.py:326
  51.1 7.5 %second_inner.1.own = f32[6,32,256]{2,1,0:T(8,128)S(1)} custom-call(bf16[16,32,1536]{2,1,0:T(8,128)(2,1)S(1)} %get-tuple-element.72.g_hi, bf16[16,32,1536]{2,1,0:T(8,128)(2,1)S(1)} %get-tuple-element.73.g_lo, bf16[288,512]{1,0:T(8,128)(2,1)S(1)} %get-tuple-element.74.refs_0_, bf16[288,512]{1,0:T(8,128)(2,1)S(1)} %get-tuple-element.75.refs_1_, ...), custom_call_target="tpu_custom_call" | custom-call | flops 4076863488 | bytes 5111808 | tf_op jit(solution)/shard_map/second_inner/pallas_call | solution.py:41
  62.6 5.6 %second_filter.1 = (f32[864,128]{1,0:T(8,128)S(1)}, f32[864,128]{1,0:T(8,128)S(1)}, f32[864,128]{1,0:T(8,128)S(1)}, f32[864,128]{1,0:T(8,128)S(1)}) custom-call(bf16[16,32,1536]{2,1,0:T(8,128)(2,1)S(1)} %get-tuple-element.72.g_hi, bf16[16,32,1536]{2,1,0:T(8,128)(2,1)S(1)} %get-tuple-element.73.g_lo, bf16[288,2048]{1,0:T(8,128)(2,1)S(1)} %get-tuple-element.79.i_hi, ...), custom_call_target="tpu_custom_call" | custom-call | flops 4076863488 | bytes 7274496 | tf_op jit(solution)/shard_map/second_filter/pallas_call | solution.py:41
  68.9 2.1 %collective-permute-done.11.refs_2_ = f32[6,32,256]{2,1,0:T(8,128)S(1)} collective-permute-done((f32[6,32,256]{2,1,0:T(8,128)S(1)}, f32[6,32,256]{2,1,0:T(8,128)S(1)}, u32[]{:S(2)}, u32[]{:S(2)}) %collective-permute-start.11) | collective-permute-done | bytes 196640 | tf_op jit(solution)/shard_map/ppermute | solution.py:326
  71.1 1.8 %collective-permute-start.19 = (f32[864,128]{1,0:T(8,128)S(1)}, f32[864,128]{1,0:T(8,128)S(1)}, u32[]{:S(2)}, u32[]{:S(2)}) collective-permute-start(f32[864,128]{1,0:T(8,128)S(1)} %get-tuple-element.86), channel_id=1, source_target_pairs={{0,64},{16,80},{32,96},{48,112},{64,128},{80,144},{96,160},{112,17... | collective-permute-start | bytes 1327112 | tf_op jit(solution)/shard_map/ppermute | solution.py:326
  77.5 5.2 %collective-permute-done.17.refs_8_ = f32[6,32,256]{2,1,0:T(8,128)S(1)} collective-permute-done((f32[6,32,256]{2,1,0:T(8,128)S(1)}, f32[6,32,256]{2,1,0:T(8,128)S(1)}, u32[]{:S(2)}, u32[]{:S(2)}) %collective-permute-start.17) | collective-permute-done | bytes 196640 | tf_op jit(solution)/shard_map/ppermute | solution.py:326
  83.3 2.1 %collective-permute-done.15.refs_6_ = f32[6,32,256]{2,1,0:T(8,128)S(1)} collective-permute-done((f32[6,32,256]{2,1,0:T(8,128)S(1)}, f32[6,32,256]{2,1,0:T(8,128)S(1)}, u32[]{:S(2)}, u32[]{:S(2)}) %collective-permute-start.15) | collective-permute-done | bytes 196640 | tf_op jit(solution)/shard_map/ppermute | solution.py:326
  85.5 2.4 %collective-permute-start.22 = (f32[864,128]{1,0:T(8,128)S(1)}, f32[864,128]{1,0:T(8,128)S(1)}, u32[]{:S(2)}, u32[]{:S(2)}) collective-permute-start(f32[864,128]{1,0:T(8,128)S(1)} %get-tuple-element.96), channel_id=1, source_target_pairs={{0,128},{16,144},{32,160},{48,176},{64,192},{80,208},{96,224},{112... | collective-permute-start | bytes 1327112 | tf_op jit(solution)/shard_map/ppermute | solution.py:326
  87.9 4.9 %first_filter.1 = (bf16[16,32,1536]{2,1,0:T(8,128)(2,1)S(1)}, bf16[16,32,1536]{2,1,0:T(8,128)(2,1)S(1)}, f32[864,128]{1,0:T(8,128)S(1)}, f32[864,128]{1,0:T(8,128)S(1)}) custom-call(s32[16]{0:T(128)S(1)} %fusion.6.refs_0_, f32[6,32,256]{2,1,0:T(8,128)S(1)} %first_grad.1.refs_1_, f32[6,32,256]{2,1,0:T(8,128)S(1)} %collective-permute-done.11.refs_2_, ...), custom_call_target="tpu_custom_call" | custom-call | flops 2038431744 | bytes 9535552 | tf_op jit(solution)/shard_map/first_filter/pallas_call | solution.py:41
  94.3 2.3 %collective-permute-start.24 = (f32[864,128]{1,0:T(8,128)S(1)}, f32[864,128]{1,0:T(8,128)S(1)}, u32[]{:S(2)}, u32[]{:S(2)}) collective-permute-start(f32[864,128]{1,0:T(8,128)S(1)} %get-tuple-element.111), channel_id=1, source_target_pairs={{0,128},{16,144},{32,160},{48,176},{64,192},{80,208},{96,224},{112... | collective-permute-start | bytes 1327112 | tf_op jit(solution)/shard_map/ppermute | solution.py:326
  96.6 3.4 %first_filter_rest.1 = (f32[864,128]{1,0:T(8,128)S(1)}, f32[864,128]{1,0:T(8,128)S(1)}) custom-call(bf16[16,32,1536]{2,1,0:T(8,128)(2,1)S(1)} %get-tuple-element.118.g_hi, bf16[16,32,1536]{2,1,0:T(8,128)(2,1)S(1)} %get-tuple-element.93.g_lo, bf16[288,2048]{1,0:T(8,128)(2,1)S(1)} %get-tuple-element.89.refs_11_.i_hi, ...), custom_call_target="tpu_custom_call" | custom-call | flops 2038431744 | bytes 6389760 | tf_op jit(solution)/shard_map/first_filter_rest/pallas_call | solution.py:41
  103.3 6.4 %collective-permute-done.23.b = f32[864,128]{1,0:T(8,128)S(1)} collective-permute-done((f32[864,128]{1,0:T(8,128)S(1)}, f32[864,128]{1,0:T(8,128)S(1)}, u32[]{:S(2)}, u32[]{:S(2)}) %collective-permute-start.23) | collective-permute-done | bytes 442400 | tf_op jit(solution)/shard_map/ppermute | solution.py:326
  109.7 7.5 %first_inner.1.own = f32[6,32,256]{2,1,0:T(8,128)S(1)} custom-call(bf16[16,32,1536]{2,1,0:T(8,128)(2,1)S(1)} %get-tuple-element.118.g_hi, bf16[16,32,1536]{2,1,0:T(8,128)(2,1)S(1)} %get-tuple-element.93.g_lo, bf16[288,512]{1,0:T(8,128)(2,1)S(1)} %get-tuple-element.104.refs_0_, bf16[288,512]{1,0:T(8,128)(2,1)S(1)} %get-tuple-element.105.refs_1_, ...), custom_call_target="tpu_custom_call" | custom-call | flops 4076863488 | bytes 5111808 | tf_op jit(solution)/shard_map/first_inner/pallas_call | solution.py:41
  120.4 3.1 %collective-permute-start.30 = (f32[32,864]{1,0:T(8,128)S(1)}, f32[32,864]{1,0:T(8,128)S(1)}, u32[]{:S(2)}, u32[]{:S(2)}) collective-permute-start(f32[32,864]{1,0:T(8,128)S(1)} %get-tuple-element.123), channel_id=1, source_target_pairs={{0,48},{16,0},{32,16},{48,32},{64,112},{80,64},{96,80},{112,96},{1... | collective-permute-start | bytes 331784 | tf_op jit(solution)/shard_map/ppermute | solution.py:326
  124.3 2.5 %collective-permute-start.26 = (f32[1,32,256]{2,1,0:T(8,128)S(1)}, f32[1,32,256]{2,1,0:T(8,128)S(1)}, u32[]{:S(2)}, u32[]{:S(2)}) collective-permute-start(f32[1,32,256]{2,1,0:T(8,128)S(1)} %get-tuple-element.119), channel_id=1, source_target_pairs={{0,16},{16,32},{32,48},{48,64},{64,80},{80,96},{96,112},{112,128},... | collective-permute-start | bytes 98312 | tf_op jit(solution)/shard_map/ppermute | solution.py:326
  126.8 6.1 %collective-permute-start.27 = (f32[1,32,256]{2,1,0:T(8,128)S(1)}, f32[1,32,256]{2,1,0:T(8,128)S(1)}, u32[]{:S(2)}, u32[]{:S(2)}) collective-permute-start(f32[1,32,256]{2,1,0:T(8,128)S(1)} %get-tuple-element.120), channel_id=1, source_target_pairs={{16,0},{32,16},{48,32},{64,48},{80,64},{96,80},{112,96},{128,112},... | collective-permute-start | bytes 98312 | tf_op jit(solution)/shard_map/ppermute | solution.py:326
  (83 shorter events, 31.4 us)
Async XLA Ops:
  1.8 12.3 %collective-permute-start.3 = (f32[6,32,256]{2,1,0:T(8,128)S(1)}, f32[6,32,256]{2,1,0:T(8,128)S(1)}, u32[]{:S(2)}, u32[]{:S(2)}) collective-permute-start(f32[6,32,256]{2,1,0:T(8,128)S(1)} %fusion.5.refs_1_), channel_id=1, source_target_pairs={{0,8},{1,9},{2,10},{3,11},{4,12},{5,13},{6,14},{7,15},{8,0},{9,1},... | collective-permute-start | bytes 589832 | tf_op jit(solution)/shard_map/ppermute | solution.py:326
  9.0 14.0 %collective-permute-start.1 = (f32[6,32,256]{2,1,0:T(8,128)S(1)}, f32[6,32,256]{2,1,0:T(8,128)S(1)}, u32[]{:S(2)}, u32[]{:S(2)}) collective-permute-start(f32[6,32,256]{2,1,0:T(8,128)S(1)} %fusion.5.refs_1_), channel_id=1, source_target_pairs={{0,6},{1,7},{2,0},{3,1},{4,2},{5,3},{6,4},{7,5},{8,14},{9,15},{10,... | collective-permute-start | bytes 589832 | tf_op jit(solution)/shard_map/ppermute | solution.py:326
  11.8 14.1 %collective-permute-start = (f32[6,32,256]{2,1,0:T(8,128)S(1)}, f32[6,32,256]{2,1,0:T(8,128)S(1)}, u32[]{:S(2)}, u32[]{:S(2)}) collective-permute-start(f32[6,32,256]{2,1,0:T(8,128)S(1)} %fusion.5.refs_1_), channel_id=1, source_target_pairs={{0,2},{1,3},{2,4},{3,5},{4,6},{5,7},{6,0},{7,1},{8,10},{9,11},{10,... | collective-permute-start | bytes 589832 | tf_op jit(solution)/shard_map/ppermute | solution.py:326
  11.8 16.2 %collective-permute-start.2 = (f32[6,32,256]{2,1,0:T(8,128)S(1)}, f32[6,32,256]{2,1,0:T(8,128)S(1)}, u32[]{:S(2)}, u32[]{:S(2)}) collective-permute-start(f32[6,32,256]{2,1,0:T(8,128)S(1)} %fusion.5.refs_1_), channel_id=1, source_target_pairs={{0,4},{1,5},{2,6},{3,7},{4,0},{5,1},{6,2},{7,3},{8,12},{9,13},{10,... | collective-permute-start | bytes 589832 | tf_op jit(solution)/shard_map/ppermute | solution.py:326
  25.9 10.7 %collective-permute-start.6 = (f32[6,32,256]{2,1,0:T(8,128)S(1)}, f32[6,32,256]{2,1,0:T(8,128)S(1)}, u32[]{:S(2)}, u32[]{:S(2)}) collective-permute-start(f32[6,32,256]{2,1,0:T(8,128)S(1)} %collective-permute-done.3.refs_5_), channel_id=1, source_target_pairs={{0,4},{1,5},{2,6},{3,7},{4,0},{5,1},{6,2},{7,3},{8,12},{9,13},{10,... | collective-permute-start | bytes 589832 | tf_op jit(solution)/shard_map/ppermute | solution.py:326
  25.9 10.0 %collective-permute-start.5 = (f32[6,32,256]{2,1,0:T(8,128)S(1)}, f32[6,32,256]{2,1,0:T(8,128)S(1)}, u32[]{:S(2)}, u32[]{:S(2)}) collective-permute-start(f32[6,32,256]{2,1,0:T(8,128)S(1)} %collective-permute-done.3.refs_5_), channel_id=1, source_target_pairs={{0,6},{1,7},{2,0},{3,1},{4,2},{5,3},{6,4},{7,5},{8,14},{9,15},{10,... | collective-permute-start | bytes 589832 | tf_op jit(solution)/shard_map/ppermute | solution.py:326
  28.9 10.6 %collective-permute-start.7 = (f32[24,32,256]{2,1,0:T(8,128)}, f32[24,32,256]{2,1,0:T(8,128)}, u32[]{:S(2)}, u32[]{:S(2)}) collective-permute-start(f32[24,32,256]{2,1,0:T(8,128)} %pad_maximum_fusion), channel_id=1, source_target_pairs={{0,1},{1,0},{2,3},{3,2},{4,5},{5,4},{6,7},{7,6},{8,9},{9,8},{10,11... | collective-permute-start | bytes 2359304 | tf_op jit(solution)/shard_map/ppermute | solution.py:326
  42.6 16.1 %collective-permute-start.9 = (f32[3,32,256]{2,1,0:T(8,128)S(1)}, f32[3,32,256]{2,1,0:T(8,128)S(1)}, u32[]{:S(2)}, u32[]{:S(2)}) collective-permute-start(f32[3,32,256]{2,1,0:T(8,128)S(1)} %get-tuple-element.76), channel_id=1, source_target_pairs={{0,16},{16,32},{32,48},{48,64},{64,80},{80,96},{96,112},{112,128},... | collective-permute-start | bytes 294920 | tf_op jit(solution)/shard_map/ppermute | solution.py:326
  45.5 13.2 %collective-permute-start.10 = (f32[3,32,256]{2,1,0:T(8,128)S(1)}, f32[3,32,256]{2,1,0:T(8,128)S(1)}, u32[]{:S(2)}, u32[]{:S(2)}) collective-permute-start(f32[3,32,256]{2,1,0:T(8,128)S(1)} %get-tuple-element.77), channel_id=1, source_target_pairs={{16,0},{32,16},{48,32},{64,48},{80,64},{96,80},{112,96},{128,112},... | collective-permute-start | bytes 294920 | tf_op jit(solution)/shard_map/ppermute | solution.py:326
  58.7 14.6 %collective-permute-start.14 = (f32[6,32,256]{2,1,0:T(8,128)S(1)}, f32[6,32,256]{2,1,0:T(8,128)S(1)}, u32[]{:S(2)}, u32[]{:S(2)}) collective-permute-start(f32[6,32,256]{2,1,0:T(8,128)S(1)} %first_grad.1.refs_1_), channel_id=1, source_target_pairs={{0,8},{1,9},{2,10},{3,11},{4,12},{5,13},{6,14},{7,15},{8,0},{9,1},... | collective-permute-start | bytes 589832 | tf_op jit(solution)/shard_map/ppermute | solution.py:326
  60.2 10.8 %collective-permute-start.11 = (f32[6,32,256]{2,1,0:T(8,128)S(1)}, f32[6,32,256]{2,1,0:T(8,128)S(1)}, u32[]{:S(2)}, u32[]{:S(2)}) collective-permute-start(f32[6,32,256]{2,1,0:T(8,128)S(1)} %first_grad.1.refs_1_), channel_id=1, source_target_pairs={{0,2},{1,3},{2,4},{3,5},{4,6},{5,7},{6,0},{7,1},{8,10},{9,11},{10,... | collective-permute-start | bytes 589832 | tf_op jit(solution)/shard_map/ppermute | solution.py:326
  71.1 14.3 %collective-permute-start.19 = (f32[864,128]{1,0:T(8,128)S(1)}, f32[864,128]{1,0:T(8,128)S(1)}, u32[]{:S(2)}, u32[]{:S(2)}) collective-permute-start(f32[864,128]{1,0:T(8,128)S(1)} %get-tuple-element.86), channel_id=1, source_target_pairs={{0,64},{16,80},{32,96},{48,112},{64,128},{80,144},{96,160},{112,17... | collective-permute-start | bytes 1327112 | tf_op jit(solution)/shard_map/ppermute | solution.py:326
  72.9 12.5 %collective-permute-start.20 = (f32[864,128]{1,0:T(8,128)S(1)}, f32[864,128]{1,0:T(8,128)S(1)}, u32[]{:S(2)}, u32[]{:S(2)}) collective-permute-start(f32[864,128]{1,0:T(8,128)S(1)} %get-tuple-element.87), channel_id=1, source_target_pairs={{0,192},{16,208},{32,224},{48,240},{64,0},{80,16},{96,32},{112,48}... | collective-permute-start | bytes 1327112 | tf_op jit(solution)/shard_map/ppermute | solution.py:326
  74.8 10.5 %collective-permute-start.15 = (f32[6,32,256]{2,1,0:T(8,128)S(1)}, f32[6,32,256]{2,1,0:T(8,128)S(1)}, u32[]{:S(2)}, u32[]{:S(2)}) collective-permute-start(f32[6,32,256]{2,1,0:T(8,128)S(1)} %collective-permute-done.14.refs_5_), channel_id=1, source_target_pairs={{0,2},{1,3},{2,4},{3,5},{4,6},{5,7},{6,0},{7,1},{8,10},{9,11},{10,... | collective-permute-start | bytes 589832 | tf_op jit(solution)/shard_map/ppermute | solution.py:326
  85.5 15.7 %collective-permute-start.22 = (f32[864,128]{1,0:T(8,128)S(1)}, f32[864,128]{1,0:T(8,128)S(1)}, u32[]{:S(2)}, u32[]{:S(2)}) collective-permute-start(f32[864,128]{1,0:T(8,128)S(1)} %get-tuple-element.96), channel_id=1, source_target_pairs={{0,128},{16,144},{32,160},{48,176},{64,192},{80,208},{96,224},{112... | collective-permute-start | bytes 1327112 | tf_op jit(solution)/shard_map/ppermute | solution.py:326
  92.8 17.0 %collective-permute-start.23 = (f32[864,128]{1,0:T(8,128)S(1)}, f32[864,128]{1,0:T(8,128)S(1)}, u32[]{:S(2)}, u32[]{:S(2)}) collective-permute-start(f32[864,128]{1,0:T(8,128)S(1)} %get-tuple-element.110), channel_id=1, source_target_pairs={{0,64},{16,80},{32,96},{48,112},{64,128},{80,144},{96,160},{112,17... | collective-permute-start | bytes 1327112 | tf_op jit(solution)/shard_map/ppermute | solution.py:326
  94.3 23.0 %collective-permute-start.24 = (f32[864,128]{1,0:T(8,128)S(1)}, f32[864,128]{1,0:T(8,128)S(1)}, u32[]{:S(2)}, u32[]{:S(2)}) collective-permute-start(f32[864,128]{1,0:T(8,128)S(1)} %get-tuple-element.111), channel_id=1, source_target_pairs={{0,128},{16,144},{32,160},{48,176},{64,192},{80,208},{96,224},{112... | collective-permute-start | bytes 1327112 | tf_op jit(solution)/shard_map/ppermute | solution.py:326
  100.0 18.5 %collective-permute-start.25 = (f32[864,128]{1,0:T(8,128)S(1)}, f32[864,128]{1,0:T(8,128)S(1)}, u32[]{:S(2)}, u32[]{:S(2)}) collective-permute-start(f32[864,128]{1,0:T(8,128)S(1)} %get-tuple-element.112), channel_id=1, source_target_pairs={{0,192},{16,208},{32,224},{48,240},{64,0},{80,16},{96,32},{112,48}... | collective-permute-start | bytes 1327112 | tf_op jit(solution)/shard_map/ppermute | solution.py:326
  102.0 18.4 %collective-permute-start.31 = (f32[32,864]{1,0:T(8,128)S(1)}, f32[32,864]{1,0:T(8,128)S(1)}, u32[]{:S(2)}, u32[]{:S(2)}) collective-permute-start(f32[32,864]{1,0:T(8,128)S(1)} %get-tuple-element.124), channel_id=1, source_target_pairs={{0,16},{16,32},{32,48},{48,0},{64,80},{80,96},{96,112},{112,64},{1... | collective-permute-start | bytes 331784 | tf_op jit(solution)/shard_map/ppermute | solution.py:326
  102.1 22.2 %collective-permute-start.32 = (f32[32,864]{1,0:T(8,128)S(1)}, f32[32,864]{1,0:T(8,128)S(1)}, u32[]{:S(2)}, u32[]{:S(2)}) collective-permute-start(f32[32,864]{1,0:T(8,128)S(1)} %get-tuple-element.125), channel_id=1, source_target_pairs={{0,32},{16,48},{32,0},{48,16},{64,96},{80,112},{96,64},{112,80},{1... | collective-permute-start | bytes 331784 | tf_op jit(solution)/shard_map/ppermute | solution.py:326
  109.7 17.1 %collective-permute-start.33 = (f32[32,864]{1,0:T(8,128)S(1)}, f32[32,864]{1,0:T(8,128)S(1)}, u32[]{:S(2)}, u32[]{:S(2)}) collective-permute-start(f32[32,864]{1,0:T(8,128)S(1)} %get-tuple-element.126), channel_id=1, source_target_pairs={{0,48},{16,0},{32,16},{48,32},{64,112},{80,64},{96,80},{112,96},{1... | collective-permute-start | bytes 331784 | tf_op jit(solution)/shard_map/ppermute | solution.py:326
  119.4 15.8 %collective-permute-start.28 = (f32[32,864]{1,0:T(8,128)S(1)}, f32[32,864]{1,0:T(8,128)S(1)}, u32[]{:S(2)}, u32[]{:S(2)}) collective-permute-start(f32[32,864]{1,0:T(8,128)S(1)} %get-tuple-element.121), channel_id=1, source_target_pairs={{0,16},{16,32},{32,48},{48,0},{64,80},{80,96},{96,112},{112,64},{1... | collective-permute-start | bytes 331784 | tf_op jit(solution)/shard_map/ppermute | solution.py:326
  120.4 14.7 %collective-permute-start.29 = (f32[32,864]{1,0:T(8,128)S(1)}, f32[32,864]{1,0:T(8,128)S(1)}, u32[]{:S(2)}, u32[]{:S(2)}) collective-permute-start(f32[32,864]{1,0:T(8,128)S(1)} %get-tuple-element.122), channel_id=1, source_target_pairs={{0,32},{16,48},{32,0},{48,16},{64,96},{80,112},{96,64},{112,80},{1... | collective-permute-start | bytes 331784 | tf_op jit(solution)/shard_map/ppermute | solution.py:326
  120.4 14.7 %collective-permute-start.30 = (f32[32,864]{1,0:T(8,128)S(1)}, f32[32,864]{1,0:T(8,128)S(1)}, u32[]{:S(2)}, u32[]{:S(2)}) collective-permute-start(f32[32,864]{1,0:T(8,128)S(1)} %get-tuple-element.123), channel_id=1, source_target_pairs={{0,48},{16,0},{32,16},{48,32},{64,112},{80,64},{96,80},{112,96},{1... | collective-permute-start | bytes 331784 | tf_op jit(solution)/shard_map/ppermute | solution.py:326
  (15 other events, 156.3 us)

commit v3 on v2

--- a/solution.py
+++ b/solution.py
@@ -104,7 +104,7 @@
     *halves, rims, slope = outs
     for n, p in enumerate((0, slope.shape[0] - 1)):
         rims[n, 0] = pre[p]
-        rims[n, 1] = saved[p]
+        rims[n, 1] = saved[n]
     slope[...] = slope_of(pre[...])
     weights_kernel(turn, source, *halves)
 
@@ -174,7 +174,7 @@
 
 
 def plane_of(g_ref, p):
-    lanes = pl.ds(pl.multiple_of(p * AREA, AREA), AREA)
+    lanes = pl.ds(p * AREA if isinstance(p, int) else pl.multiple_of(p * AREA, AREA), AREA)
     return g_ref[:, :, lanes].reshape(g_ref.shape[0] * g_ref.shape[1], AREA)
 
 
@@ -189,25 +189,25 @@
 def inner_part(g_hi, g_lo, *refs):
     weights, (own_ref, sums) = refs[:6], refs[6:]
     planes = own_ref.shape[0]
-    third = sums.shape[1]
-    for n, a in enumerate((1, 0, 2)):
-        w_hi, w_lo = weights[2 * n:2 * n + 2]
-
-        def one_plane(p, _):
-            out = three_products(w_hi[...], w_lo[...], plane_of(g_hi, p), plane_of(g_lo, p))
-            if a == 1:
-                sums[p] = out
-            else:
-                sums[p + a - 1] += out
-            return 0
-
-        lax.fori_loop(max(0, 1 - a), planes - max(0, a - 1), one_plane, 0)
-
-    def one_out(p, _):
-        own_ref[p] = spread(sums[p])
+
+    def add_up(q, taps):
+        total = None
+        for a in taps:
+            out = three_products(weights[2 * a][...], weights[2 * a + 1][...],
+                                 plane_of(g_hi, q + 1 - a), plane_of(g_lo, q + 1 - a))
+            total = out if total is None else total + out
+        sums[q % 2] = total
+
+    def one_plane(q, _):
+        add_up(q, (0, 1, 2))
+        own_ref[q - 1] = spread(sums.at[(q - 1) % 2])
         return 0
 
-    lax.fori_loop(0, planes, one_out, 0)
+    add_up(0, (0, 1))
+    lax.fori_loop(1, planes - 1, one_plane, 0)
+    add_up(planes - 1, (1, 2))
+    own_ref[planes - 2] = spread(sums.at[(planes - 2) % 2])
+    own_ref[planes - 1] = spread(sums.at[(planes - 1) % 2])
 
 
 def filter_part(g_hi, g_lo, i_hi, i_lo, outs, quarters):
@@ -255,8 +255,8 @@
 def inner(halves, weights, planes, flops, name):
     third = weights[0].shape[0]
     channels = third // len(SHIFTS)
-    return call(inner_part, shape(planes, channels, AREA), [pltpu.VMEM((planes, third, AREA), F32)],
-                [*halves, *weights[2:4], *weights[:2], *weights[4:]], 0, flops, name)
+    return call(inner_part, shape(planes, channels, AREA), [pltpu.VMEM((2, third, AREA), F32)],
+                [*halves, *weights], 0, flops, name)
 
 
 def turned_kernel(spots, a, b, c, d, *refs):
@@ -377,7 +377,7 @@
     quarter = shape(rows, total // 4)
     second_grad = grad * slope_of(pre2)
     def second_weights_of(_, near, wide):
-        return second_ready(after(turn, [wide]), weight_second, pre1, saved), ()
+        return second_ready(after(turn, [wide]), weight_second, pre1, jnp.stack([saved[0], saved[planes - 1]])), ()
 
     pieces, (*w2, rims, slope) = gathered(second_grad, [], second_weights_of)
 
@@ -413,12 +413,12 @@
     second_rows = lax.optimization_barrier((*second_rows, part_0))[:4]
     second_rows = turned_sum(z_spots, second_rows)
     w1 = weight_halves(after(turn, [second_rows[0]]), weight_first, "first_weights")
-    own = inner(halves, w1, planes, flops, "first_inner")
-    first_rows = lax.optimization_barrier((*first_rows, own))[:4]
-    first_rows = turned_sum(z_spots, first_rows)
     before, behind = call(
         lambda g_hi, g_lo, *refs: outer_part(g_hi, g_lo, refs[:4], *refs[4:]), [shape(1, channels, area)] * 2, [],
-        [after(halves[0], [first_rows[0]]), halves[1], *w1[:2], *w1[4:]], 0, flops // 9, "first_outer")
+        [*halves, *w1[:2], *w1[4:]], 0, flops // 9, "first_outer")
+    first_rows = lax.optimization_barrier((*first_rows, before))[:4]
+    first_rows = turned_sum(z_spots, first_rows)
+    own = inner([after(halves[0], [first_rows[0]]), halves[1]], w1, planes, flops, "first_inner")
     second_weights = owner_sum(second_rows, scale)
     first_weights = owner_sum(first_rows, scale)
     before, behind = edges(before, behind)

time: 138 us -> 133 us (0.964)
  Pallas kernels: 41.8 us -> 37.3 us
    pallas_call x17, Pallas kernels: 41.8 us -> 37.3 us  [call(): pl.pallas_call(whole if fetched else kernel, out_shape=out_shape, in_spec...]
    unnamed x13 -> x11, local copies, waits for them, and re-layouts: 3.03 us -> 2.1 us
  transfers between devices with their start and end apart: 34 -> 34, of which waited for: 12 -> 12; matrix products, arithmetic and copies ran while one was open for 3% -> 4% of each run, Pallas kernels for 28% -> 26%
where the time goes in v3:
time: 133 us; the launch traced here: 132 us
  starting transfers between devices  49.9 us (38%)
  waiting for transfers between devices  38.1 us (29%)
  Pallas kernels  37.3 us (28%)
  local copies, waits for them, and re-layouts  3.66 us (3%)
  other arithmetic  2.22 us (2%)
    ppermute x34, starting transfers between devices, send(): return lax.ppermute(value, axis, moves)  49.9 us
    ppermute x34, waiting for transfers between devices, send(): return lax.ppermute(value, axis, moves)  38.1 us
    pallas_call x17, Pallas kernels, call(): pl.pallas_call(whole if fetched else kernel, out_shape=out_shape, in_spec...  37.3 us
  transfers between devices with their start and end apart: 34, of which 12 were waited for; matrix products, arithmetic and copies ran while one was open for 4% of the time, Pallas kernels for 26%

profile of v3, /device:TPU:8, one launch (start us, length us, event | category | flops | bytes accessed | tf_op | source)
XLA Modules:
  0.0 132.2 jit_solution(2858163080098615595)
XLA Ops:
  1.8 7.3 %collective-permute-start.3 = (f32[6,32,256]{2,1,0:T(8,128)S(1)}, f32[6,32,256]{2,1,0:T(8,128)S(1)}, u32[]{:S(2)}, u32[]{:S(2)}) collective-permute-start(f32[6,32,256]{2,1,0:T(8,128)S(1)} %fusion.5.refs_1_), channel_id=1, source_target_pairs={{0,8},{1,9},{2,10},{3,11},{4,12},{5,13},{6,14},{7,15},{8,0},{9,1},... | collective-permute-start | bytes 589832 | tf_op jit(solution)/shard_map/ppermute | solution.py:326
  9.0 2.8 %collective-permute-start.1 = (f32[6,32,256]{2,1,0:T(8,128)S(1)}, f32[6,32,256]{2,1,0:T(8,128)S(1)}, u32[]{:S(2)}, u32[]{:S(2)}) collective-permute-start(f32[6,32,256]{2,1,0:T(8,128)S(1)} %fusion.5.refs_1_), channel_id=1, source_target_pairs={{0,6},{1,7},{2,0},{3,1},{4,2},{5,3},{6,4},{7,5},{8,14},{9,15},{10,... | collective-permute-start | bytes 589832 | tf_op jit(solution)/shard_map/ppermute | solution.py:326
  11.8 2.3 %collective-permute-start.2 = (f32[6,32,256]{2,1,0:T(8,128)S(1)}, f32[6,32,256]{2,1,0:T(8,128)S(1)}, u32[]{:S(2)}, u32[]{:S(2)}) collective-permute-start(f32[6,32,256]{2,1,0:T(8,128)S(1)} %fusion.5.refs_1_), channel_id=1, source_target_pairs={{0,4},{1,5},{2,6},{3,7},{4,0},{5,1},{6,2},{7,3},{8,12},{9,13},{10,... | collective-permute-start | bytes 589832 | tf_op jit(solution)/shard_map/ppermute | solution.py:326
  14.1 9.0 %collective-permute-done.1.refs_3_ = f32[6,32,256]{2,1,0:T(8,128)S(1)} collective-permute-done((f32[6,32,256]{2,1,0:T(8,128)S(1)}, f32[6,32,256]{2,1,0:T(8,128)S(1)}, u32[]{:S(2)}, u32[]{:S(2)}) %collective-permute-start.1) | collective-permute-done | bytes 196640 | tf_op jit(solution)/shard_map/ppermute | solution.py:326
  23.1 2.9 %collective-permute-done.refs_2_ = f32[6,32,256]{2,1,0:T(8,128)S(1)} collective-permute-done((f32[6,32,256]{2,1,0:T(8,128)S(1)}, f32[6,32,256]{2,1,0:T(8,128)S(1)}, u32[]{:S(2)}, u32[]{:S(2)}) %collective-permute-start) | collective-permute-done | bytes 196640 | tf_op jit(solution)/shard_map/ppermute | solution.py:326
  29.6 5.6 %collective-permute-done.4.refs_6_ = f32[6,32,256]{2,1,0:T(8,128)S(1)} collective-permute-done((f32[6,32,256]{2,1,0:T(8,128)S(1)}, f32[6,32,256]{2,1,0:T(8,128)S(1)}, u32[]{:S(2)}, u32[]{:S(2)}) %collective-permute-start.4) | collective-permute-done | bytes 196640 | tf_op jit(solution)/shard_map/ppermute | solution.py:326
  39.9 2.6 %second_outer.1 = (bf16[16,32,1536]{2,1,0:T(8,128)(2,1)S(1)}, bf16[16,32,1536]{2,1,0:T(8,128)(2,1)S(1)}, f32[3,32,256]{2,1,0:T(8,128)S(1)}, f32[3,32,256]{2,1,0:T(8,128)S(1)}) custom-call(s32[16]{0:T(128)S(1)} %fusion.6.refs_0_, f32[6,32,256]{2,1,0:T(8,128)S(1)} %fusion.5.refs_1_, f32[6,32,256]{2,1,0:T(8,128)S(1)} %collective-permute-done.refs_2_, ...), custom_call_target="tpu_custom_call" | custom-call | flops 452984832 | bytes 7798848 | tf_op jit(solution)/shard_map/second_outer/pallas_call | solution.py:41
  42.5 2.9 %collective-permute-start.9 = (f32[3,32,256]{2,1,0:T(8,128)S(1)}, f32[3,32,256]{2,1,0:T(8,128)S(1)}, u32[]{:S(2)}, u32[]{:S(2)}) collective-permute-start(f32[3,32,256]{2,1,0:T(8,128)S(1)} %get-tuple-element.76), channel_id=1, source_target_pairs={{0,16},{16,32},{32,48},{48,64},{64,80},{80,96},{96,112},{112,128},... | collective-permute-start | bytes 294920 | tf_op jit(solution)/shard_map/ppermute | solution.py:326
  45.4 5.6 %collective-permute-start.10 = (f32[3,32,256]{2,1,0:T(8,128)S(1)}, f32[3,32,256]{2,1,0:T(8,128)S(1)}, u32[]{:S(2)}, u32[]{:S(2)}) collective-permute-start(f32[3,32,256]{2,1,0:T(8,128)S(1)} %get-tuple-element.77), channel_id=1, source_target_pairs={{16,0},{32,16},{48,32},{64,48},{80,64},{96,80},{112,96},{128,112},... | collective-permute-start | bytes 294920 | tf_op jit(solution)/shard_map/ppermute | solution.py:326
  51.1 5.5 %second_inner.1.own = f32[6,32,256]{2,1,0:T(8,128)S(1)} custom-call(bf16[16,32,1536]{2,1,0:T(8,128)(2,1)S(1)} %get-tuple-element.72.g_hi, bf16[16,32,1536]{2,1,0:T(8,128)(2,1)S(1)} %get-tuple-element.73.g_lo, bf16[288,512]{1,0:T(8,128)(2,1)S(1)} %get-tuple-element.68.refs_12_.refs_0_, bf16[288,512]{1,0:T(8,128)(2,1)S(1)} %get-tuple-element.69.refs_13_.refs_1_, ...), custom_call_target="tpu_custom_call" | custom-call | flops 4076863488 | bytes 5111808 | tf_op jit(solution)/shard_map/second_inner/pallas_call | solution.py:41
  60.5 5.4 %second_filter.1 = (f32[864,128]{1,0:T(8,128)S(1)}, f32[864,128]{1,0:T(8,128)S(1)}, f32[864,128]{1,0:T(8,128)S(1)}, f32[864,128]{1,0:T(8,128)S(1)}) custom-call(bf16[16,32,1536]{2,1,0:T(8,128)(2,1)S(1)} %get-tuple-element.72.g_hi, bf16[16,32,1536]{2,1,0:T(8,128)(2,1)S(1)} %get-tuple-element.73.g_lo, bf16[288,2048]{1,0:T(8,128)(2,1)S(1)} %get-tuple-element.79.i_hi, ...), custom_call_target="tpu_custom_call" | custom-call | flops 4076863488 | bytes 7274496 | tf_op jit(solution)/shard_map/second_filter/pallas_call | solution.py:41
  66.8 2.1 %collective-permute-done.11.refs_2_ = f32[6,32,256]{2,1,0:T(8,128)S(1)} collective-permute-done((f32[6,32,256]{2,1,0:T(8,128)S(1)}, f32[6,32,256]{2,1,0:T(8,128)S(1)}, u32[]{:S(2)}, u32[]{:S(2)}) %collective-permute-start.11) | collective-permute-done | bytes 196640 | tf_op jit(solution)/shard_map/ppermute | solution.py:326
  68.9 1.7 %collective-permute-start.19 = (f32[864,128]{1,0:T(8,128)S(1)}, f32[864,128]{1,0:T(8,128)S(1)}, u32[]{:S(2)}, u32[]{:S(2)}) collective-permute-start(f32[864,128]{1,0:T(8,128)S(1)} %get-tuple-element.86), channel_id=1, source_target_pairs={{0,64},{16,80},{32,96},{48,112},{64,128},{80,144},{96,160},{112,17... | collective-permute-start | bytes 1327112 | tf_op jit(solution)/shard_map/ppermute | solution.py:326
  75.1 5.4 %collective-permute-done.17.refs_8_ = f32[6,32,256]{2,1,0:T(8,128)S(1)} collective-permute-done((f32[6,32,256]{2,1,0:T(8,128)S(1)}, f32[6,32,256]{2,1,0:T(8,128)S(1)}, u32[]{:S(2)}, u32[]{:S(2)}) %collective-permute-start.17) | collective-permute-done | bytes 196640 | tf_op jit(solution)/shard_map/ppermute | solution.py:326
  81.0 2.1 %collective-permute-done.15.refs_6_ = f32[6,32,256]{2,1,0:T(8,128)S(1)} collective-permute-done((f32[6,32,256]{2,1,0:T(8,128)S(1)}, f32[6,32,256]{2,1,0:T(8,128)S(1)}, u32[]{:S(2)}, u32[]{:S(2)}) %collective-permute-start.15) | collective-permute-done | bytes 196640 | tf_op jit(solution)/shard_map/ppermute | solution.py:326
  83.2 2.4 %collective-permute-start.25 = (f32[864,128]{1,0:T(8,128)S(1)}, f32[864,128]{1,0:T(8,128)S(1)}, u32[]{:S(2)}, u32[]{:S(2)}) collective-permute-start(f32[864,128]{1,0:T(8,128)S(1)} %get-tuple-element.100), channel_id=1, source_target_pairs={{0,128},{16,144},{32,160},{48,176},{64,192},{80,208},{96,224},{112... | collective-permute-start | bytes 1327112 | tf_op jit(solution)/shard_map/ppermute | solution.py:326
  85.6 4.8 %first_filter.1 = (bf16[16,32,1536]{2,1,0:T(8,128)(2,1)S(1)}, bf16[16,32,1536]{2,1,0:T(8,128)(2,1)S(1)}, f32[864,128]{1,0:T(8,128)S(1)}, f32[864,128]{1,0:T(8,128)S(1)}) custom-call(s32[16]{0:T(128)S(1)} %fusion.6.refs_0_, f32[6,32,256]{2,1,0:T(8,128)S(1)} %first_grad.1.refs_1_, f32[6,32,256]{2,1,0:T(8,128)S(1)} %collective-permute-done.11.refs_2_, ...), custom_call_target="tpu_custom_call" | custom-call | flops 2038431744 | bytes 9535552 | tf_op jit(solution)/shard_map/first_filter/pallas_call | solution.py:41
  91.9 2.3 %collective-permute-start.23 = (f32[864,128]{1,0:T(8,128)S(1)}, f32[864,128]{1,0:T(8,128)S(1)}, u32[]{:S(2)}, u32[]{:S(2)}) collective-permute-start(f32[864,128]{1,0:T(8,128)S(1)} %get-tuple-element.96), channel_id=1, source_target_pairs={{0,128},{16,144},{32,160},{48,176},{64,192},{80,208},{96,224},{112... | collective-permute-start | bytes 1327112 | tf_op jit(solution)/shard_map/ppermute | solution.py:326
  94.2 3.4 %first_filter_rest.1 = (f32[864,128]{1,0:T(8,128)S(1)}, f32[864,128]{1,0:T(8,128)S(1)}) custom-call(bf16[16,32,1536]{2,1,0:T(8,128)(2,1)S(1)} %get-tuple-element.117.g_hi, bf16[16,32,1536]{2,1,0:T(8,128)(2,1)S(1)} %get-tuple-element.93.g_lo, bf16[288,2048]{1,0:T(8,128)(2,1)S(1)} %get-tuple-element.89.refs_11_.i_hi, ...), custom_call_target="tpu_custom_call" | custom-call | flops 2038431744 | bytes 6389760 | tf_op jit(solution)/shard_map/first_filter_rest/pallas_call | solution.py:41
  99.7 7.8 %collective-permute-done.31.refs_1_ = f32[32,864]{1,0:T(8,128)S(1)} collective-permute-done((f32[32,864]{1,0:T(8,128)S(1)}, f32[32,864]{1,0:T(8,128)S(1)}, u32[]{:S(2)}, u32[]{:S(2)}) %collective-permute-start.31) | collective-permute-done | bytes 110624 | tf_op jit(solution)/shard_map/ppermute | solution.py:326
  110.8 2.5 %collective-permute-start.26 = (f32[1,32,256]{2,1,0:T(8,128)S(1)}, f32[1,32,256]{2,1,0:T(8,128)S(1)}, u32[]{:S(2)}, u32[]{:S(2)}) collective-permute-start(f32[1,32,256]{2,1,0:T(8,128)S(1)} %get-tuple-element.120), channel_id=1, source_target_pairs={{0,16},{16,32},{32,48},{48,64},{64,80},{80,96},{96,112},{112,128},... | collective-permute-start | bytes 98312 | tf_op jit(solution)/shard_map/ppermute | solution.py:326
  113.4 6.0 %collective-permute-start.27 = (f32[1,32,256]{2,1,0:T(8,128)S(1)}, f32[1,32,256]{2,1,0:T(8,128)S(1)}, u32[]{:S(2)}, u32[]{:S(2)}) collective-permute-start(f32[1,32,256]{2,1,0:T(8,128)S(1)} %get-tuple-element.111), channel_id=1, source_target_pairs={{16,0},{32,16},{48,32},{64,48},{80,64},{96,80},{112,96},{128,112},... | collective-permute-start | bytes 98312 | tf_op jit(solution)/shard_map/ppermute | solution.py:326
  121.3 3.7 %collective-permute-start.30 = (f32[32,864]{1,0:T(8,128)S(1)}, f32[32,864]{1,0:T(8,128)S(1)}, u32[]{:S(2)}, u32[]{:S(2)}) collective-permute-start(f32[32,864]{1,0:T(8,128)S(1)} %get-tuple-element.123), channel_id=1, source_target_pairs={{0,48},{16,0},{32,16},{48,32},{64,112},{80,64},{96,80},{112,96},{1... | collective-permute-start | bytes 331784 | tf_op jit(solution)/shard_map/ppermute | solution.py:326
  125.1 5.5 %first_inner.1.own = f32[6,32,256]{2,1,0:T(8,128)S(1)} custom-call(bf16[16,32,1536]{2,1,0:T(8,128)(2,1)S(1)} %get-tuple-element.117.g_hi, bf16[16,32,1536]{2,1,0:T(8,128)(2,1)S(1)} %get-tuple-element.93.g_lo, bf16[288,512]{1,0:T(8,128)(2,1)S(1)} %get-tuple-element.107.refs_0_, bf16[288,512]{1,0:T(8,128)(2,1)S(1)} %get-tuple-element.108.refs_1_, ...), custom_call_target="tpu_custom_call" | custom-call | flops 4076863488 | bytes 5111808 | tf_op jit(solution)/shard_map/first_inner/pallas_call | solution.py:41
  (83 shorter events, 30.0 us)
Async XLA Ops:
  1.8 12.3 %collective-permute-start.3 = (f32[6,32,256]{2,1,0:T(8,128)S(1)}, f32[6,32,256]{2,1,0:T(8,128)S(1)}, u32[]{:S(2)}, u32[]{:S(2)}) collective-permute-start(f32[6,32,256]{2,1,0:T(8,128)S(1)} %fusion.5.refs_1_), channel_id=1, source_target_pairs={{0,8},{1,9},{2,10},{3,11},{4,12},{5,13},{6,14},{7,15},{8,0},{9,1},... | collective-permute-start | bytes 589832 | tf_op jit(solution)/shard_map/ppermute | solution.py:326
  9.0 14.0 %collective-permute-start.1 = (f32[6,32,256]{2,1,0:T(8,128)S(1)}, f32[6,32,256]{2,1,0:T(8,128)S(1)}, u32[]{:S(2)}, u32[]{:S(2)}) collective-permute-start(f32[6,32,256]{2,1,0:T(8,128)S(1)} %fusion.5.refs_1_), channel_id=1, source_target_pairs={{0,6},{1,7},{2,0},{3,1},{4,2},{5,3},{6,4},{7,5},{8,14},{9,15},{10,... | collective-permute-start | bytes 589832 | tf_op jit(solution)/shard_map/ppermute | solution.py:326
  11.8 14.1 %collective-permute-start = (f32[6,32,256]{2,1,0:T(8,128)S(1)}, f32[6,32,256]{2,1,0:T(8,128)S(1)}, u32[]{:S(2)}, u32[]{:S(2)}) collective-permute-start(f32[6,32,256]{2,1,0:T(8,128)S(1)} %fusion.5.refs_1_), channel_id=1, source_target_pairs={{0,2},{1,3},{2,4},{3,5},{4,6},{5,7},{6,0},{7,1},{8,10},{9,11},{10,... | collective-permute-start | bytes 589832 | tf_op jit(solution)/shard_map/ppermute | solution.py:326
  11.8 16.2 %collective-permute-start.2 = (f32[6,32,256]{2,1,0:T(8,128)S(1)}, f32[6,32,256]{2,1,0:T(8,128)S(1)}, u32[]{:S(2)}, u32[]{:S(2)}) collective-permute-start(f32[6,32,256]{2,1,0:T(8,128)S(1)} %fusion.5.refs_1_), channel_id=1, source_target_pairs={{0,4},{1,5},{2,6},{3,7},{4,0},{5,1},{6,2},{7,3},{8,12},{9,13},{10,... | collective-permute-start | bytes 589832 | tf_op jit(solution)/shard_map/ppermute | solution.py:326
  25.9 10.7 %collective-permute-start.6 = (f32[6,32,256]{2,1,0:T(8,128)S(1)}, f32[6,32,256]{2,1,0:T(8,128)S(1)}, u32[]{:S(2)}, u32[]{:S(2)}) collective-permute-start(f32[6,32,256]{2,1,0:T(8,128)S(1)} %collective-permute-done.3.refs_5_), channel_id=1, source_target_pairs={{0,4},{1,5},{2,6},{3,7},{4,0},{5,1},{6,2},{7,3},{8,12},{9,13},{10,... | collective-permute-start | bytes 589832 | tf_op jit(solution)/shard_map/ppermute | solution.py:326
  25.9 10.0 %collective-permute-start.5 = (f32[6,32,256]{2,1,0:T(8,128)S(1)}, f32[6,32,256]{2,1,0:T(8,128)S(1)}, u32[]{:S(2)}, u32[]{:S(2)}) collective-permute-start(f32[6,32,256]{2,1,0:T(8,128)S(1)} %collective-permute-done.3.refs_5_), channel_id=1, source_target_pairs={{0,6},{1,7},{2,0},{3,1},{4,2},{5,3},{6,4},{7,5},{8,14},{9,15},{10,... | collective-permute-start | bytes 589832 | tf_op jit(solution)/shard_map/ppermute | solution.py:326
  28.9 10.5 %collective-permute-start.7 = (f32[24,32,256]{2,1,0:T(8,128)}, f32[24,32,256]{2,1,0:T(8,128)}, u32[]{:S(2)}, u32[]{:S(2)}) collective-permute-start(f32[24,32,256]{2,1,0:T(8,128)} %pad_maximum_fusion), channel_id=1, source_target_pairs={{0,1},{1,0},{2,3},{3,2},{4,5},{5,4},{6,7},{7,6},{8,9},{9,8},{10,11... | collective-permute-start | bytes 2359304 | tf_op jit(solution)/shard_map/ppermute | solution.py:326
  42.5 14.0 %collective-permute-start.9 = (f32[3,32,256]{2,1,0:T(8,128)S(1)}, f32[3,32,256]{2,1,0:T(8,128)S(1)}, u32[]{:S(2)}, u32[]{:S(2)}) collective-permute-start(f32[3,32,256]{2,1,0:T(8,128)S(1)} %get-tuple-element.76), channel_id=1, source_target_pairs={{0,16},{16,32},{32,48},{48,64},{64,80},{80,96},{96,112},{112,128},... | collective-permute-start | bytes 294920 | tf_op jit(solution)/shard_map/ppermute | solution.py:326
  45.4 11.1 %collective-permute-start.10 = (f32[3,32,256]{2,1,0:T(8,128)S(1)}, f32[3,32,256]{2,1,0:T(8,128)S(1)}, u32[]{:S(2)}, u32[]{:S(2)}) collective-permute-start(f32[3,32,256]{2,1,0:T(8,128)S(1)} %get-tuple-element.77), channel_id=1, source_target_pairs={{16,0},{32,16},{48,32},{64,48},{80,64},{96,80},{112,96},{128,112},... | collective-permute-start | bytes 294920 | tf_op jit(solution)/shard_map/ppermute | solution.py:326
  56.6 14.5 %collective-permute-start.14 = (f32[6,32,256]{2,1,0:T(8,128)S(1)}, f32[6,32,256]{2,1,0:T(8,128)S(1)}, u32[]{:S(2)}, u32[]{:S(2)}) collective-permute-start(f32[6,32,256]{2,1,0:T(8,128)S(1)} %first_grad.1.refs_1_), channel_id=1, source_target_pairs={{0,8},{1,9},{2,10},{3,11},{4,12},{5,13},{6,14},{7,15},{8,0},{9,1},... | collective-permute-start | bytes 589832 | tf_op jit(solution)/shard_map/ppermute | solution.py:326
  58.1 10.8 %collective-permute-start.11 = (f32[6,32,256]{2,1,0:T(8,128)S(1)}, f32[6,32,256]{2,1,0:T(8,128)S(1)}, u32[]{:S(2)}, u32[]{:S(2)}) collective-permute-start(f32[6,32,256]{2,1,0:T(8,128)S(1)} %first_grad.1.refs_1_), channel_id=1, source_target_pairs={{0,2},{1,3},{2,4},{3,5},{4,6},{5,7},{6,0},{7,1},{8,10},{9,11},{10,... | collective-permute-start | bytes 589832 | tf_op jit(solution)/shard_map/ppermute | solution.py:326
  68.9 14.2 %collective-permute-start.19 = (f32[864,128]{1,0:T(8,128)S(1)}, f32[864,128]{1,0:T(8,128)S(1)}, u32[]{:S(2)}, u32[]{:S(2)}) collective-permute-start(f32[864,128]{1,0:T(8,128)S(1)} %get-tuple-element.86), channel_id=1, source_target_pairs={{0,64},{16,80},{32,96},{48,112},{64,128},{80,144},{96,160},{112,17... | collective-permute-start | bytes 1327112 | tf_op jit(solution)/shard_map/ppermute | solution.py:326
  70.6 12.5 %collective-permute-start.20 = (f32[864,128]{1,0:T(8,128)S(1)}, f32[864,128]{1,0:T(8,128)S(1)}, u32[]{:S(2)}, u32[]{:S(2)}) collective-permute-start(f32[864,128]{1,0:T(8,128)S(1)} %get-tuple-element.87), channel_id=1, source_target_pairs={{0,192},{16,208},{32,224},{48,240},{64,0},{80,16},{96,32},{112,48}... | collective-permute-start | bytes 1327112 | tf_op jit(solution)/shard_map/ppermute | solution.py:326
  72.5 10.5 %collective-permute-start.15 = (f32[6,32,256]{2,1,0:T(8,128)S(1)}, f32[6,32,256]{2,1,0:T(8,128)S(1)}, u32[]{:S(2)}, u32[]{:S(2)}) collective-permute-start(f32[6,32,256]{2,1,0:T(8,128)S(1)} %collective-permute-done.14.refs_5_), channel_id=1, source_target_pairs={{0,2},{1,3},{2,4},{3,5},{4,6},{5,7},{6,0},{7,1},{8,10},{9,11},{10,... | collective-permute-start | bytes 589832 | tf_op jit(solution)/shard_map/ppermute | solution.py:326
  83.2 15.5 %collective-permute-start.25 = (f32[864,128]{1,0:T(8,128)S(1)}, f32[864,128]{1,0:T(8,128)S(1)}, u32[]{:S(2)}, u32[]{:S(2)}) collective-permute-start(f32[864,128]{1,0:T(8,128)S(1)} %get-tuple-element.100), channel_id=1, source_target_pairs={{0,128},{16,144},{32,160},{48,176},{64,192},{80,208},{96,224},{112... | collective-permute-start | bytes 1327112 | tf_op jit(solution)/shard_map/ppermute | solution.py:326
  90.4 30.0 %collective-permute-start.22 = (f32[864,128]{1,0:T(8,128)S(1)}, f32[864,128]{1,0:T(8,128)S(1)}, u32[]{:S(2)}, u32[]{:S(2)}) collective-permute-start(f32[864,128]{1,0:T(8,128)S(1)} %get-tuple-element.95), channel_id=1, source_target_pairs={{0,64},{16,80},{32,96},{48,112},{64,128},{80,144},{96,160},{112,17... | collective-permute-start | bytes 1327112 | tf_op jit(solution)/shard_map/ppermute | solution.py:326
  91.9 28.4 %collective-permute-start.23 = (f32[864,128]{1,0:T(8,128)S(1)}, f32[864,128]{1,0:T(8,128)S(1)}, u32[]{:S(2)}, u32[]{:S(2)}) collective-permute-start(f32[864,128]{1,0:T(8,128)S(1)} %get-tuple-element.96), channel_id=1, source_target_pairs={{0,128},{16,144},{32,160},{48,176},{64,192},{80,208},{96,224},{112... | collective-permute-start | bytes 1327112 | tf_op jit(solution)/shard_map/ppermute | solution.py:326
  97.6 22.8 %collective-permute-start.24 = (f32[864,128]{1,0:T(8,128)S(1)}, f32[864,128]{1,0:T(8,128)S(1)}, u32[]{:S(2)}, u32[]{:S(2)}) collective-permute-start(f32[864,128]{1,0:T(8,128)S(1)} %get-tuple-element.97), channel_id=1, source_target_pairs={{0,192},{16,208},{32,224},{48,240},{64,0},{80,16},{96,32},{112,48}... | collective-permute-start | bytes 1327112 | tf_op jit(solution)/shard_map/ppermute | solution.py:326
  99.6 11.2 %collective-permute-start.32 = (f32[32,864]{1,0:T(8,128)S(1)}, f32[32,864]{1,0:T(8,128)S(1)}, u32[]{:S(2)}, u32[]{:S(2)}) collective-permute-start(f32[32,864]{1,0:T(8,128)S(1)} %get-tuple-element.125), channel_id=1, source_target_pairs={{0,32},{16,48},{32,0},{48,16},{64,96},{80,112},{96,64},{112,80},{1... | collective-permute-start | bytes 331784 | tf_op jit(solution)/shard_map/ppermute | solution.py:326
  110.8 19.7 %collective-permute-start.26 = (f32[1,32,256]{2,1,0:T(8,128)S(1)}, f32[1,32,256]{2,1,0:T(8,128)S(1)}, u32[]{:S(2)}, u32[]{:S(2)}) collective-permute-start(f32[1,32,256]{2,1,0:T(8,128)S(1)} %get-tuple-element.120), channel_id=1, source_target_pairs={{0,16},{16,32},{32,48},{48,64},{64,80},{80,96},{96,112},{112,128},... | collective-permute-start | bytes 98312 | tf_op jit(solution)/shard_map/ppermute | solution.py:326
  113.4 17.2 %collective-permute-start.27 = (f32[1,32,256]{2,1,0:T(8,128)S(1)}, f32[1,32,256]{2,1,0:T(8,128)S(1)}, u32[]{:S(2)}, u32[]{:S(2)}) collective-permute-start(f32[1,32,256]{2,1,0:T(8,128)S(1)} %get-tuple-element.111), channel_id=1, source_target_pairs={{16,0},{32,16},{48,32},{64,48},{80,64},{96,80},{112,96},{128,112},... | collective-permute-start | bytes 98312 | tf_op jit(solution)/shard_map/ppermute | solution.py:326
  121.2 10.1 %collective-permute-start.28 = (f32[32,864]{1,0:T(8,128)S(1)}, f32[32,864]{1,0:T(8,128)S(1)}, u32[]{:S(2)}, u32[]{:S(2)}) collective-permute-start(f32[32,864]{1,0:T(8,128)S(1)} %get-tuple-element.121), channel_id=1, source_target_pairs={{0,16},{16,32},{32,48},{48,0},{64,80},{80,96},{96,112},{112,64},{1... | collective-permute-start | bytes 331784 | tf_op jit(solution)/shard_map/ppermute | solution.py:326
  121.2 10.0 %collective-permute-start.29 = (f32[32,864]{1,0:T(8,128)S(1)}, f32[32,864]{1,0:T(8,128)S(1)}, u32[]{:S(2)}, u32[]{:S(2)}) collective-permute-start(f32[32,864]{1,0:T(8,128)S(1)} %get-tuple-element.122), channel_id=1, source_target_pairs={{0,32},{16,48},{32,0},{48,16},{64,96},{80,112},{96,64},{112,80},{1... | collective-permute-start | bytes 331784 | tf_op jit(solution)/shard_map/ppermute | solution.py:326
  121.3 9.9 %collective-permute-start.30 = (f32[32,864]{1,0:T(8,128)S(1)}, f32[32,864]{1,0:T(8,128)S(1)}, u32[]{:S(2)}, u32[]{:S(2)}) collective-permute-start(f32[32,864]{1,0:T(8,128)S(1)} %get-tuple-element.123), channel_id=1, source_target_pairs={{0,48},{16,0},{32,16},{48,32},{64,112},{80,64},{96,80},{112,96},{1... | collective-permute-start | bytes 331784 | tf_op jit(solution)/shard_map/ppermute | solution.py:326
  (14 other events, 161.3 us)

commit v4 on v3

--- a/solution.py
+++ b/solution.py
@@ -22,38 +22,20 @@
     return sigma * (1.0 + values * (1.0 - sigma))
 
 
-def call(kernel, out_shape, scratch, args, n_smem=0, flops=0, name=None, fetched=(), vmem=16):
+def call(kernel, out_shape, scratch, args, n_smem=0, flops=0, name=None):
     many = isinstance(out_shape, list)
-    moved = sum(a.size * a.dtype.itemsize for a in (*args, *fetched))
+    moved = sum(a.size * a.dtype.itemsize for a in args)
     moved += sum(o.size * o.dtype.itemsize for o in (out_shape if many else [out_shape]))
-    n, m = len(args), len(fetched)
-
-    def whole(*refs):
-        sources, rest = refs[n:n + m], refs[n + m:]
-        rest, targets, sems = rest[:len(rest) - m - 1], rest[len(rest) - m - 1:-1], rest[-1]
-        copies = [(pltpu.make_async_copy(s, t, sems.at[k]), t) for k, (s, t) in enumerate(zip(sources, targets))]
-        for copy, _ in copies:
-            copy.start()
-        kernel(copies, *refs[:n], *rest)
-
-    if fetched:
-        scratch = [*scratch, *(pltpu.VMEM(f.shape, f.dtype) for f in fetched), pltpu.SemaphoreType.DMA((m,))]
     return pl.pallas_call(
-        whole if fetched else kernel,
+        kernel,
         out_shape=out_shape,
-        in_specs=[SM] * n_smem + [VM] * (n - n_smem) + [pl.BlockSpec(memory_space=pltpu.HBM)] * m,
+        in_specs=[SM] * n_smem + [VM] * (len(args) - n_smem),
         out_specs=[VM] * len(out_shape) if many else VM,
         scratch_shapes=scratch,
-        compiler_params=pltpu.CompilerParams(vmem_limit_bytes=vmem << 20),
+        compiler_params=pltpu.CompilerParams(vmem_limit_bytes=16 << 20),
         cost_estimate=pl.CostEstimate(flops=flops, bytes_accessed=moved, transcendentals=0),
         name=name,
-    )(*args, *fetched)
-
-
-def arrived(copies):
-    for copy, _ in copies:
-        copy.wait()
-    return [target for _, target in copies]
+    )(*args)
 
 
 def shape(*dims, dtype=F32):
@@ -142,17 +124,18 @@
                 [own, low, high], name=name)
 
 
-def gather_blocks(spots, pieces, g_hi, g_lo):
-    planes = pieces[0].shape[0]
+def lanes_of(p):
+    return pl.ds(p * AREA if isinstance(p, int) else pl.multiple_of(p * AREA, AREA), AREA)
+
+
+def split_plane(spots, pieces, p, planes, g_hi, g_lo):
     k = 0
     for piece in pieces:
         for first in range(0, piece.shape[0], planes):
-            spot = spots[k]
+            hi, lo = split(piece[first + p])
+            g_hi[spots[k], :, lanes_of(p)] = hi
+            g_lo[spots[k], :, lanes_of(p)] = lo
             k += 1
-            for p in range(planes):
-                hi, lo = split(piece[first + p])
-                g_hi[spot, :, p * AREA:(p + 1) * AREA] = hi
-                g_lo[spot, :, p * AREA:(p + 1) * AREA] = lo
 
 
 def spread(sums):
@@ -174,16 +157,29 @@
 
 
 def plane_of(g_ref, p):
-    lanes = pl.ds(p * AREA if isinstance(p, int) else pl.multiple_of(p * AREA, AREA), AREA)
-    return g_ref[:, :, lanes].reshape(g_ref.shape[0] * g_ref.shape[1], AREA)
-
-
-def outer_part(g_hi, g_lo, w_refs, before_ref, behind_ref, rims=None):
+    return g_ref[:, :, lanes_of(p)].reshape(g_ref.shape[0] * g_ref.shape[1], AREA)
+
+
+def outer_part(first, last, w_refs, before_ref, behind_ref, rims=None):
+    for n, (planes, w_hi, w_lo, out) in enumerate(((first, *w_refs[:2], before_ref), (last, *w_refs[2:], behind_ref))):
+        out[0] = spread(three_products(w_hi[...], w_lo[...], *planes))
+        if rims is not None:
+            out[1:] = rims[n]
+
+
+def second_outer_kernel(n, spots, *refs):
+    pieces, rims, weights, (g_hi, g_lo, before_ref, behind_ref) = refs[:n], refs[n], refs[n + 1:n + 5], refs[n + 5:]
     last = g_hi.shape[2] // AREA - 1
-    for p, w_hi, w_lo, out in ((0, *w_refs[:2], before_ref), (last, *w_refs[2:], behind_ref)):
-        out[0] = spread(three_products(w_hi[...], w_lo[...], plane_of(g_hi, p), plane_of(g_lo, p)))
-        if rims is not None:
-            out[1:] = rims[min(p, 1)]
+    split_plane(spots, pieces, 0, last + 1, g_hi, g_lo)
+    split_plane(spots, pieces, last, last + 1, g_hi, g_lo)
+    outer_part(*([plane_of(g, p) for g in (g_hi, g_lo)] for p in (0, last)), weights, before_ref, behind_ref, rims)
+    for p in range(1, last):
+        split_plane(spots, pieces, p, last + 1, g_hi, g_lo)
+
+
+def first_outer_kernel(g_hi, g_lo, *refs):
+    last = g_hi.shape[2] // AREA - 1
+    outer_part(*([plane_of(g, p) for g in (g_hi, g_lo)] for p in (0, last)), refs[:4], *refs[4:])
 
 
 def inner_part(g_hi, g_lo, *refs):
@@ -210,45 +206,54 @@
     own_ref[planes - 1] = spread(sums.at[(planes - 1) % 2])
 
 
-def filter_part(g_hi, g_lo, i_hi, i_lo, outs, quarters):
-    planes = g_hi.shape[2] // AREA
+def filter_add(p, hi, lo, i_hi, i_lo, outs):
     width = outs[0].shape[1]
-    blocks = width // g_hi.shape[1]
+    left_hi, left_lo = (jnp.concatenate([i[:, lanes_of(p + a)] for a in range(3)], 0) for i in (i_hi, i_lo))
+    dims = (((1,), (1,)), ((), ()))
+    part = lax.dot_general(left_hi, hi, dims, preferred_element_type=F32)
+    part += lax.dot_general(left_hi, lo, dims, preferred_element_type=F32)
+    part += lax.dot_general(left_lo, hi, dims, preferred_element_type=F32)
+    for n, out in enumerate(outs):
+        out[...] += part[:, n * width:(n + 1) * width]
+
+
+def quarters_of(g_ref, p, quarters):
+    blocks = g_ref.shape[0] // 4
+    width = blocks * g_ref.shape[1]
+    return jnp.concatenate([g_ref[d * blocks:(d + 1) * blocks, :, lanes_of(p)].reshape(width, AREA) for d in quarters], 0)
+
+
+def filter_kernel(quarters, g_hi, g_lo, i_hi, i_lo, *outs):
     for out in outs:
         out[...] = jnp.zeros_like(out)
 
-    def one_plane(p, _):
-        lanes = pl.ds(pl.multiple_of(p * AREA, AREA), AREA)
-        hi, lo = (jnp.concatenate(
-            [g[d * blocks:(d + 1) * blocks, :, lanes].reshape(width, AREA) for d in quarters], 0) for g in (g_hi, g_lo))
-        windows = [pl.ds(pl.multiple_of((p + a) * AREA, AREA), AREA) for a in range(3)]
-        left_hi = jnp.concatenate([i_hi[:, w] for w in windows], 0)
-        left_lo = jnp.concatenate([i_lo[:, w] for w in windows], 0)
-        dims = (((1,), (1,)), ((), ()))
-        part = lax.dot_general(left_hi, hi, dims, preferred_element_type=F32)
-        part += lax.dot_general(left_hi, lo, dims, preferred_element_type=F32)
-        part += lax.dot_general(left_lo, hi, dims, preferred_element_type=F32)
-        for n, out in enumerate(outs):
-            out[...] += part[:, n * width:(n + 1) * width]
-        return 0
-
-    lax.fori_loop(0, planes, one_plane, 0)
-
-
-def first_use(body, spots, pieces, others, outs, flops, name, fetched, vmem=16):
+    for p in range(g_hi.shape[2] // AREA):
+        filter_add(p, quarters_of(g_hi, p, quarters), quarters_of(g_lo, p, quarters), i_hi, i_lo, outs)
+
+
+def filter_quarters(quarters, halves, inputs, flops, name):
+    rows, total = 3 * inputs[0].shape[0], halves[0].shape[0] * halves[0].shape[1]
+    return call(lambda *refs: filter_kernel(quarters, *refs), [shape(rows, total // 4)] * len(quarters), [],
+                [*halves, *inputs], 0, flops, name)
+
+
+def first_filter_kernel(n, quarters, spots, *refs):
+    pieces, inputs, (g_hi, g_lo), outs = refs[:n], refs[n:n + 2], refs[n + 2:n + 4], refs[n + 4:n + 4 + len(quarters)]
+    planes = g_hi.shape[2] // AREA
+    for out in outs:
+        out[...] = jnp.zeros_like(out)
+    split_plane(spots, pieces, 0, planes, g_hi, g_lo)
+    for p in range(planes):
+        filter_add(p, quarters_of(g_hi, p, quarters), quarters_of(g_lo, p, quarters), *inputs, outs)
+        if p + 1 < planes:
+            split_plane(spots, pieces, p + 1, planes, g_hi, g_lo)
+
+
+def first_use(kernel, spots, pieces, others, outs, flops, name):
     planes, channels, area = pieces[0].shape
-    n, m = len(pieces), len(pieces) + len(others)
     shards = sum(piece.shape[0] for piece in pieces) // planes
     halves = [shape(shards, channels, planes * area, dtype=BF16)] * 2
-
-    def kernel(*refs):
-        copies = refs[0] if fetched else []
-        spots, *refs = refs[1:] if fetched else refs
-        g_hi, g_lo = refs[m:m + 2]
-        gather_blocks(spots, refs[:n], g_hi, g_lo)
-        body(g_hi, g_lo, copies, *refs[n:m], *refs[m + 2:])
-
-    g_hi, g_lo, *rest = call(kernel, halves + outs, [], [spots, *pieces, *others], 1, flops, name, fetched, vmem)
+    g_hi, g_lo, *rest = call(kernel, halves + outs, [], [spots, *pieces, *others], 1, flops, name)
     return (g_hi, g_lo), rest
 
 
@@ -358,8 +363,8 @@
     return send(part, along_y(d), "slab")
 
 
-def owner_sum(rows, scale):
-    return last_sum([rows[0]] + [send(rows[d], along_z(d), "slab") for d in (1, 2, 3)], scale)
+def to_owners(rows):
+    return [rows[0]] + [send(rows[d], along_z(d), "slab") for d in (1, 2, 3)]
 
 
 def per_device(saved_input, pre_first, pre_second, out_grad, weight_first, weight_second):
@@ -376,51 +381,50 @@
     spots = (((ids // 4 - slab // 4) % 4) * 4 + ids % 4).astype(jnp.int32)
     quarter = shape(rows, total // 4)
     second_grad = grad * slope_of(pre2)
+    saved_rims = jnp.stack([saved[0], saved[planes - 1]])
+
     def second_weights_of(_, near, wide):
-        return second_ready(after(turn, [wide]), weight_second, pre1, jnp.stack([saved[0], saved[planes - 1]])), ()
+        return second_ready(after(turn, [wide]), weight_second, pre1, saved_rims), [saved_rims]
 
     pieces, (*w2, rims, slope) = gathered(second_grad, [], second_weights_of)
 
+    n = len(pieces)
     halves, (before, behind) = first_use(
-        lambda g_hi, g_lo, _, rims, *refs: outer_part(g_hi, g_lo, refs[:4], *refs[4:], rims),
-        spots, pieces, [rims, *w2[:2], *w2[4:]], [shape(3, channels, area)] * 2, flops // 9, "second_outer", [])
+        lambda *refs: second_outer_kernel(n, *refs), spots, pieces, [rims, *w2[:2], *w2[4:]],
+        [shape(3, channels, area)] * 2, flops // 9, "second_outer")
     before, behind = edges(before, behind)
     own = inner(halves, w2, planes, flops, "second_inner")
     first_grad = call(first_kernel, shape(planes, channels, area), [], [own, before, behind, slope], name="first_grad")
     h_hi, h_lo = input_halves(0, pre1, before, behind, "second_input")
 
-    second_parts = call(
-        lambda g_hi, g_lo, i_hi, i_lo, *outs: filter_part(g_hi, g_lo, i_hi, i_lo, outs, range(4)),
-        [quarter] * 4, [], [*halves, h_hi, h_lo], 0, flops, "second_filter")
+    second_parts = filter_quarters(range(4), halves, (h_hi, h_lo), flops, "second_filter")
 
     def second_sum(far, near, _):
         parts = lax.optimization_barrier((*second_parts, near))[:4]
         one, three = to_row(parts[1], 1), to_row(parts[3], 3)
         two = to_row(after(parts[2], [one, three]), 2)
         halves = input_halves(1, after(saved, [far]), before, behind, "first_input")
-        return ([parts[0], one, two, three], halves), [one, three, *halves]
-
-    pieces, (second_rows, (x_hi, x_lo)) = gathered(first_grad, second_parts, second_sum)
+        w1 = weight_halves(after(turn, [far]), weight_first, "first_weights")
+        return ([parts[0], one, two, three], halves, w1), [one, three, *halves, *w1]
+
+    pieces, (second_rows, inputs, w1) = gathered(first_grad, second_parts, second_sum)
     halves, (part_2, part_1) = first_use(
-        lambda g_hi, g_lo, copies, *outs: filter_part(g_hi, g_lo, *arrived(copies), outs, (2, 1)),
-        spots, pieces, [], [quarter] * 2, flops // 2, "first_filter", [x_hi, x_lo])
+        lambda *refs: first_filter_kernel(n, (2, 1), *refs), spots, pieces, inputs, [quarter] * 2, flops // 2,
+        "first_filter")
     row_2, row_1 = to_row(part_2, 2), to_row(part_1, 1)
-    part_3, part_0 = call(
-        lambda g_hi, g_lo, i_hi, i_lo, *outs: filter_part(g_hi, g_lo, i_hi, i_lo, outs, (3, 0)),
-        [quarter] * 2, [], [*halves, x_hi, x_lo], 0, flops // 2, "first_filter_rest")
+    part_3, part_0 = filter_quarters((3, 0), halves, inputs, flops // 2, "first_filter_rest")
     first_rows = [part_0, row_1, row_2, to_row(part_3, 3)]
 
     second_rows = lax.optimization_barrier((*second_rows, part_0))[:4]
     second_rows = turned_sum(z_spots, second_rows)
-    w1 = weight_halves(after(turn, [second_rows[0]]), weight_first, "first_weights")
-    before, behind = call(
-        lambda g_hi, g_lo, *refs: outer_part(g_hi, g_lo, refs[:4], *refs[4:]), [shape(1, channels, area)] * 2, [],
-        [*halves, *w1[:2], *w1[4:]], 0, flops // 9, "first_outer")
-    first_rows = lax.optimization_barrier((*first_rows, before))[:4]
+    own = inner(halves, w1, planes, flops, "first_inner")
+    first_rows = lax.optimization_barrier((*first_rows, own))[:4]
     first_rows = turned_sum(z_spots, first_rows)
-    own = inner([after(halves[0], [first_rows[0]]), halves[1]], w1, planes, flops, "first_inner")
-    second_weights = owner_sum(second_rows, scale)
-    first_weights = owner_sum(first_rows, scale)
+    before, behind = call(first_outer_kernel, [shape(1, channels, area)] * 2, [],
+                          [after(halves[0], [first_rows[0]]), halves[1], *w1[:2], *w1[4:]], 0, flops // 9, "first_outer")
+    second_rows = lax.optimization_barrier((*to_owners(second_rows), first_rows[0]))[:4]
+    second_weights = last_sum(second_rows, scale)
+    first_weights = last_sum(to_owners(first_rows), scale)
     before, behind = edges(before, behind)
     input_grad = call(input_kernel, shape(planes, channels, area), [], [own, before, behind], name="input_grad")
     return (jnp.transpose(input_grad, (1, 0, 2)), first_weights.reshape(taps, channels, -1),

time: 133 us -> 134 us (level)
  starting transfers between devices: 49.9 us -> 59 us
  waiting for transfers between devices: 38.1 us -> 31.6 us
  Pallas kernels: 37.3 us -> 33.5 us
    ppermute x34, starting transfers between devices: 49.9 us -> 59 us  [send(): return lax.ppermute(value, axis, moves)]
    ppermute x34, waiting for transfers between devices: 38.1 us -> 31.6 us  [send(): return lax.ppermute(value, axis, moves)]
    pallas_call x17, Pallas kernels: 37.3 us -> 33.5 us  [call(): pl.pallas_call(kernel, out_shape=out_shape, in_specs=[SM] * n_smem + [VM]...]
    unnamed x11 -> x13, local copies, waits for them, and re-layouts: 2.1 us -> 2.92 us
  transfers between devices with their start and end apart: 34 -> 34, of which waited for: 12 -> 13; matrix products, arithmetic and copies ran while one was open for 4% -> 4% of each run, Pallas kernels for 26% -> 23%
where the time goes in v4:
time: 134 us; the launch traced here: 132 us
  starting transfers between devices  59 us (44%)
  Pallas kernels  33.5 us (25%)
  waiting for transfers between devices  31.6 us (24%)
  local copies, waits for them, and re-layouts  4.49 us (3%)
  other arithmetic  2.85 us (2%)
    ppermute x34, starting transfers between devices, send(): return lax.ppermute(value, axis, moves)  59 us
    pallas_call x17, Pallas kernels, call(): pl.pallas_call(kernel, out_shape=out_shape, in_specs=[SM] * n_smem + [VM]...  33.5 us
    ppermute x34, waiting for transfers between devices, send(): return lax.ppermute(value, axis, moves)  31.6 us
    unnamed x13, local copies, waits for them, and re-layouts  2.92 us
  transfers between devices with their start and end apart: 34, of which 13 were waited for; matrix products, arithmetic and copies ran while one was open for 4% of the time, Pallas kernels for 23%

profile of v4, /device:TPU:8, one launch (start us, length us, event | category | flops | bytes accessed | tf_op | source)
XLA Modules:
  0.0 132.4 jit_solution(11553947183576379658)
XLA Ops:
  1.7 7.3 %collective-permute-start.3 = (f32[6,32,256]{2,1,0:T(8,128)S(1)}, f32[6,32,256]{2,1,0:T(8,128)S(1)}, u32[]{:S(2)}, u32[]{:S(2)}) collective-permute-start(f32[6,32,256]{2,1,0:T(8,128)S(1)} %fusion.5.refs_1_), channel_id=1, source_target_pairs={{0,8},{1,9},{2,10},{3,11},{4,12},{5,13},{6,14},{7,15},{8,0},{9,1},... | collective-permute-start | bytes 589832 | tf_op jit(solution)/shard_map/ppermute | solution.py:331
  9.0 3.0 %collective-permute-start.2 = (f32[6,32,256]{2,1,0:T(8,128)S(1)}, f32[6,32,256]{2,1,0:T(8,128)S(1)}, u32[]{:S(2)}, u32[]{:S(2)}) collective-permute-start(f32[6,32,256]{2,1,0:T(8,128)S(1)} %fusion.5.refs_1_), channel_id=1, source_target_pairs={{0,4},{1,5},{2,6},{3,7},{4,0},{5,1},{6,2},{7,3},{8,12},{9,13},{10,... | collective-permute-start | bytes 589832 | tf_op jit(solution)/shard_map/ppermute | solution.py:331
  15.5 5.7 %collective-permute-done.1.refs_3_ = f32[6,32,256]{2,1,0:T(8,128)S(1)} collective-permute-done((f32[6,32,256]{2,1,0:T(8,128)S(1)}, f32[6,32,256]{2,1,0:T(8,128)S(1)}, u32[]{:S(2)}, u32[]{:S(2)}) %collective-permute-start.1) | collective-permute-done | bytes 196640 | tf_op jit(solution)/shard_map/ppermute | solution.py:331
  21.4 2.7 %collective-permute-start.6 = (f32[6,32,256]{2,1,0:T(8,128)S(1)}, f32[6,32,256]{2,1,0:T(8,128)S(1)}, u32[]{:S(2)}, u32[]{:S(2)}) collective-permute-start(f32[6,32,256]{2,1,0:T(8,128)S(1)} %collective-permute-done.3.refs_5_), channel_id=1, source_target_pairs={{0,4},{1,5},{2,6},{3,7},{4,0},{5,1},{6,2},{7,3},{8,12},{9,13},{10,... | collective-permute-start | bytes 589832 | tf_op jit(solution)/shard_map/ppermute | solution.py:331
  27.8 6.0 %collective-permute-done.4.refs_6_ = f32[6,32,256]{2,1,0:T(8,128)S(1)} collective-permute-done((f32[6,32,256]{2,1,0:T(8,128)S(1)}, f32[6,32,256]{2,1,0:T(8,128)S(1)}, u32[]{:S(2)}, u32[]{:S(2)}) %collective-permute-start.4) | collective-permute-done | bytes 196640 | tf_op jit(solution)/shard_map/ppermute | solution.py:331
  38.5 2.6 %second_outer.1 = (bf16[16,32,1536]{2,1,0:T(8,128)(2,1)S(1)}, bf16[16,32,1536]{2,1,0:T(8,128)(2,1)S(1)}, f32[3,32,256]{2,1,0:T(8,128)S(1)}, f32[3,32,256]{2,1,0:T(8,128)S(1)}) custom-call(s32[16]{0:T(128)S(1)} %fusion.6.refs_0_, f32[6,32,256]{2,1,0:T(8,128)S(1)} %fusion.5.refs_1_, f32[6,32,256]{2,1,0:T(8,128)S(1)} %collective-permute-done.refs_2_, ...), custom_call_target="tpu_custom_call" | custom-call | flops 452984832 | bytes 7798848 | tf_op jit(solution)/shard_map/second_outer/pallas_call | solution.py:29
  41.1 2.9 %collective-permute-start.9 = (f32[3,32,256]{2,1,0:T(8,128)S(1)}, f32[3,32,256]{2,1,0:T(8,128)S(1)}, u32[]{:S(2)}, u32[]{:S(2)}) collective-permute-start(f32[3,32,256]{2,1,0:T(8,128)S(1)} %get-tuple-element.82), channel_id=1, source_target_pairs={{0,16},{16,32},{32,48},{48,64},{64,80},{80,96},{96,112},{112,128},... | collective-permute-start | bytes 294920 | tf_op jit(solution)/shard_map/ppermute | solution.py:331
  44.1 5.6 %collective-permute-start.10 = (f32[3,32,256]{2,1,0:T(8,128)S(1)}, f32[3,32,256]{2,1,0:T(8,128)S(1)}, u32[]{:S(2)}, u32[]{:S(2)}) collective-permute-start(f32[3,32,256]{2,1,0:T(8,128)S(1)} %get-tuple-element.83), channel_id=1, source_target_pairs={{16,0},{32,16},{48,32},{64,48},{80,64},{96,80},{112,96},{128,112},... | collective-permute-start | bytes 294920 | tf_op jit(solution)/shard_map/ppermute | solution.py:331
  49.7 5.5 %second_inner.1.own = f32[6,32,256]{2,1,0:T(8,128)S(1)} custom-call(bf16[16,32,1536]{2,1,0:T(8,128)(2,1)S(1)} %get-tuple-element.78.g_hi.refs_0_, bf16[16,32,1536]{2,1,0:T(8,128)(2,1)S(1)} %get-tuple-element.79.g_lo.refs_1_, bf16[288,512]{1,0:T(8,128)(2,1)S(1)} %get-tuple-element.74.refs_12_.refs_0_, ...), custom_call_target="tpu_custom_call" | custom-call | flops 4076863488 | bytes 5111808 | tf_op jit(solution)/shard_map/second_inner/pallas_call | solution.py:29
  56.4 2.2 %collective-permute-start.13 = (f32[6,32,256]{2,1,0:T(8,128)S(1)}, f32[6,32,256]{2,1,0:T(8,128)S(1)}, u32[]{:S(2)}, u32[]{:S(2)}) collective-permute-start(f32[6,32,256]{2,1,0:T(8,128)S(1)} %first_grad.1.refs_1_), channel_id=1, source_target_pairs={{0,4},{1,5},{2,6},{3,7},{4,0},{5,1},{6,2},{7,3},{8,12},{9,13},{10,... | collective-permute-start | bytes 589832 | tf_op jit(solution)/shard_map/ppermute | solution.py:331
  62.2 4.3 %second_filter.1 = (f32[864,128]{1,0:T(8,128)S(1)}, f32[864,128]{1,0:T(8,128)S(1)}, f32[864,128]{1,0:T(8,128)S(1)}, f32[864,128]{1,0:T(8,128)S(1)}) custom-call(bf16[16,32,1536]{2,1,0:T(8,128)(2,1)S(1)} %get-tuple-element.78.g_hi.refs_0_, bf16[16,32,1536]{2,1,0:T(8,128)(2,1)S(1)} %get-tuple-element.79.g_lo.refs_1_, ...), custom_call_target="tpu_custom_call" | custom-call | flops 4076863488 | bytes 7274496 | tf_op jit(solution)/shard_map/second_filter/pallas_call | solution.py:29
  70.4 2.1 %collective-permute-start.17 = (f32[6,32,256]{2,1,0:T(8,128)S(1)}, f32[6,32,256]{2,1,0:T(8,128)S(1)}, u32[]{:S(2)}, u32[]{:S(2)}) collective-permute-start(f32[6,32,256]{2,1,0:T(8,128)S(1)} %collective-permute-done.14.refs_5_), channel_id=1, source_target_pairs={{0,4},{1,5},{2,6},{3,7},{4,0},{5,1},{6,2},{7,3},{8,12},{9,13},{10,... | collective-permute-start | bytes 589832 | tf_op jit(solution)/shard_map/ppermute | solution.py:331
  77.2 2.2 %collective-permute-done.17.refs_8_ = f32[6,32,256]{2,1,0:T(8,128)S(1)} collective-permute-done((f32[6,32,256]{2,1,0:T(8,128)S(1)}, f32[6,32,256]{2,1,0:T(8,128)S(1)}, u32[]{:S(2)}, u32[]{:S(2)}) %collective-permute-start.17) | collective-permute-done | bytes 196640 | tf_op jit(solution)/shard_map/ppermute | solution.py:331
  82.1 2.4 %collective-permute-start.30 = (f32[864,128]{1,0:T(8,128)S(1)}, f32[864,128]{1,0:T(8,128)S(1)}, u32[]{:S(2)}, u32[]{:S(2)}) collective-permute-start(f32[864,128]{1,0:T(8,128)S(1)} %get-tuple-element.124), channel_id=1, source_target_pairs={{0,128},{16,144},{32,160},{48,176},{64,192},{80,208},{96,224},{112... | collective-permute-start | bytes 1327112 | tf_op jit(solution)/shard_map/ppermute | solution.py:331
  84.4 3.1 %first_filter.1 = (bf16[16,32,1536]{2,1,0:T(8,128)(2,1)S(1)}, bf16[16,32,1536]{2,1,0:T(8,128)(2,1)S(1)}, f32[864,128]{1,0:T(8,128)S(1)}, f32[864,128]{1,0:T(8,128)S(1)}) custom-call(s32[16]{0:T(128)S(1)} %fusion.6.refs_0_, f32[6,32,256]{2,1,0:T(8,128)S(1)} %first_grad.1.refs_1_, f32[6,32,256]{2,1,0:T(8,128)S(1)} %collective-permute-done.11.refs_2_, ...), custom_call_target="tpu_custom_call" | custom-call | flops 2038431744 | bytes 9535552 | tf_op jit(solution)/shard_map/first_filter/pallas_call | solution.py:29
  89.1 2.1 %collective-permute-start.23 = (f32[864,128]{1,0:T(8,128)S(1)}, f32[864,128]{1,0:T(8,128)S(1)}, u32[]{:S(2)}, u32[]{:S(2)}) collective-permute-start(f32[864,128]{1,0:T(8,128)S(1)} %get-tuple-element.109), channel_id=1, source_target_pairs={{0,128},{16,144},{32,160},{48,176},{64,192},{80,208},{96,224},{112... | collective-permute-start | bytes 1327112 | tf_op jit(solution)/shard_map/ppermute | solution.py:331
  91.2 2.3 %first_filter_rest.1 = (f32[864,128]{1,0:T(8,128)S(1)}, f32[864,128]{1,0:T(8,128)S(1)}) custom-call(bf16[16,32,1536]{2,1,0:T(8,128)(2,1)S(1)} %get-tuple-element.116.g_hi.refs_0_, bf16[16,32,1536]{2,1,0:T(8,128)(2,1)S(1)} %get-tuple-element.106.g_lo.refs_1_, bf16[288,2048]{1,0:T(8,128)(2,1)S(1)} %get-tuple-element.95.refs_11_.refs_2_, ...), custom_call_target="tpu_custom_call" | custom-call | flops 2038431744 | bytes 6389760 | tf_op jit(solution)/shard_map/first_filter_rest/pallas_call | solution.py:29
  94.8 1.9 %collective-permute-done.30.c = f32[864,128]{1,0:T(8,128)S(1)} collective-permute-done((f32[864,128]{1,0:T(8,128)S(1)}, f32[864,128]{1,0:T(8,128)S(1)}, u32[]{:S(2)}, u32[]{:S(2)}) %collective-permute-start.30) | collective-permute-done | bytes 442400 | tf_op jit(solution)/shard_map/ppermute | solution.py:331
  98.9 7.3 %collective-permute-done.22.b = f32[864,128]{1,0:T(8,128)S(1)} collective-permute-done((f32[864,128]{1,0:T(8,128)S(1)}, f32[864,128]{1,0:T(8,128)S(1)}, u32[]{:S(2)}, u32[]{:S(2)}) %collective-permute-start.22) | collective-permute-done | bytes 442400 | tf_op jit(solution)/shard_map/ppermute | solution.py:331
  106.8 5.5 %first_inner.1.own = f32[6,32,256]{2,1,0:T(8,128)S(1)} custom-call(bf16[16,32,1536]{2,1,0:T(8,128)(2,1)S(1)} %get-tuple-element.116.g_hi.refs_0_, bf16[16,32,1536]{2,1,0:T(8,128)(2,1)S(1)} %get-tuple-element.106.g_lo.refs_1_, bf16[288,512]{1,0:T(8,128)(2,1)S(1)} %get-tuple-element.98.refs_0_, bf16[288,512]{1,0:T(8,128)(2,1)S(1)} %get-tuple-element.99.refs_1_, ...), custom_call_target="tpu_custom_call" | custom-call | flops 4076863488 | bytes 5111808 | tf_op jit(solution)/shard_map/first_inner/pallas_call | solution.py:29
  112.3 2.8 %collective-permute-done.24.d = f32[864,128]{1,0:T(8,128)S(1)} collective-permute-done((f32[864,128]{1,0:T(8,128)S(1)}, f32[864,128]{1,0:T(8,128)S(1)}, u32[]{:S(2)}, u32[]{:S(2)}) %collective-permute-start.24) | collective-permute-done | bytes 442400 | tf_op jit(solution)/shard_map/ppermute | solution.py:331
  117.3 2.5 %collective-permute-start.29 = (f32[32,864]{1,0:T(8,128)S(1)}, f32[32,864]{1,0:T(8,128)S(1)}, u32[]{:S(2)}, u32[]{:S(2)}) collective-permute-start(f32[32,864]{1,0:T(8,128)S(1)} %get-tuple-element.121), channel_id=1, source_target_pairs={{0,48},{16,0},{32,16},{48,32},{64,112},{80,64},{96,80},{112,96},{1... | collective-permute-start | bytes 331784 | tf_op jit(solution)/shard_map/ppermute | solution.py:331
  120.6 2.5 %collective-permute-start.25 = (f32[1,32,256]{2,1,0:T(8,128)S(1)}, f32[1,32,256]{2,1,0:T(8,128)S(1)}, u32[]{:S(2)}, u32[]{:S(2)}) collective-permute-start(f32[1,32,256]{2,1,0:T(8,128)S(1)} %get-tuple-element.117), channel_id=1, source_target_pairs={{0,16},{16,32},{32,48},{48,64},{64,80},{80,96},{96,112},{112,128},... | collective-permute-start | bytes 98312 | tf_op jit(solution)/shard_map/ppermute | solution.py:331
  123.1 6.1 %collective-permute-start.26 = (f32[1,32,256]{2,1,0:T(8,128)S(1)}, f32[1,32,256]{2,1,0:T(8,128)S(1)}, u32[]{:S(2)}, u32[]{:S(2)}) collective-permute-start(f32[1,32,256]{2,1,0:T(8,128)S(1)} %get-tuple-element.118), channel_id=1, source_target_pairs={{16,0},{32,16},{48,32},{64,48},{80,64},{96,80},{112,96},{128,112},... | collective-permute-start | bytes 98312 | tf_op jit(solution)/shard_map/ppermute | solution.py:331
  (85 shorter events, 40.8 us)
Async XLA Ops:
  1.7 13.7 %collective-permute-start.3 = (f32[6,32,256]{2,1,0:T(8,128)S(1)}, f32[6,32,256]{2,1,0:T(8,128)S(1)}, u32[]{:S(2)}, u32[]{:S(2)}) collective-permute-start(f32[6,32,256]{2,1,0:T(8,128)S(1)} %fusion.5.refs_1_), channel_id=1, source_target_pairs={{0,8},{1,9},{2,10},{3,11},{4,12},{5,13},{6,14},{7,15},{8,0},{9,1},... | collective-permute-start | bytes 589832 | tf_op jit(solution)/shard_map/ppermute | solution.py:331
  9.0 17.1 %collective-permute-start.2 = (f32[6,32,256]{2,1,0:T(8,128)S(1)}, f32[6,32,256]{2,1,0:T(8,128)S(1)}, u32[]{:S(2)}, u32[]{:S(2)}) collective-permute-start(f32[6,32,256]{2,1,0:T(8,128)S(1)} %fusion.5.refs_1_), channel_id=1, source_target_pairs={{0,4},{1,5},{2,6},{3,7},{4,0},{5,1},{6,2},{7,3},{8,12},{9,13},{10,... | collective-permute-start | bytes 589832 | tf_op jit(solution)/shard_map/ppermute | solution.py:331
  12.0 9.2 %collective-permute-start.1 = (f32[6,32,256]{2,1,0:T(8,128)S(1)}, f32[6,32,256]{2,1,0:T(8,128)S(1)}, u32[]{:S(2)}, u32[]{:S(2)}) collective-permute-start(f32[6,32,256]{2,1,0:T(8,128)S(1)} %fusion.5.refs_1_), channel_id=1, source_target_pairs={{0,6},{1,7},{2,0},{3,1},{4,2},{5,3},{6,4},{7,5},{8,14},{9,15},{10,... | collective-permute-start | bytes 589832 | tf_op jit(solution)/shard_map/ppermute | solution.py:331
  21.4 13.8 %collective-permute-start.6 = (f32[6,32,256]{2,1,0:T(8,128)S(1)}, f32[6,32,256]{2,1,0:T(8,128)S(1)}, u32[]{:S(2)}, u32[]{:S(2)}) collective-permute-start(f32[6,32,256]{2,1,0:T(8,128)S(1)} %collective-permute-done.3.refs_5_), channel_id=1, source_target_pairs={{0,4},{1,5},{2,6},{3,7},{4,0},{5,1},{6,2},{7,3},{8,12},{9,13},{10,... | collective-permute-start | bytes 589832 | tf_op jit(solution)/shard_map/ppermute | solution.py:331
  24.1 10.4 %collective-permute-start.5 = (f32[6,32,256]{2,1,0:T(8,128)S(1)}, f32[6,32,256]{2,1,0:T(8,128)S(1)}, u32[]{:S(2)}, u32[]{:S(2)}) collective-permute-start(f32[6,32,256]{2,1,0:T(8,128)S(1)} %collective-permute-done.3.refs_5_), channel_id=1, source_target_pairs={{0,6},{1,7},{2,0},{3,1},{4,2},{5,3},{6,4},{7,5},{8,14},{9,15},{10,... | collective-permute-start | bytes 589832 | tf_op jit(solution)/shard_map/ppermute | solution.py:331
  27.1 11.0 %collective-permute-start.7 = (f32[24,32,256]{2,1,0:T(8,128)}, f32[24,32,256]{2,1,0:T(8,128)}, u32[]{:S(2)}, u32[]{:S(2)}) collective-permute-start(f32[24,32,256]{2,1,0:T(8,128)} %pad_maximum_fusion), channel_id=1, source_target_pairs={{0,1},{1,0},{2,3},{3,2},{4,5},{5,4},{6,7},{7,6},{8,9},{9,8},{10,11... | collective-permute-start | bytes 2359304 | tf_op jit(solution)/shard_map/ppermute | solution.py:331
  41.1 14.1 %collective-permute-start.9 = (f32[3,32,256]{2,1,0:T(8,128)S(1)}, f32[3,32,256]{2,1,0:T(8,128)S(1)}, u32[]{:S(2)}, u32[]{:S(2)}) collective-permute-start(f32[3,32,256]{2,1,0:T(8,128)S(1)} %get-tuple-element.82), channel_id=1, source_target_pairs={{0,16},{16,32},{32,48},{48,64},{64,80},{80,96},{96,112},{112,128},... | collective-permute-start | bytes 294920 | tf_op jit(solution)/shard_map/ppermute | solution.py:331
  44.1 11.2 %collective-permute-start.10 = (f32[3,32,256]{2,1,0:T(8,128)S(1)}, f32[3,32,256]{2,1,0:T(8,128)S(1)}, u32[]{:S(2)}, u32[]{:S(2)}) collective-permute-start(f32[3,32,256]{2,1,0:T(8,128)S(1)} %get-tuple-element.83), channel_id=1, source_target_pairs={{16,0},{32,16},{48,32},{64,48},{80,64},{96,80},{112,96},{128,112},... | collective-permute-start | bytes 294920 | tf_op jit(solution)/shard_map/ppermute | solution.py:331
  55.3 15.2 %collective-permute-start.14 = (f32[6,32,256]{2,1,0:T(8,128)S(1)}, f32[6,32,256]{2,1,0:T(8,128)S(1)}, u32[]{:S(2)}, u32[]{:S(2)}) collective-permute-start(f32[6,32,256]{2,1,0:T(8,128)S(1)} %first_grad.1.refs_1_), channel_id=1, source_target_pairs={{0,8},{1,9},{2,10},{3,11},{4,12},{5,13},{6,14},{7,15},{8,0},{9,1},... | collective-permute-start | bytes 589832 | tf_op jit(solution)/shard_map/ppermute | solution.py:331
  56.4 10.1 %collective-permute-start.13 = (f32[6,32,256]{2,1,0:T(8,128)S(1)}, f32[6,32,256]{2,1,0:T(8,128)S(1)}, u32[]{:S(2)}, u32[]{:S(2)}) collective-permute-start(f32[6,32,256]{2,1,0:T(8,128)S(1)} %first_grad.1.refs_1_), channel_id=1, source_target_pairs={{0,4},{1,5},{2,6},{3,7},{4,0},{5,1},{6,2},{7,3},{8,12},{9,13},{10,... | collective-permute-start | bytes 589832 | tf_op jit(solution)/shard_map/ppermute | solution.py:331
  68.3 13.6 %collective-permute-start.19 = (f32[864,128]{1,0:T(8,128)S(1)}, f32[864,128]{1,0:T(8,128)S(1)}, u32[]{:S(2)}, u32[]{:S(2)}) collective-permute-start(f32[864,128]{1,0:T(8,128)S(1)} %get-tuple-element.92), channel_id=1, source_target_pairs={{0,64},{16,80},{32,96},{48,112},{64,128},{80,144},{96,160},{112,17... | collective-permute-start | bytes 1327112 | tf_op jit(solution)/shard_map/ppermute | solution.py:331
  70.0 12.0 %collective-permute-start.20 = (f32[864,128]{1,0:T(8,128)S(1)}, f32[864,128]{1,0:T(8,128)S(1)}, u32[]{:S(2)}, u32[]{:S(2)}) collective-permute-start(f32[864,128]{1,0:T(8,128)S(1)} %get-tuple-element.93), channel_id=1, source_target_pairs={{0,192},{16,208},{32,224},{48,240},{64,0},{80,16},{96,32},{112,48}... | collective-permute-start | bytes 1327112 | tf_op jit(solution)/shard_map/ppermute | solution.py:331
  70.4 8.9 %collective-permute-start.17 = (f32[6,32,256]{2,1,0:T(8,128)S(1)}, f32[6,32,256]{2,1,0:T(8,128)S(1)}, u32[]{:S(2)}, u32[]{:S(2)}) collective-permute-start(f32[6,32,256]{2,1,0:T(8,128)S(1)} %collective-permute-done.14.refs_5_), channel_id=1, source_target_pairs={{0,4},{1,5},{2,6},{3,7},{4,0},{5,1},{6,2},{7,3},{8,12},{9,13},{10,... | collective-permute-start | bytes 589832 | tf_op jit(solution)/shard_map/ppermute | solution.py:331
  82.1 14.7 %collective-permute-start.30 = (f32[864,128]{1,0:T(8,128)S(1)}, f32[864,128]{1,0:T(8,128)S(1)}, u32[]{:S(2)}, u32[]{:S(2)}) collective-permute-start(f32[864,128]{1,0:T(8,128)S(1)} %get-tuple-element.124), channel_id=1, source_target_pairs={{0,128},{16,144},{32,160},{48,176},{64,192},{80,208},{96,224},{112... | collective-permute-start | bytes 1327112 | tf_op jit(solution)/shard_map/ppermute | solution.py:331
  87.5 18.7 %collective-permute-start.22 = (f32[864,128]{1,0:T(8,128)S(1)}, f32[864,128]{1,0:T(8,128)S(1)}, u32[]{:S(2)}, u32[]{:S(2)}) collective-permute-start(f32[864,128]{1,0:T(8,128)S(1)} %get-tuple-element.108), channel_id=1, source_target_pairs={{0,64},{16,80},{32,96},{48,112},{64,128},{80,144},{96,160},{112,17... | collective-permute-start | bytes 1327112 | tf_op jit(solution)/shard_map/ppermute | solution.py:331
  89.1 23.2 %collective-permute-start.23 = (f32[864,128]{1,0:T(8,128)S(1)}, f32[864,128]{1,0:T(8,128)S(1)}, u32[]{:S(2)}, u32[]{:S(2)}) collective-permute-start(f32[864,128]{1,0:T(8,128)S(1)} %get-tuple-element.109), channel_id=1, source_target_pairs={{0,128},{16,144},{32,160},{48,176},{64,192},{80,208},{96,224},{112... | collective-permute-start | bytes 1327112 | tf_op jit(solution)/shard_map/ppermute | solution.py:331
  93.5 21.6 %collective-permute-start.24 = (f32[864,128]{1,0:T(8,128)S(1)}, f32[864,128]{1,0:T(8,128)S(1)}, u32[]{:S(2)}, u32[]{:S(2)}) collective-permute-start(f32[864,128]{1,0:T(8,128)S(1)} %get-tuple-element.110), channel_id=1, source_target_pairs={{0,192},{16,208},{32,224},{48,240},{64,0},{80,16},{96,32},{112,48}... | collective-permute-start | bytes 1327112 | tf_op jit(solution)/shard_map/ppermute | solution.py:331
  97.5 19.8 %collective-permute-start.31 = (f32[32,864]{1,0:T(8,128)S(1)}, f32[32,864]{1,0:T(8,128)S(1)}, u32[]{:S(2)}, u32[]{:S(2)}) collective-permute-start(f32[32,864]{1,0:T(8,128)S(1)} %get-tuple-element.130), channel_id=1, source_target_pairs={{0,16},{16,32},{32,48},{48,0},{64,80},{80,96},{96,112},{112,64},{1... | collective-permute-start | bytes 331784 | tf_op jit(solution)/shard_map/ppermute | solution.py:331
  97.6 23.0 %collective-permute-start.32 = (f32[32,864]{1,0:T(8,128)S(1)}, f32[32,864]{1,0:T(8,128)S(1)}, u32[]{:S(2)}, u32[]{:S(2)}) collective-permute-start(f32[32,864]{1,0:T(8,128)S(1)} %get-tuple-element.131), channel_id=1, source_target_pairs={{0,32},{16,48},{32,0},{48,16},{64,96},{80,112},{96,64},{112,80},{1... | collective-permute-start | bytes 331784 | tf_op jit(solution)/shard_map/ppermute | solution.py:331
  106.3 16.8 %collective-permute-start.33 = (f32[32,864]{1,0:T(8,128)S(1)}, f32[32,864]{1,0:T(8,128)S(1)}, u32[]{:S(2)}, u32[]{:S(2)}) collective-permute-start(f32[32,864]{1,0:T(8,128)S(1)} %get-tuple-element.132), channel_id=1, source_target_pairs={{0,48},{16,0},{32,16},{48,32},{64,112},{80,64},{96,80},{112,96},{1... | collective-permute-start | bytes 331784 | tf_op jit(solution)/shard_map/ppermute | solution.py:331
  115.9 15.6 %collective-permute-start.27 = (f32[32,864]{1,0:T(8,128)S(1)}, f32[32,864]{1,0:T(8,128)S(1)}, u32[]{:S(2)}, u32[]{:S(2)}) collective-permute-start(f32[32,864]{1,0:T(8,128)S(1)} %get-tuple-element.119), channel_id=1, source_target_pairs={{0,16},{16,32},{32,48},{48,0},{64,80},{80,96},{96,112},{112,64},{1... | collective-permute-start | bytes 331784 | tf_op jit(solution)/shard_map/ppermute | solution.py:331
  116.0 15.5 %collective-permute-start.28 = (f32[32,864]{1,0:T(8,128)S(1)}, f32[32,864]{1,0:T(8,128)S(1)}, u32[]{:S(2)}, u32[]{:S(2)}) collective-permute-start(f32[32,864]{1,0:T(8,128)S(1)} %get-tuple-element.120), channel_id=1, source_target_pairs={{0,32},{16,48},{32,0},{48,16},{64,96},{80,112},{96,64},{112,80},{1... | collective-permute-start | bytes 331784 | tf_op jit(solution)/shard_map/ppermute | solution.py:331
  117.3 14.1 %collective-permute-start.29 = (f32[32,864]{1,0:T(8,128)S(1)}, f32[32,864]{1,0:T(8,128)S(1)}, u32[]{:S(2)}, u32[]{:S(2)}) collective-permute-start(f32[32,864]{1,0:T(8,128)S(1)} %get-tuple-element.121), channel_id=1, source_target_pairs={{0,48},{16,0},{32,16},{48,32},{64,112},{80,64},{96,80},{112,96},{1... | collective-permute-start | bytes 331784 | tf_op jit(solution)/shard_map/ppermute | solution.py:331
  120.6 9.5 %collective-permute-start.25 = (f32[1,32,256]{2,1,0:T(8,128)S(1)}, f32[1,32,256]{2,1,0:T(8,128)S(1)}, u32[]{:S(2)}, u32[]{:S(2)}) collective-permute-start(f32[1,32,256]{2,1,0:T(8,128)S(1)} %get-tuple-element.117), channel_id=1, source_target_pairs={{0,16},{16,32},{32,48},{48,64},{64,80},{80,96},{96,112},{112,128},... | collective-permute-start | bytes 98312 | tf_op jit(solution)/shard_map/ppermute | solution.py:331
  (15 other events, 130.9 us)

commit v5 on v4

--- a/solution.py
+++ b/solution.py
@@ -257,11 +257,30 @@
     return (g_hi, g_lo), rest
 
 
-def inner(halves, weights, planes, flops, name):
+def flat_part(g_hi, g_lo, *refs):
+    weights, (own_ref, sums) = refs[:6], refs[6:]
+    planes, third = own_ref.shape[0], sums.shape[1]
+    for p in range(planes):
+        taps = [a for a in range(3) if 0 <= p + a - 1 < planes]
+        w_hi, w_lo = (jnp.concatenate([weights[2 * a + n][...] for a in taps], 0) for n in range(2))
+        out = three_products(w_hi, w_lo, plane_of(g_hi, p), plane_of(g_lo, p))
+        for n, a in enumerate(taps):
+            q = p + a - 1
+            part = out[n * third:(n + 1) * third]
+            if p == max(q - 1, 0):
+                sums[q] = part
+            else:
+                sums[q] += part
+        if p:
+            own_ref[p - 1] = spread(sums.at[p - 1])
+    own_ref[planes - 1] = spread(sums.at[planes - 1])
+
+
+def inner(halves, weights, planes, flops, name, flat=False):
     third = weights[0].shape[0]
     channels = third // len(SHIFTS)
-    return call(inner_part, shape(planes, channels, AREA), [pltpu.VMEM((2, third, AREA), F32)],
-                [*halves, *weights], 0, flops, name)
+    return call(flat_part if flat else inner_part, shape(planes, channels, AREA),
+                [pltpu.VMEM((planes if flat else 2, third, AREA), F32)], [*halves, *weights], 0, flops, name)
 
 
 def turned_kernel(spots, a, b, c, d, *refs):
@@ -393,7 +412,7 @@
         lambda *refs: second_outer_kernel(n, *refs), spots, pieces, [rims, *w2[:2], *w2[4:]],
         [shape(3, channels, area)] * 2, flops // 9, "second_outer")
     before, behind = edges(before, behind)
-    own = inner(halves, w2, planes, flops, "second_inner")
+    own = inner(halves, w2, planes, flops, "second_inner", True)
     first_grad = call(first_kernel, shape(planes, channels, area), [], [own, before, behind, slope], name="first_grad")
     h_hi, h_lo = input_halves(0, pre1, before, behind, "second_input")
 
@@ -417,13 +436,12 @@
 
     second_rows = lax.optimization_barrier((*second_rows, part_0))[:4]
     second_rows = turned_sum(z_spots, second_rows)
-    own = inner(halves, w1, planes, flops, "first_inner")
-    first_rows = lax.optimization_barrier((*first_rows, own))[:4]
+    before, behind = call(first_outer_kernel, [shape(1, channels, area)] * 2, [],
+                          [*halves, *w1[:2], *w1[4:]], 0, flops // 9, "first_outer")
+    first_rows = lax.optimization_barrier((*first_rows, before))[:4]
     first_rows = turned_sum(z_spots, first_rows)
-    before, behind = call(first_outer_kernel, [shape(1, channels, area)] * 2, [],
-                          [after(halves[0], [first_rows[0]]), halves[1], *w1[:2], *w1[4:]], 0, flops // 9, "first_outer")
-    second_rows = lax.optimization_barrier((*to_owners(second_rows), first_rows[0]))[:4]
-    second_weights = last_sum(second_rows, scale)
+    own = inner([after(halves[0], [first_rows[0]]), halves[1]], w1, planes, flops, "first_inner")
+    second_weights = last_sum(to_owners(second_rows), scale)
     first_weights = last_sum(to_owners(first_rows), scale)
     before, behind = edges(before, behind)
     input_grad = call(input_kernel, shape(planes, channels, area), [], [own, before, behind], name="input_grad")

time: 134 us -> 129 us (0.963)
  waiting for transfers between devices: 31.6 us -> 28.2 us
  Pallas kernels: 33.5 us -> 32 us
    ppermute x34, waiting for transfers between devices: 31.6 us -> 28.2 us  [send(): return lax.ppermute(value, axis, moves)]
    pallas_call x17, Pallas kernels: 33.5 us -> 32 us  [call(): pl.pallas_call(kernel, out_shape=out_shape, in_specs=[SM] * n_smem + [VM]...]
  transfers between devices with their start and end apart: 34 -> 34, of which waited for: 13 -> 12; matrix products, arithmetic and copies ran while one was open for 4% -> 4% of each run, Pallas kernels for 23% -> 22%
where the time goes in v5:
time: 129 us
  starting transfers between devices  60 us (47%)
  Pallas kernels  32 us (25%)
  waiting for transfers between devices  28.2 us (22%)
  local copies, waits for them, and re-layouts  4.49 us (3%)
  other arithmetic  2.84 us (2%)
    ppermute x34, starting transfers between devices, send(): return lax.ppermute(value, axis, moves)  60 us
    pallas_call x17, Pallas kernels, call(): pl.pallas_call(kernel, out_shape=out_shape, in_specs=[SM] * n_smem + [VM]...  32 us
    ppermute x34, waiting for transfers between devices, send(): return lax.ppermute(value, axis, moves)  28.2 us
    unnamed x13, local copies, waits for them, and re-layouts  2.92 us
  transfers between devices with their start and end apart: 34, of which 12 were waited for; matrix products, arithmetic and copies ran while one was open for 4% of the time, Pallas kernels for 22%

profile of v5, /device:TPU:8, one launch (start us, length us, event | category | flops | bytes accessed | tf_op | source)
XLA Modules:
  0.0 128.5 jit_solution(13247326468833937443)
XLA Ops:
  1.7 7.3 %collective-permute-start.3 = (f32[6,32,256]{2,1,0:T(8,128)S(1)}, f32[6,32,256]{2,1,0:T(8,128)S(1)}, u32[]{:S(2)}, u32[]{:S(2)}) collective-permute-start(f32[6,32,256]{2,1,0:T(8,128)S(1)} %fusion.5.refs_1_), channel_id=1, source_target_pairs={{0,8},{1,9},{2,10},{3,11},{4,12},{5,13},{6,14},{7,15},{8,0},{9,1},... | collective-permute-start | bytes 589832 | tf_op jit(solution)/shard_map/ppermute | solution.py:350
  9.0 3.0 %collective-permute-start.2 = (f32[6,32,256]{2,1,0:T(8,128)S(1)}, f32[6,32,256]{2,1,0:T(8,128)S(1)}, u32[]{:S(2)}, u32[]{:S(2)}) collective-permute-start(f32[6,32,256]{2,1,0:T(8,128)S(1)} %fusion.5.refs_1_), channel_id=1, source_target_pairs={{0,4},{1,5},{2,6},{3,7},{4,0},{5,1},{6,2},{7,3},{8,12},{9,13},{10,... | collective-permute-start | bytes 589832 | tf_op jit(solution)/shard_map/ppermute | solution.py:350
  15.5 5.7 %collective-permute-done.1.refs_3_ = f32[6,32,256]{2,1,0:T(8,128)S(1)} collective-permute-done((f32[6,32,256]{2,1,0:T(8,128)S(1)}, f32[6,32,256]{2,1,0:T(8,128)S(1)}, u32[]{:S(2)}, u32[]{:S(2)}) %collective-permute-start.1) | collective-permute-done | bytes 196640 | tf_op jit(solution)/shard_map/ppermute | solution.py:350
  21.4 2.7 %collective-permute-start.6 = (f32[6,32,256]{2,1,0:T(8,128)S(1)}, f32[6,32,256]{2,1,0:T(8,128)S(1)}, u32[]{:S(2)}, u32[]{:S(2)}) collective-permute-start(f32[6,32,256]{2,1,0:T(8,128)S(1)} %collective-permute-done.3.refs_5_), channel_id=1, source_target_pairs={{0,4},{1,5},{2,6},{3,7},{4,0},{5,1},{6,2},{7,3},{8,12},{9,13},{10,... | collective-permute-start | bytes 589832 | tf_op jit(solution)/shard_map/ppermute | solution.py:350
  27.8 6.0 %collective-permute-done.4.refs_6_ = f32[6,32,256]{2,1,0:T(8,128)S(1)} collective-permute-done((f32[6,32,256]{2,1,0:T(8,128)S(1)}, f32[6,32,256]{2,1,0:T(8,128)S(1)}, u32[]{:S(2)}, u32[]{:S(2)}) %collective-permute-start.4) | collective-permute-done | bytes 196640 | tf_op jit(solution)/shard_map/ppermute | solution.py:350
  38.5 2.6 %second_outer.1 = (bf16[16,32,1536]{2,1,0:T(8,128)(2,1)S(1)}, bf16[16,32,1536]{2,1,0:T(8,128)(2,1)S(1)}, f32[3,32,256]{2,1,0:T(8,128)S(1)}, f32[3,32,256]{2,1,0:T(8,128)S(1)}) custom-call(s32[16]{0:T(128)S(1)} %fusion.6.refs_0_, f32[6,32,256]{2,1,0:T(8,128)S(1)} %fusion.5.refs_1_, f32[6,32,256]{2,1,0:T(8,128)S(1)} %collective-permute-done.refs_2_, ...), custom_call_target="tpu_custom_call" | custom-call | flops 452984832 | bytes 7798848 | tf_op jit(solution)/shard_map/second_outer/pallas_call | solution.py:29
  41.1 2.9 %collective-permute-start.9 = (f32[3,32,256]{2,1,0:T(8,128)S(1)}, f32[3,32,256]{2,1,0:T(8,128)S(1)}, u32[]{:S(2)}, u32[]{:S(2)}) collective-permute-start(f32[3,32,256]{2,1,0:T(8,128)S(1)} %get-tuple-element.78), channel_id=1, source_target_pairs={{0,16},{16,32},{32,48},{48,64},{64,80},{80,96},{96,112},{112,128},... | collective-permute-start | bytes 294920 | tf_op jit(solution)/shard_map/ppermute | solution.py:350
  44.1 5.6 %collective-permute-start.10 = (f32[3,32,256]{2,1,0:T(8,128)S(1)}, f32[3,32,256]{2,1,0:T(8,128)S(1)}, u32[]{:S(2)}, u32[]{:S(2)}) collective-permute-start(f32[3,32,256]{2,1,0:T(8,128)S(1)} %get-tuple-element.79), channel_id=1, source_target_pairs={{16,0},{32,16},{48,32},{64,48},{80,64},{96,80},{112,96},{128,112},... | collective-permute-start | bytes 294920 | tf_op jit(solution)/shard_map/ppermute | solution.py:350
  49.7 4.0 %second_inner.1.own = f32[6,32,256]{2,1,0:T(8,128)S(1)} custom-call(bf16[16,32,1536]{2,1,0:T(8,128)(2,1)S(1)} %get-tuple-element.74.g_hi.refs_0_, bf16[16,32,1536]{2,1,0:T(8,128)(2,1)S(1)} %get-tuple-element.75.g_lo.refs_1_, bf16[288,512]{1,0:T(8,128)(2,1)S(1)} %get-tuple-element.70.refs_12_.refs_0_, ...), custom_call_target="tpu_custom_call" | custom-call | flops 4076863488 | bytes 5111808 | tf_op jit(solution)/shard_map/second_inner/pallas_call | solution.py:29
  54.9 2.2 %collective-permute-start.13 = (f32[6,32,256]{2,1,0:T(8,128)S(1)}, f32[6,32,256]{2,1,0:T(8,128)S(1)}, u32[]{:S(2)}, u32[]{:S(2)}) collective-permute-start(f32[6,32,256]{2,1,0:T(8,128)S(1)} %first_grad.1.refs_1_), channel_id=1, source_target_pairs={{0,4},{1,5},{2,6},{3,7},{4,0},{5,1},{6,2},{7,3},{8,12},{9,13},{10,... | collective-permute-start | bytes 589832 | tf_op jit(solution)/shard_map/ppermute | solution.py:350
  60.7 4.3 %second_filter.1 = (f32[864,128]{1,0:T(8,128)S(1)}, f32[864,128]{1,0:T(8,128)S(1)}, f32[864,128]{1,0:T(8,128)S(1)}, f32[864,128]{1,0:T(8,128)S(1)}) custom-call(bf16[16,32,1536]{2,1,0:T(8,128)(2,1)S(1)} %get-tuple-element.74.g_hi.refs_0_, bf16[16,32,1536]{2,1,0:T(8,128)(2,1)S(1)} %get-tuple-element.75.g_lo.refs_1_, ...), custom_call_target="tpu_custom_call" | custom-call | flops 4076863488 | bytes 7274496 | tf_op jit(solution)/shard_map/second_filter/pallas_call | solution.py:29
  68.9 2.1 %collective-permute-start.17 = (f32[6,32,256]{2,1,0:T(8,128)S(1)}, f32[6,32,256]{2,1,0:T(8,128)S(1)}, u32[]{:S(2)}, u32[]{:S(2)}) collective-permute-start(f32[6,32,256]{2,1,0:T(8,128)S(1)} %collective-permute-done.14.refs_5_), channel_id=1, source_target_pairs={{0,4},{1,5},{2,6},{3,7},{4,0},{5,1},{6,2},{7,3},{8,12},{9,13},{10,... | collective-permute-start | bytes 589832 | tf_op jit(solution)/shard_map/ppermute | solution.py:350
  75.7 2.2 %collective-permute-done.17.refs_8_ = f32[6,32,256]{2,1,0:T(8,128)S(1)} collective-permute-done((f32[6,32,256]{2,1,0:T(8,128)S(1)}, f32[6,32,256]{2,1,0:T(8,128)S(1)}, u32[]{:S(2)}, u32[]{:S(2)}) %collective-permute-start.17) | collective-permute-done | bytes 196640 | tf_op jit(solution)/shard_map/ppermute | solution.py:350
  80.5 2.4 %collective-permute-start.30 = (f32[864,128]{1,0:T(8,128)S(1)}, f32[864,128]{1,0:T(8,128)S(1)}, u32[]{:S(2)}, u32[]{:S(2)}) collective-permute-start(f32[864,128]{1,0:T(8,128)S(1)} %get-tuple-element.120), channel_id=1, source_target_pairs={{0,128},{16,144},{32,160},{48,176},{64,192},{80,208},{96,224},{112... | collective-permute-start | bytes 1327112 | tf_op jit(solution)/shard_map/ppermute | solution.py:350
  82.9 3.1 %first_filter.1 = (bf16[16,32,1536]{2,1,0:T(8,128)(2,1)S(1)}, bf16[16,32,1536]{2,1,0:T(8,128)(2,1)S(1)}, f32[864,128]{1,0:T(8,128)S(1)}, f32[864,128]{1,0:T(8,128)S(1)}) custom-call(s32[16]{0:T(128)S(1)} %fusion.6.refs_0_, f32[6,32,256]{2,1,0:T(8,128)S(1)} %first_grad.1.refs_1_, f32[6,32,256]{2,1,0:T(8,128)S(1)} %collective-permute-done.11.refs_2_, ...), custom_call_target="tpu_custom_call" | custom-call | flops 2038431744 | bytes 9535552 | tf_op jit(solution)/shard_map/first_filter/pallas_call | solution.py:29
  87.6 2.2 %collective-permute-start.23 = (f32[864,128]{1,0:T(8,128)S(1)}, f32[864,128]{1,0:T(8,128)S(1)}, u32[]{:S(2)}, u32[]{:S(2)}) collective-permute-start(f32[864,128]{1,0:T(8,128)S(1)} %get-tuple-element.105), channel_id=1, source_target_pairs={{0,128},{16,144},{32,160},{48,176},{64,192},{80,208},{96,224},{112... | collective-permute-start | bytes 1327112 | tf_op jit(solution)/shard_map/ppermute | solution.py:350
  89.7 2.3 %first_filter_rest.1 = (f32[864,128]{1,0:T(8,128)S(1)}, f32[864,128]{1,0:T(8,128)S(1)}) custom-call(bf16[16,32,1536]{2,1,0:T(8,128)(2,1)S(1)} %get-tuple-element.113.refs_0_.g_hi, bf16[16,32,1536]{2,1,0:T(8,128)(2,1)S(1)} %get-tuple-element.102.refs_1_.g_lo, bf16[288,2048]{1,0:T(8,128)(2,1)S(1)} %get-tuple-element.91.refs_11_.refs_2_, ...), custom_call_target="tpu_custom_call" | custom-call | flops 2038431744 | bytes 6389760 | tf_op jit(solution)/shard_map/first_filter_rest/pallas_call | solution.py:29
  93.3 1.9 %collective-permute-done.30.c = f32[864,128]{1,0:T(8,128)S(1)} collective-permute-done((f32[864,128]{1,0:T(8,128)S(1)}, f32[864,128]{1,0:T(8,128)S(1)}, u32[]{:S(2)}, u32[]{:S(2)}) %collective-permute-start.30) | collective-permute-done | bytes 442400 | tf_op jit(solution)/shard_map/ppermute | solution.py:350
  96.1 2.8 %collective-permute-start.32 = (f32[32,864]{1,0:T(8,128)S(1)}, f32[32,864]{1,0:T(8,128)S(1)}, u32[]{:S(2)}, u32[]{:S(2)}) collective-permute-start(f32[32,864]{1,0:T(8,128)S(1)} %get-tuple-element.127), channel_id=1, source_target_pairs={{0,32},{16,48},{32,0},{48,16},{64,96},{80,112},{96,64},{112,80},{1... | collective-permute-start | bytes 331784 | tf_op jit(solution)/shard_map/ppermute | solution.py:350
  98.9 5.1 %collective-permute-done.31.refs_1_ = f32[32,864]{1,0:T(8,128)S(1)} collective-permute-done((f32[32,864]{1,0:T(8,128)S(1)}, f32[32,864]{1,0:T(8,128)S(1)}, u32[]{:S(2)}, u32[]{:S(2)}) %collective-permute-start.31) | collective-permute-done | bytes 110624 | tf_op jit(solution)/shard_map/ppermute | solution.py:350
  104.8 2.3 %collective-permute-done.32.refs_2_ = f32[32,864]{1,0:T(8,128)S(1)} collective-permute-done((f32[32,864]{1,0:T(8,128)S(1)}, f32[32,864]{1,0:T(8,128)S(1)}, u32[]{:S(2)}, u32[]{:S(2)}) %collective-permute-start.32) | collective-permute-done | bytes 110624 | tf_op jit(solution)/shard_map/ppermute | solution.py:350
  109.0 6.6 %collective-permute-start.26 = (f32[1,32,256]{2,1,0:T(8,128)S(1)}, f32[1,32,256]{2,1,0:T(8,128)S(1)}, u32[]{:S(2)}, u32[]{:S(2)}) collective-permute-start(f32[1,32,256]{2,1,0:T(8,128)S(1)} %get-tuple-element.107), channel_id=1, source_target_pairs={{16,0},{32,16},{48,32},{64,48},{80,64},{96,80},{112,96},{128,112},... | collective-permute-start | bytes 98312 | tf_op jit(solution)/shard_map/ppermute | solution.py:350
  118.2 3.1 %collective-permute-start.29 = (f32[32,864]{1,0:T(8,128)S(1)}, f32[32,864]{1,0:T(8,128)S(1)}, u32[]{:S(2)}, u32[]{:S(2)}) collective-permute-start(f32[32,864]{1,0:T(8,128)S(1)} %get-tuple-element.117), channel_id=1, source_target_pairs={{0,48},{16,0},{32,16},{48,32},{64,112},{80,64},{96,80},{112,96},{1... | collective-permute-start | bytes 331784 | tf_op jit(solution)/shard_map/ppermute | solution.py:350
  121.3 5.5 %first_inner.1.own = f32[6,32,256]{2,1,0:T(8,128)S(1)} custom-call(bf16[16,32,1536]{2,1,0:T(8,128)(2,1)S(1)} %get-tuple-element.113.refs_0_.g_hi, bf16[16,32,1536]{2,1,0:T(8,128)(2,1)S(1)} %get-tuple-element.102.refs_1_.g_lo, bf16[288,512]{1,0:T(8,128)(2,1)S(1)} %get-tuple-element.94.refs_0_, bf16[288,512]{1,0:T(8,128)(2,1)S(1)} %get-tuple-element.95.refs_1_, ...), custom_call_target="tpu_custom_call" | custom-call | flops 4076863488 | bytes 5111808 | tf_op jit(solution)/shard_map/first_inner/pallas_call | solution.py:29
  (85 shorter events, 39.6 us)
Async XLA Ops:
  1.7 13.7 %collective-permute-start.3 = (f32[6,32,256]{2,1,0:T(8,128)S(1)}, f32[6,32,256]{2,1,0:T(8,128)S(1)}, u32[]{:S(2)}, u32[]{:S(2)}) collective-permute-start(f32[6,32,256]{2,1,0:T(8,128)S(1)} %fusion.5.refs_1_), channel_id=1, source_target_pairs={{0,8},{1,9},{2,10},{3,11},{4,12},{5,13},{6,14},{7,15},{8,0},{9,1},... | collective-permute-start | bytes 589832 | tf_op jit(solution)/shard_map/ppermute | solution.py:350
  9.0 17.1 %collective-permute-start.2 = (f32[6,32,256]{2,1,0:T(8,128)S(1)}, f32[6,32,256]{2,1,0:T(8,128)S(1)}, u32[]{:S(2)}, u32[]{:S(2)}) collective-permute-start(f32[6,32,256]{2,1,0:T(8,128)S(1)} %fusion.5.refs_1_), channel_id=1, source_target_pairs={{0,4},{1,5},{2,6},{3,7},{4,0},{5,1},{6,2},{7,3},{8,12},{9,13},{10,... | collective-permute-start | bytes 589832 | tf_op jit(solution)/shard_map/ppermute | solution.py:350
  12.0 9.2 %collective-permute-start.1 = (f32[6,32,256]{2,1,0:T(8,128)S(1)}, f32[6,32,256]{2,1,0:T(8,128)S(1)}, u32[]{:S(2)}, u32[]{:S(2)}) collective-permute-start(f32[6,32,256]{2,1,0:T(8,128)S(1)} %fusion.5.refs_1_), channel_id=1, source_target_pairs={{0,6},{1,7},{2,0},{3,1},{4,2},{5,3},{6,4},{7,5},{8,14},{9,15},{10,... | collective-permute-start | bytes 589832 | tf_op jit(solution)/shard_map/ppermute | solution.py:350
  21.4 13.8 %collective-permute-start.6 = (f32[6,32,256]{2,1,0:T(8,128)S(1)}, f32[6,32,256]{2,1,0:T(8,128)S(1)}, u32[]{:S(2)}, u32[]{:S(2)}) collective-permute-start(f32[6,32,256]{2,1,0:T(8,128)S(1)} %collective-permute-done.3.refs_5_), channel_id=1, source_target_pairs={{0,4},{1,5},{2,6},{3,7},{4,0},{5,1},{6,2},{7,3},{8,12},{9,13},{10,... | collective-permute-start | bytes 589832 | tf_op jit(solution)/shard_map/ppermute | solution.py:350
  24.1 10.4 %collective-permute-start.5 = (f32[6,32,256]{2,1,0:T(8,128)S(1)}, f32[6,32,256]{2,1,0:T(8,128)S(1)}, u32[]{:S(2)}, u32[]{:S(2)}) collective-permute-start(f32[6,32,256]{2,1,0:T(8,128)S(1)} %collective-permute-done.3.refs_5_), channel_id=1, source_target_pairs={{0,6},{1,7},{2,0},{3,1},{4,2},{5,3},{6,4},{7,5},{8,14},{9,15},{10,... | collective-permute-start | bytes 589832 | tf_op jit(solution)/shard_map/ppermute | solution.py:350
  27.1 11.0 %collective-permute-start.7 = (f32[24,32,256]{2,1,0:T(8,128)}, f32[24,32,256]{2,1,0:T(8,128)}, u32[]{:S(2)}, u32[]{:S(2)}) collective-permute-start(f32[24,32,256]{2,1,0:T(8,128)} %pad_maximum_fusion), channel_id=1, source_target_pairs={{0,1},{1,0},{2,3},{3,2},{4,5},{5,4},{6,7},{7,6},{8,9},{9,8},{10,11... | collective-permute-start | bytes 2359304 | tf_op jit(solution)/shard_map/ppermute | solution.py:350
  41.1 12.6 %collective-permute-start.9 = (f32[3,32,256]{2,1,0:T(8,128)S(1)}, f32[3,32,256]{2,1,0:T(8,128)S(1)}, u32[]{:S(2)}, u32[]{:S(2)}) collective-permute-start(f32[3,32,256]{2,1,0:T(8,128)S(1)} %get-tuple-element.78), channel_id=1, source_target_pairs={{0,16},{16,32},{32,48},{48,64},{64,80},{80,96},{96,112},{112,128},... | collective-permute-start | bytes 294920 | tf_op jit(solution)/shard_map/ppermute | solution.py:350
  44.1 9.7 %collective-permute-start.10 = (f32[3,32,256]{2,1,0:T(8,128)S(1)}, f32[3,32,256]{2,1,0:T(8,128)S(1)}, u32[]{:S(2)}, u32[]{:S(2)}) collective-permute-start(f32[3,32,256]{2,1,0:T(8,128)S(1)} %get-tuple-element.79), channel_id=1, source_target_pairs={{16,0},{32,16},{48,32},{64,48},{80,64},{96,80},{112,96},{128,112},... | collective-permute-start | bytes 294920 | tf_op jit(solution)/shard_map/ppermute | solution.py:350
  53.8 15.1 %collective-permute-start.14 = (f32[6,32,256]{2,1,0:T(8,128)S(1)}, f32[6,32,256]{2,1,0:T(8,128)S(1)}, u32[]{:S(2)}, u32[]{:S(2)}) collective-permute-start(f32[6,32,256]{2,1,0:T(8,128)S(1)} %first_grad.1.refs_1_), channel_id=1, source_target_pairs={{0,8},{1,9},{2,10},{3,11},{4,12},{5,13},{6,14},{7,15},{8,0},{9,1},... | collective-permute-start | bytes 589832 | tf_op jit(solution)/shard_map/ppermute | solution.py:350
  54.9 10.1 %collective-permute-start.13 = (f32[6,32,256]{2,1,0:T(8,128)S(1)}, f32[6,32,256]{2,1,0:T(8,128)S(1)}, u32[]{:S(2)}, u32[]{:S(2)}) collective-permute-start(f32[6,32,256]{2,1,0:T(8,128)S(1)} %first_grad.1.refs_1_), channel_id=1, source_target_pairs={{0,4},{1,5},{2,6},{3,7},{4,0},{5,1},{6,2},{7,3},{8,12},{9,13},{10,... | collective-permute-start | bytes 589832 | tf_op jit(solution)/shard_map/ppermute | solution.py:350
  58.2 8.5 %collective-permute-start.11 = (f32[6,32,256]{2,1,0:T(8,128)S(1)}, f32[6,32,256]{2,1,0:T(8,128)S(1)}, u32[]{:S(2)}, u32[]{:S(2)}) collective-permute-start(f32[6,32,256]{2,1,0:T(8,128)S(1)} %first_grad.1.refs_1_), channel_id=1, source_target_pairs={{0,2},{1,3},{2,4},{3,5},{4,6},{5,7},{6,0},{7,1},{8,10},{9,11},{10,... | collective-permute-start | bytes 589832 | tf_op jit(solution)/shard_map/ppermute | solution.py:350
  66.8 13.6 %collective-permute-start.19 = (f32[864,128]{1,0:T(8,128)S(1)}, f32[864,128]{1,0:T(8,128)S(1)}, u32[]{:S(2)}, u32[]{:S(2)}) collective-permute-start(f32[864,128]{1,0:T(8,128)S(1)} %get-tuple-element.88), channel_id=1, source_target_pairs={{0,64},{16,80},{32,96},{48,112},{64,128},{80,144},{96,160},{112,17... | collective-permute-start | bytes 1327112 | tf_op jit(solution)/shard_map/ppermute | solution.py:350
  68.5 12.0 %collective-permute-start.20 = (f32[864,128]{1,0:T(8,128)S(1)}, f32[864,128]{1,0:T(8,128)S(1)}, u32[]{:S(2)}, u32[]{:S(2)}) collective-permute-start(f32[864,128]{1,0:T(8,128)S(1)} %get-tuple-element.89), channel_id=1, source_target_pairs={{0,192},{16,208},{32,224},{48,240},{64,0},{80,16},{96,32},{112,48}... | collective-permute-start | bytes 1327112 | tf_op jit(solution)/shard_map/ppermute | solution.py:350
  68.9 8.9 %collective-permute-start.17 = (f32[6,32,256]{2,1,0:T(8,128)S(1)}, f32[6,32,256]{2,1,0:T(8,128)S(1)}, u32[]{:S(2)}, u32[]{:S(2)}) collective-permute-start(f32[6,32,256]{2,1,0:T(8,128)S(1)} %collective-permute-done.14.refs_5_), channel_id=1, source_target_pairs={{0,4},{1,5},{2,6},{3,7},{4,0},{5,1},{6,2},{7,3},{8,12},{9,13},{10,... | collective-permute-start | bytes 589832 | tf_op jit(solution)/shard_map/ppermute | solution.py:350
  80.5 14.7 %collective-permute-start.30 = (f32[864,128]{1,0:T(8,128)S(1)}, f32[864,128]{1,0:T(8,128)S(1)}, u32[]{:S(2)}, u32[]{:S(2)}) collective-permute-start(f32[864,128]{1,0:T(8,128)S(1)} %get-tuple-element.120), channel_id=1, source_target_pairs={{0,128},{16,144},{32,160},{48,176},{64,192},{80,208},{96,224},{112... | collective-permute-start | bytes 1327112 | tf_op jit(solution)/shard_map/ppermute | solution.py:350
  86.0 30.6 %collective-permute-start.22 = (f32[864,128]{1,0:T(8,128)S(1)}, f32[864,128]{1,0:T(8,128)S(1)}, u32[]{:S(2)}, u32[]{:S(2)}) collective-permute-start(f32[864,128]{1,0:T(8,128)S(1)} %get-tuple-element.104), channel_id=1, source_target_pairs={{0,64},{16,80},{32,96},{48,112},{64,128},{80,144},{96,160},{112,17... | collective-permute-start | bytes 1327112 | tf_op jit(solution)/shard_map/ppermute | solution.py:350
  87.6 29.0 %collective-permute-start.23 = (f32[864,128]{1,0:T(8,128)S(1)}, f32[864,128]{1,0:T(8,128)S(1)}, u32[]{:S(2)}, u32[]{:S(2)}) collective-permute-start(f32[864,128]{1,0:T(8,128)S(1)} %get-tuple-element.105), channel_id=1, source_target_pairs={{0,128},{16,144},{32,160},{48,176},{64,192},{80,208},{96,224},{112... | collective-permute-start | bytes 1327112 | tf_op jit(solution)/shard_map/ppermute | solution.py:350
  92.0 24.6 %collective-permute-start.24 = (f32[864,128]{1,0:T(8,128)S(1)}, f32[864,128]{1,0:T(8,128)S(1)}, u32[]{:S(2)}, u32[]{:S(2)}) collective-permute-start(f32[864,128]{1,0:T(8,128)S(1)} %get-tuple-element.106), channel_id=1, source_target_pairs={{0,192},{16,208},{32,224},{48,240},{64,0},{80,16},{96,32},{112,48}... | collective-permute-start | bytes 1327112 | tf_op jit(solution)/shard_map/ppermute | solution.py:350
  96.1 11.0 %collective-permute-start.32 = (f32[32,864]{1,0:T(8,128)S(1)}, f32[32,864]{1,0:T(8,128)S(1)}, u32[]{:S(2)}, u32[]{:S(2)}) collective-permute-start(f32[32,864]{1,0:T(8,128)S(1)} %get-tuple-element.127), channel_id=1, source_target_pairs={{0,32},{16,48},{32,0},{48,16},{64,96},{80,112},{96,64},{112,80},{1... | collective-permute-start | bytes 331784 | tf_op jit(solution)/shard_map/ppermute | solution.py:350
  107.1 19.7 %collective-permute-start.25 = (f32[1,32,256]{2,1,0:T(8,128)S(1)}, f32[1,32,256]{2,1,0:T(8,128)S(1)}, u32[]{:S(2)}, u32[]{:S(2)}) collective-permute-start(f32[1,32,256]{2,1,0:T(8,128)S(1)} %get-tuple-element.114), channel_id=1, source_target_pairs={{0,16},{16,32},{32,48},{48,64},{64,80},{80,96},{96,112},{112,128},... | collective-permute-start | bytes 98312 | tf_op jit(solution)/shard_map/ppermute | solution.py:350
  109.0 17.8 %collective-permute-start.26 = (f32[1,32,256]{2,1,0:T(8,128)S(1)}, f32[1,32,256]{2,1,0:T(8,128)S(1)}, u32[]{:S(2)}, u32[]{:S(2)}) collective-permute-start(f32[1,32,256]{2,1,0:T(8,128)S(1)} %get-tuple-element.107), channel_id=1, source_target_pairs={{16,0},{32,16},{48,32},{64,48},{80,64},{96,80},{112,96},{128,112},... | collective-permute-start | bytes 98312 | tf_op jit(solution)/shard_map/ppermute | solution.py:350
  117.4 10.1 %collective-permute-start.27 = (f32[32,864]{1,0:T(8,128)S(1)}, f32[32,864]{1,0:T(8,128)S(1)}, u32[]{:S(2)}, u32[]{:S(2)}) collective-permute-start(f32[32,864]{1,0:T(8,128)S(1)} %get-tuple-element.115), channel_id=1, source_target_pairs={{0,16},{16,32},{32,48},{48,0},{64,80},{80,96},{96,112},{112,64},{1... | collective-permute-start | bytes 331784 | tf_op jit(solution)/shard_map/ppermute | solution.py:350
  117.5 10.1 %collective-permute-start.28 = (f32[32,864]{1,0:T(8,128)S(1)}, f32[32,864]{1,0:T(8,128)S(1)}, u32[]{:S(2)}, u32[]{:S(2)}) collective-permute-start(f32[32,864]{1,0:T(8,128)S(1)} %get-tuple-element.116), channel_id=1, source_target_pairs={{0,32},{16,48},{32,0},{48,16},{64,96},{80,112},{96,64},{112,80},{1... | collective-permute-start | bytes 331784 | tf_op jit(solution)/shard_map/ppermute | solution.py:350
  118.2 9.3 %collective-permute-start.29 = (f32[32,864]{1,0:T(8,128)S(1)}, f32[32,864]{1,0:T(8,128)S(1)}, u32[]{:S(2)}, u32[]{:S(2)}) collective-permute-start(f32[32,864]{1,0:T(8,128)S(1)} %get-tuple-element.117), channel_id=1, source_target_pairs={{0,48},{16,0},{32,16},{48,32},{64,112},{80,64},{96,80},{112,96},{1... | collective-permute-start | bytes 331784 | tf_op jit(solution)/shard_map/ppermute | solution.py:350
  (15 other events, 127.7 us)

commit v6 on v5

--- a/solution.py
+++ b/solution.py
@@ -434,16 +434,17 @@
     part_3, part_0 = filter_quarters((3, 0), halves, inputs, flops // 2, "first_filter_rest")
     first_rows = [part_0, row_1, row_2, to_row(part_3, 3)]
 
-    second_rows = lax.optimization_barrier((*second_rows, part_0))[:4]
+    before, behind = call(first_outer_kernel, [shape(1, channels, area)] * 2, [],
+                          [after(halves[0], [part_0]), halves[1], *w1[:2], *w1[4:]], 0, flops // 9, "first_outer")
+    before, behind = edges(before, behind)
+    second_rows = lax.optimization_barrier((*second_rows, part_0, before, behind))[:4]
     second_rows = turned_sum(z_spots, second_rows)
-    before, behind = call(first_outer_kernel, [shape(1, channels, area)] * 2, [],
-                          [*halves, *w1[:2], *w1[4:]], 0, flops // 9, "first_outer")
-    first_rows = lax.optimization_barrier((*first_rows, before))[:4]
+    first_rows = lax.optimization_barrier((*first_rows, second_rows[0]))[:4]
     first_rows = turned_sum(z_spots, first_rows)
-    own = inner([after(halves[0], [first_rows[0]]), halves[1]], w1, planes, flops, "first_inner")
-    second_weights = last_sum(to_owners(second_rows), scale)
+    own = inner([after(halves[0], [first_rows[0]]), halves[1]], w1, planes, flops, "first_inner", True)
+    second_rows = lax.optimization_barrier((*to_owners(second_rows), first_rows[0]))[:4]
+    second_weights = last_sum(second_rows, scale)
     first_weights = last_sum(to_owners(first_rows), scale)
-    before, behind = edges(before, behind)
     input_grad = call(input_kernel, shape(planes, channels, area), [], [own, before, behind], name="input_grad")
     return (jnp.transpose(input_grad, (1, 0, 2)), first_weights.reshape(taps, channels, -1),
             second_weights.reshape(taps, channels, -1))

time: 129 us -> 129 us (level)
  starting transfers between devices: 60 us -> 62.3 us
  waiting for transfers between devices: 28.2 us -> 26.2 us
  Pallas kernels: 32 us -> 30.5 us
    ppermute x34, starting transfers between devices: 60 us -> 62.3 us  [send(): return lax.ppermute(value, axis, moves)]
    ppermute x34, waiting for transfers between devices: 28.2 us -> 26.2 us  [send(): return lax.ppermute(value, axis, moves)]
    pallas_call x17, Pallas kernels: 32 us -> 30.5 us  [call(): pl.pallas_call(kernel, out_shape=out_shape, in_specs=[SM] * n_smem + [VM]...]
  transfers between devices with their start and end apart: 34 -> 34, of which waited for: 12 -> 12; matrix products, arithmetic and copies ran while one was open for 4% -> 4% of each run, Pallas kernels for 22% -> 21%
where the time goes in v6:
time: 129 us; the launch traced here: 127 us
  starting transfers between devices  62.3 us (48%)
  Pallas kernels  30.5 us (24%)
  waiting for transfers between devices  26.2 us (20%)
  local copies, waits for them, and re-layouts  4.49 us (3%)
  other arithmetic  2.84 us (2%)
    ppermute x34, starting transfers between devices, send(): return lax.ppermute(value, axis, moves)  62.3 us
    pallas_call x17, Pallas kernels, call(): pl.pallas_call(kernel, out_shape=out_shape, in_specs=[SM] * n_smem + [VM]...  30.5 us
    ppermute x34, waiting for transfers between devices, send(): return lax.ppermute(value, axis, moves)  26.2 us
    unnamed x13, local copies, waits for them, and re-layouts  2.92 us
  transfers between devices with their start and end apart: 34, of which 12 were waited for; matrix products, arithmetic and copies ran while one was open for 4% of the time, Pallas kernels for 21%

profile of v6, /device:TPU:8, one launch (start us, length us, event | category | flops | bytes accessed | tf_op | source)
XLA Modules:
  0.0 127.3 jit_solution(10584409570163293454)
XLA Ops:
  1.7 7.3 %collective-permute-start.3 = (f32[6,32,256]{2,1,0:T(8,128)S(1)}, f32[6,32,256]{2,1,0:T(8,128)S(1)}, u32[]{:S(2)}, u32[]{:S(2)}) collective-permute-start(f32[6,32,256]{2,1,0:T(8,128)S(1)} %fusion.5.refs_1_), channel_id=1, source_target_pairs={{0,8},{1,9},{2,10},{3,11},{4,12},{5,13},{6,14},{7,15},{8,0},{9,1},... | collective-permute-start | bytes 589832 | tf_op jit(solution)/shard_map/ppermute | solution.py:350
  9.0 3.0 %collective-permute-start.2 = (f32[6,32,256]{2,1,0:T(8,128)S(1)}, f32[6,32,256]{2,1,0:T(8,128)S(1)}, u32[]{:S(2)}, u32[]{:S(2)}) collective-permute-start(f32[6,32,256]{2,1,0:T(8,128)S(1)} %fusion.5.refs_1_), channel_id=1, source_target_pairs={{0,4},{1,5},{2,6},{3,7},{4,0},{5,1},{6,2},{7,3},{8,12},{9,13},{10,... | collective-permute-start | bytes 589832 | tf_op jit(solution)/shard_map/ppermute | solution.py:350
  15.5 5.7 %collective-permute-done.1.refs_3_ = f32[6,32,256]{2,1,0:T(8,128)S(1)} collective-permute-done((f32[6,32,256]{2,1,0:T(8,128)S(1)}, f32[6,32,256]{2,1,0:T(8,128)S(1)}, u32[]{:S(2)}, u32[]{:S(2)}) %collective-permute-start.1) | collective-permute-done | bytes 196640 | tf_op jit(solution)/shard_map/ppermute | solution.py:350
  21.4 2.7 %collective-permute-start.6 = (f32[6,32,256]{2,1,0:T(8,128)S(1)}, f32[6,32,256]{2,1,0:T(8,128)S(1)}, u32[]{:S(2)}, u32[]{:S(2)}) collective-permute-start(f32[6,32,256]{2,1,0:T(8,128)S(1)} %collective-permute-done.3.refs_5_), channel_id=1, source_target_pairs={{0,4},{1,5},{2,6},{3,7},{4,0},{5,1},{6,2},{7,3},{8,12},{9,13},{10,... | collective-permute-start | bytes 589832 | tf_op jit(solution)/shard_map/ppermute | solution.py:350
  27.8 6.0 %collective-permute-done.4.refs_6_ = f32[6,32,256]{2,1,0:T(8,128)S(1)} collective-permute-done((f32[6,32,256]{2,1,0:T(8,128)S(1)}, f32[6,32,256]{2,1,0:T(8,128)S(1)}, u32[]{:S(2)}, u32[]{:S(2)}) %collective-permute-start.4) | collective-permute-done | bytes 196640 | tf_op jit(solution)/shard_map/ppermute | solution.py:350
  38.5 2.6 %second_outer.1 = (bf16[16,32,1536]{2,1,0:T(8,128)(2,1)S(1)}, bf16[16,32,1536]{2,1,0:T(8,128)(2,1)S(1)}, f32[3,32,256]{2,1,0:T(8,128)S(1)}, f32[3,32,256]{2,1,0:T(8,128)S(1)}) custom-call(s32[16]{0:T(128)S(1)} %fusion.6.refs_0_, f32[6,32,256]{2,1,0:T(8,128)S(1)} %fusion.5.refs_1_, f32[6,32,256]{2,1,0:T(8,128)S(1)} %collective-permute-done.refs_2_, ...), custom_call_target="tpu_custom_call" | custom-call | flops 452984832 | bytes 7798848 | tf_op jit(solution)/shard_map/second_outer/pallas_call | solution.py:29
  41.1 2.9 %collective-permute-start.9 = (f32[3,32,256]{2,1,0:T(8,128)S(1)}, f32[3,32,256]{2,1,0:T(8,128)S(1)}, u32[]{:S(2)}, u32[]{:S(2)}) collective-permute-start(f32[3,32,256]{2,1,0:T(8,128)S(1)} %get-tuple-element.83), channel_id=1, source_target_pairs={{0,16},{16,32},{32,48},{48,64},{64,80},{80,96},{96,112},{112,128},... | collective-permute-start | bytes 294920 | tf_op jit(solution)/shard_map/ppermute | solution.py:350
  44.1 5.6 %collective-permute-start.10 = (f32[3,32,256]{2,1,0:T(8,128)S(1)}, f32[3,32,256]{2,1,0:T(8,128)S(1)}, u32[]{:S(2)}, u32[]{:S(2)}) collective-permute-start(f32[3,32,256]{2,1,0:T(8,128)S(1)} %get-tuple-element.84), channel_id=1, source_target_pairs={{16,0},{32,16},{48,32},{64,48},{80,64},{96,80},{112,96},{128,112},... | collective-permute-start | bytes 294920 | tf_op jit(solution)/shard_map/ppermute | solution.py:350
  49.7 4.0 %second_inner.1.own = f32[6,32,256]{2,1,0:T(8,128)S(1)} custom-call(bf16[16,32,1536]{2,1,0:T(8,128)(2,1)S(1)} %get-tuple-element.79.g_hi.refs_0_, bf16[16,32,1536]{2,1,0:T(8,128)(2,1)S(1)} %get-tuple-element.80.g_lo.refs_1_, bf16[288,512]{1,0:T(8,128)(2,1)S(1)} %get-tuple-element.75.refs_12_.refs_0_, ...), custom_call_target="tpu_custom_call" | custom-call | flops 4076863488 | bytes 5111808 | tf_op jit(solution)/shard_map/second_inner/pallas_call | solution.py:29
  54.9 2.2 %collective-permute-start.13 = (f32[6,32,256]{2,1,0:T(8,128)S(1)}, f32[6,32,256]{2,1,0:T(8,128)S(1)}, u32[]{:S(2)}, u32[]{:S(2)}) collective-permute-start(f32[6,32,256]{2,1,0:T(8,128)S(1)} %first_grad.1.refs_1_), channel_id=1, source_target_pairs={{0,4},{1,5},{2,6},{3,7},{4,0},{5,1},{6,2},{7,3},{8,12},{9,13},{10,... | collective-permute-start | bytes 589832 | tf_op jit(solution)/shard_map/ppermute | solution.py:350
  60.7 4.3 %second_filter.1 = (f32[864,128]{1,0:T(8,128)S(1)}, f32[864,128]{1,0:T(8,128)S(1)}, f32[864,128]{1,0:T(8,128)S(1)}, f32[864,128]{1,0:T(8,128)S(1)}) custom-call(bf16[16,32,1536]{2,1,0:T(8,128)(2,1)S(1)} %get-tuple-element.79.g_hi.refs_0_, bf16[16,32,1536]{2,1,0:T(8,128)(2,1)S(1)} %get-tuple-element.80.g_lo.refs_1_, ...), custom_call_target="tpu_custom_call" | custom-call | flops 4076863488 | bytes 7274496 | tf_op jit(solution)/shard_map/second_filter/pallas_call | solution.py:29
  68.9 2.1 %collective-permute-start.17 = (f32[6,32,256]{2,1,0:T(8,128)S(1)}, f32[6,32,256]{2,1,0:T(8,128)S(1)}, u32[]{:S(2)}, u32[]{:S(2)}) collective-permute-start(f32[6,32,256]{2,1,0:T(8,128)S(1)} %collective-permute-done.14.refs_5_), channel_id=1, source_target_pairs={{0,4},{1,5},{2,6},{3,7},{4,0},{5,1},{6,2},{7,3},{8,12},{9,13},{10,... | collective-permute-start | bytes 589832 | tf_op jit(solution)/shard_map/ppermute | solution.py:350
  75.7 2.2 %collective-permute-done.17.refs_8_ = f32[6,32,256]{2,1,0:T(8,128)S(1)} collective-permute-done((f32[6,32,256]{2,1,0:T(8,128)S(1)}, f32[6,32,256]{2,1,0:T(8,128)S(1)}, u32[]{:S(2)}, u32[]{:S(2)}) %collective-permute-start.17) | collective-permute-done | bytes 196640 | tf_op jit(solution)/shard_map/ppermute | solution.py:350
  80.5 2.4 %collective-permute-start.25 = (f32[864,128]{1,0:T(8,128)S(1)}, f32[864,128]{1,0:T(8,128)S(1)}, u32[]{:S(2)}, u32[]{:S(2)}) collective-permute-start(f32[864,128]{1,0:T(8,128)S(1)} %get-tuple-element.114), channel_id=1, source_target_pairs={{0,128},{16,144},{32,160},{48,176},{64,192},{80,208},{96,224},{112... | collective-permute-start | bytes 1327112 | tf_op jit(solution)/shard_map/ppermute | solution.py:350
  82.9 3.1 %first_filter.1 = (bf16[16,32,1536]{2,1,0:T(8,128)(2,1)S(1)}, bf16[16,32,1536]{2,1,0:T(8,128)(2,1)S(1)}, f32[864,128]{1,0:T(8,128)S(1)}, f32[864,128]{1,0:T(8,128)S(1)}) custom-call(s32[16]{0:T(128)S(1)} %fusion.6.refs_0_, f32[6,32,256]{2,1,0:T(8,128)S(1)} %first_grad.1.refs_1_, f32[6,32,256]{2,1,0:T(8,128)S(1)} %collective-permute-done.11.refs_2_, ...), custom_call_target="tpu_custom_call" | custom-call | flops 2038431744 | bytes 9535552 | tf_op jit(solution)/shard_map/first_filter/pallas_call | solution.py:29
  87.6 2.1 %collective-permute-start.23 = (f32[864,128]{1,0:T(8,128)S(1)}, f32[864,128]{1,0:T(8,128)S(1)}, u32[]{:S(2)}, u32[]{:S(2)}) collective-permute-start(f32[864,128]{1,0:T(8,128)S(1)} %get-tuple-element.110), channel_id=1, source_target_pairs={{0,128},{16,144},{32,160},{48,176},{64,192},{80,208},{96,224},{112... | collective-permute-start | bytes 1327112 | tf_op jit(solution)/shard_map/ppermute | solution.py:350
  89.7 2.2 %first_filter_rest.1 = (f32[864,128]{1,0:T(8,128)S(1)}, f32[864,128]{1,0:T(8,128)S(1)}) custom-call(bf16[16,32,1536]{2,1,0:T(8,128)(2,1)S(1)} %get-tuple-element.128.refs_0_.g_hi, bf16[16,32,1536]{2,1,0:T(8,128)(2,1)S(1)} %get-tuple-element.107.refs_1_.g_lo, bf16[288,2048]{1,0:T(8,128)(2,1)S(1)} %get-tuple-element.96.refs_11_.refs_2_, ...), custom_call_target="tpu_custom_call" | custom-call | flops 2038431744 | bytes 6389760 | tf_op jit(solution)/shard_map/first_filter_rest/pallas_call | solution.py:29
  94.1 1.9 %collective-permute-start.26 = (f32[1,32,256]{2,1,0:T(8,128)S(1)}, f32[1,32,256]{2,1,0:T(8,128)S(1)}, u32[]{:S(2)}, u32[]{:S(2)}) collective-permute-start(f32[1,32,256]{2,1,0:T(8,128)S(1)} %get-tuple-element.116), channel_id=1, source_target_pairs={{0,16},{16,32},{32,48},{48,64},{64,80},{80,96},{96,112},{112,128},... | collective-permute-start | bytes 98312 | tf_op jit(solution)/shard_map/ppermute | solution.py:350
  96.0 6.6 %collective-permute-start.27 = (f32[1,32,256]{2,1,0:T(8,128)S(1)}, f32[1,32,256]{2,1,0:T(8,128)S(1)}, u32[]{:S(2)}, u32[]{:S(2)}) collective-permute-start(f32[1,32,256]{2,1,0:T(8,128)S(1)} %get-tuple-element.117), channel_id=1, source_target_pairs={{16,0},{32,16},{48,32},{64,48},{80,64},{96,80},{112,96},{128,112},... | collective-permute-start | bytes 98312 | tf_op jit(solution)/shard_map/ppermute | solution.py:350
  105.3 5.1 %collective-permute-start.32 = (f32[32,864]{1,0:T(8,128)S(1)}, f32[32,864]{1,0:T(8,128)S(1)}, u32[]{:S(2)}, u32[]{:S(2)}) collective-permute-start(f32[32,864]{1,0:T(8,128)S(1)} %get-tuple-element.133), channel_id=1, source_target_pairs={{0,32},{16,48},{32,0},{48,16},{64,96},{80,112},{96,64},{112,80},{1... | collective-permute-start | bytes 331784 | tf_op jit(solution)/shard_map/ppermute | solution.py:350
  110.4 3.2 %collective-permute-done.24.d = f32[864,128]{1,0:T(8,128)S(1)} collective-permute-done((f32[864,128]{1,0:T(8,128)S(1)}, f32[864,128]{1,0:T(8,128)S(1)}, u32[]{:S(2)}, u32[]{:S(2)}) %collective-permute-start.24) | collective-permute-done | bytes 442400 | tf_op jit(solution)/shard_map/ppermute | solution.py:350
  114.5 3.5 %collective-permute-start.29 = (f32[32,864]{1,0:T(8,128)S(1)}, f32[32,864]{1,0:T(8,128)S(1)}, u32[]{:S(2)}, u32[]{:S(2)}) collective-permute-start(f32[32,864]{1,0:T(8,128)S(1)} %get-tuple-element.130), channel_id=1, source_target_pairs={{0,32},{16,48},{32,0},{48,16},{64,96},{80,112},{96,64},{112,80},{1... | collective-permute-start | bytes 331784 | tf_op jit(solution)/shard_map/ppermute | solution.py:350
  118.3 4.0 %first_inner.1.own = f32[6,32,256]{2,1,0:T(8,128)S(1)} custom-call(bf16[16,32,1536]{2,1,0:T(8,128)(2,1)S(1)} %get-tuple-element.128.refs_0_.g_hi, bf16[16,32,1536]{2,1,0:T(8,128)(2,1)S(1)} %get-tuple-element.107.refs_1_.g_lo, bf16[288,512]{1,0:T(8,128)(2,1)S(1)} %get-tuple-element.99.refs_0_, bf16[288,512]{1,0:T(8,128)(2,1)S(1)} %get-tuple-element.100.refs_1_, ...), custom_call_target="tpu_custom_call" | custom-call | flops 4076863488 | bytes 5111808 | tf_op jit(solution)/shard_map/first_inner/pallas_call | solution.py:29
  124.0 2.3 %collective-permute-done.29.refs_2_ = f32[32,864]{1,0:T(8,128)S(1)} collective-permute-done((f32[32,864]{1,0:T(8,128)S(1)}, f32[32,864]{1,0:T(8,128)S(1)}, u32[]{:S(2)}, u32[]{:S(2)}) %collective-permute-start.29) | collective-permute-done | bytes 110624 | tf_op jit(solution)/shard_map/ppermute | solution.py:350
  (85 shorter events, 39.0 us)
Async XLA Ops:
  1.7 13.7 %collective-permute-start.3 = (f32[6,32,256]{2,1,0:T(8,128)S(1)}, f32[6,32,256]{2,1,0:T(8,128)S(1)}, u32[]{:S(2)}, u32[]{:S(2)}) collective-permute-start(f32[6,32,256]{2,1,0:T(8,128)S(1)} %fusion.5.refs_1_), channel_id=1, source_target_pairs={{0,8},{1,9},{2,10},{3,11},{4,12},{5,13},{6,14},{7,15},{8,0},{9,1},... | collective-permute-start | bytes 589832 | tf_op jit(solution)/shard_map/ppermute | solution.py:350
  9.0 17.1 %collective-permute-start.2 = (f32[6,32,256]{2,1,0:T(8,128)S(1)}, f32[6,32,256]{2,1,0:T(8,128)S(1)}, u32[]{:S(2)}, u32[]{:S(2)}) collective-permute-start(f32[6,32,256]{2,1,0:T(8,128)S(1)} %fusion.5.refs_1_), channel_id=1, source_target_pairs={{0,4},{1,5},{2,6},{3,7},{4,0},{5,1},{6,2},{7,3},{8,12},{9,13},{10,... | collective-permute-start | bytes 589832 | tf_op jit(solution)/shard_map/ppermute | solution.py:350
  12.0 9.2 %collective-permute-start.1 = (f32[6,32,256]{2,1,0:T(8,128)S(1)}, f32[6,32,256]{2,1,0:T(8,128)S(1)}, u32[]{:S(2)}, u32[]{:S(2)}) collective-permute-start(f32[6,32,256]{2,1,0:T(8,128)S(1)} %fusion.5.refs_1_), channel_id=1, source_target_pairs={{0,6},{1,7},{2,0},{3,1},{4,2},{5,3},{6,4},{7,5},{8,14},{9,15},{10,... | collective-permute-start | bytes 589832 | tf_op jit(solution)/shard_map/ppermute | solution.py:350
  21.4 13.8 %collective-permute-start.6 = (f32[6,32,256]{2,1,0:T(8,128)S(1)}, f32[6,32,256]{2,1,0:T(8,128)S(1)}, u32[]{:S(2)}, u32[]{:S(2)}) collective-permute-start(f32[6,32,256]{2,1,0:T(8,128)S(1)} %collective-permute-done.3.refs_5_), channel_id=1, source_target_pairs={{0,4},{1,5},{2,6},{3,7},{4,0},{5,1},{6,2},{7,3},{8,12},{9,13},{10,... | collective-permute-start | bytes 589832 | tf_op jit(solution)/shard_map/ppermute | solution.py:350
  24.1 10.4 %collective-permute-start.5 = (f32[6,32,256]{2,1,0:T(8,128)S(1)}, f32[6,32,256]{2,1,0:T(8,128)S(1)}, u32[]{:S(2)}, u32[]{:S(2)}) collective-permute-start(f32[6,32,256]{2,1,0:T(8,128)S(1)} %collective-permute-done.3.refs_5_), channel_id=1, source_target_pairs={{0,6},{1,7},{2,0},{3,1},{4,2},{5,3},{6,4},{7,5},{8,14},{9,15},{10,... | collective-permute-start | bytes 589832 | tf_op jit(solution)/shard_map/ppermute | solution.py:350
  27.1 11.0 %collective-permute-start.7 = (f32[24,32,256]{2,1,0:T(8,128)}, f32[24,32,256]{2,1,0:T(8,128)}, u32[]{:S(2)}, u32[]{:S(2)}) collective-permute-start(f32[24,32,256]{2,1,0:T(8,128)} %pad_maximum_fusion), channel_id=1, source_target_pairs={{0,1},{1,0},{2,3},{3,2},{4,5},{5,4},{6,7},{7,6},{8,9},{9,8},{10,11... | collective-permute-start | bytes 2359304 | tf_op jit(solution)/shard_map/ppermute | solution.py:350
  41.1 12.6 %collective-permute-start.9 = (f32[3,32,256]{2,1,0:T(8,128)S(1)}, f32[3,32,256]{2,1,0:T(8,128)S(1)}, u32[]{:S(2)}, u32[]{:S(2)}) collective-permute-start(f32[3,32,256]{2,1,0:T(8,128)S(1)} %get-tuple-element.83), channel_id=1, source_target_pairs={{0,16},{16,32},{32,48},{48,64},{64,80},{80,96},{96,112},{112,128},... | collective-permute-start | bytes 294920 | tf_op jit(solution)/shard_map/ppermute | solution.py:350
  44.1 9.7 %collective-permute-start.10 = (f32[3,32,256]{2,1,0:T(8,128)S(1)}, f32[3,32,256]{2,1,0:T(8,128)S(1)}, u32[]{:S(2)}, u32[]{:S(2)}) collective-permute-start(f32[3,32,256]{2,1,0:T(8,128)S(1)} %get-tuple-element.84), channel_id=1, source_target_pairs={{16,0},{32,16},{48,32},{64,48},{80,64},{96,80},{112,96},{128,112},... | collective-permute-start | bytes 294920 | tf_op jit(solution)/shard_map/ppermute | solution.py:350
  53.8 15.2 %collective-permute-start.14 = (f32[6,32,256]{2,1,0:T(8,128)S(1)}, f32[6,32,256]{2,1,0:T(8,128)S(1)}, u32[]{:S(2)}, u32[]{:S(2)}) collective-permute-start(f32[6,32,256]{2,1,0:T(8,128)S(1)} %first_grad.1.refs_1_), channel_id=1, source_target_pairs={{0,8},{1,9},{2,10},{3,11},{4,12},{5,13},{6,14},{7,15},{8,0},{9,1},... | collective-permute-start | bytes 589832 | tf_op jit(solution)/shard_map/ppermute | solution.py:350
  54.9 10.1 %collective-permute-start.13 = (f32[6,32,256]{2,1,0:T(8,128)S(1)}, f32[6,32,256]{2,1,0:T(8,128)S(1)}, u32[]{:S(2)}, u32[]{:S(2)}) collective-permute-start(f32[6,32,256]{2,1,0:T(8,128)S(1)} %first_grad.1.refs_1_), channel_id=1, source_target_pairs={{0,4},{1,5},{2,6},{3,7},{4,0},{5,1},{6,2},{7,3},{8,12},{9,13},{10,... | collective-permute-start | bytes 589832 | tf_op jit(solution)/shard_map/ppermute | solution.py:350
  58.2 8.5 %collective-permute-start.11 = (f32[6,32,256]{2,1,0:T(8,128)S(1)}, f32[6,32,256]{2,1,0:T(8,128)S(1)}, u32[]{:S(2)}, u32[]{:S(2)}) collective-permute-start(f32[6,32,256]{2,1,0:T(8,128)S(1)} %first_grad.1.refs_1_), channel_id=1, source_target_pairs={{0,2},{1,3},{2,4},{3,5},{4,6},{5,7},{6,0},{7,1},{8,10},{9,11},{10,... | collective-permute-start | bytes 589832 | tf_op jit(solution)/shard_map/ppermute | solution.py:350
  66.8 13.6 %collective-permute-start.19 = (f32[864,128]{1,0:T(8,128)S(1)}, f32[864,128]{1,0:T(8,128)S(1)}, u32[]{:S(2)}, u32[]{:S(2)}) collective-permute-start(f32[864,128]{1,0:T(8,128)S(1)} %get-tuple-element.93), channel_id=1, source_target_pairs={{0,64},{16,80},{32,96},{48,112},{64,128},{80,144},{96,160},{112,17... | collective-permute-start | bytes 1327112 | tf_op jit(solution)/shard_map/ppermute | solution.py:350
  68.5 12.0 %collective-permute-start.20 = (f32[864,128]{1,0:T(8,128)S(1)}, f32[864,128]{1,0:T(8,128)S(1)}, u32[]{:S(2)}, u32[]{:S(2)}) collective-permute-start(f32[864,128]{1,0:T(8,128)S(1)} %get-tuple-element.94), channel_id=1, source_target_pairs={{0,192},{16,208},{32,224},{48,240},{64,0},{80,16},{96,32},{112,48}... | collective-permute-start | bytes 1327112 | tf_op jit(solution)/shard_map/ppermute | solution.py:350
  68.9 8.9 %collective-permute-start.17 = (f32[6,32,256]{2,1,0:T(8,128)S(1)}, f32[6,32,256]{2,1,0:T(8,128)S(1)}, u32[]{:S(2)}, u32[]{:S(2)}) collective-permute-start(f32[6,32,256]{2,1,0:T(8,128)S(1)} %collective-permute-done.14.refs_5_), channel_id=1, source_target_pairs={{0,4},{1,5},{2,6},{3,7},{4,0},{5,1},{6,2},{7,3},{8,12},{9,13},{10,... | collective-permute-start | bytes 589832 | tf_op jit(solution)/shard_map/ppermute | solution.py:350
  80.5 15.4 %collective-permute-start.25 = (f32[864,128]{1,0:T(8,128)S(1)}, f32[864,128]{1,0:T(8,128)S(1)}, u32[]{:S(2)}, u32[]{:S(2)}) collective-permute-start(f32[864,128]{1,0:T(8,128)S(1)} %get-tuple-element.114), channel_id=1, source_target_pairs={{0,128},{16,144},{32,160},{48,176},{64,192},{80,208},{96,224},{112... | collective-permute-start | bytes 1327112 | tf_op jit(solution)/shard_map/ppermute | solution.py:350
  86.0 24.4 %collective-permute-start.22 = (f32[864,128]{1,0:T(8,128)S(1)}, f32[864,128]{1,0:T(8,128)S(1)}, u32[]{:S(2)}, u32[]{:S(2)}) collective-permute-start(f32[864,128]{1,0:T(8,128)S(1)} %get-tuple-element.109), channel_id=1, source_target_pairs={{0,64},{16,80},{32,96},{48,112},{64,128},{80,144},{96,160},{112,17... | collective-permute-start | bytes 1327112 | tf_op jit(solution)/shard_map/ppermute | solution.py:350
  87.6 22.8 %collective-permute-start.23 = (f32[864,128]{1,0:T(8,128)S(1)}, f32[864,128]{1,0:T(8,128)S(1)}, u32[]{:S(2)}, u32[]{:S(2)}) collective-permute-start(f32[864,128]{1,0:T(8,128)S(1)} %get-tuple-element.110), channel_id=1, source_target_pairs={{0,128},{16,144},{32,160},{48,176},{64,192},{80,208},{96,224},{112... | collective-permute-start | bytes 1327112 | tf_op jit(solution)/shard_map/ppermute | solution.py:350
  92.0 21.6 %collective-permute-start.24 = (f32[864,128]{1,0:T(8,128)S(1)}, f32[864,128]{1,0:T(8,128)S(1)}, u32[]{:S(2)}, u32[]{:S(2)}) collective-permute-start(f32[864,128]{1,0:T(8,128)S(1)} %get-tuple-element.111), channel_id=1, source_target_pairs={{0,192},{16,208},{32,224},{48,240},{64,0},{80,16},{96,32},{112,48}... | collective-permute-start | bytes 1327112 | tf_op jit(solution)/shard_map/ppermute | solution.py:350
  94.1 8.6 %collective-permute-start.26 = (f32[1,32,256]{2,1,0:T(8,128)S(1)}, f32[1,32,256]{2,1,0:T(8,128)S(1)}, u32[]{:S(2)}, u32[]{:S(2)}) collective-permute-start(f32[1,32,256]{2,1,0:T(8,128)S(1)} %get-tuple-element.116), channel_id=1, source_target_pairs={{0,16},{16,32},{32,48},{48,64},{64,80},{80,96},{96,112},{112,128},... | collective-permute-start | bytes 98312 | tf_op jit(solution)/shard_map/ppermute | solution.py:350
  105.2 12.9 %collective-permute-start.31 = (f32[32,864]{1,0:T(8,128)S(1)}, f32[32,864]{1,0:T(8,128)S(1)}, u32[]{:S(2)}, u32[]{:S(2)}) collective-permute-start(f32[32,864]{1,0:T(8,128)S(1)} %get-tuple-element.132), channel_id=1, source_target_pairs={{0,16},{16,32},{32,48},{48,0},{64,80},{80,96},{96,112},{112,64},{1... | collective-permute-start | bytes 331784 | tf_op jit(solution)/shard_map/ppermute | solution.py:350
  105.3 17.1 %collective-permute-start.32 = (f32[32,864]{1,0:T(8,128)S(1)}, f32[32,864]{1,0:T(8,128)S(1)}, u32[]{:S(2)}, u32[]{:S(2)}) collective-permute-start(f32[32,864]{1,0:T(8,128)S(1)} %get-tuple-element.133), channel_id=1, source_target_pairs={{0,32},{16,48},{32,0},{48,16},{64,96},{80,112},{96,64},{112,80},{1... | collective-permute-start | bytes 331784 | tf_op jit(solution)/shard_map/ppermute | solution.py:350
  110.4 12.0 %collective-permute-start.33 = (f32[32,864]{1,0:T(8,128)S(1)}, f32[32,864]{1,0:T(8,128)S(1)}, u32[]{:S(2)}, u32[]{:S(2)}) collective-permute-start(f32[32,864]{1,0:T(8,128)S(1)} %get-tuple-element.134), channel_id=1, source_target_pairs={{0,48},{16,0},{32,16},{48,32},{64,112},{80,64},{96,80},{112,96},{1... | collective-permute-start | bytes 331784 | tf_op jit(solution)/shard_map/ppermute | solution.py:350
  114.4 9.6 %collective-permute-start.28 = (f32[32,864]{1,0:T(8,128)S(1)}, f32[32,864]{1,0:T(8,128)S(1)}, u32[]{:S(2)}, u32[]{:S(2)}) collective-permute-start(f32[32,864]{1,0:T(8,128)S(1)} %get-tuple-element.129), channel_id=1, source_target_pairs={{0,16},{16,32},{32,48},{48,0},{64,80},{80,96},{96,112},{112,64},{1... | collective-permute-start | bytes 331784 | tf_op jit(solution)/shard_map/ppermute | solution.py:350
  114.5 11.9 %collective-permute-start.29 = (f32[32,864]{1,0:T(8,128)S(1)}, f32[32,864]{1,0:T(8,128)S(1)}, u32[]{:S(2)}, u32[]{:S(2)}) collective-permute-start(f32[32,864]{1,0:T(8,128)S(1)} %get-tuple-element.130), channel_id=1, source_target_pairs={{0,32},{16,48},{32,0},{48,16},{64,96},{80,112},{96,64},{112,80},{1... | collective-permute-start | bytes 331784 | tf_op jit(solution)/shard_map/ppermute | solution.py:350
  (15 other events, 131.4 us)

commit v7 on v6

--- a/solution.py
+++ b/solution.py
@@ -420,11 +420,11 @@
 
     def second_sum(far, near, _):
         parts = lax.optimization_barrier((*second_parts, near))[:4]
-        one, three = to_row(parts[1], 1), to_row(parts[3], 3)
-        two = to_row(after(parts[2], [one, three]), 2)
+        two = to_row(parts[2], 2)
+        one, three = to_row(after(parts[1], [two]), 1), to_row(after(parts[3], [two]), 3)
         halves = input_halves(1, after(saved, [far]), before, behind, "first_input")
         w1 = weight_halves(after(turn, [far]), weight_first, "first_weights")
-        return ([parts[0], one, two, three], halves, w1), [one, three, *halves, *w1]
+        return ([parts[0], one, two, three], halves, w1), [two, *halves, *w1]
 
     pieces, (second_rows, inputs, w1) = gathered(first_grad, second_parts, second_sum)
     halves, (part_2, part_1) = first_use(

time: 129 us -> 134 us (1.039)
  starting transfers between devices: 62.3 us -> 68.3 us
  waiting for transfers between devices: 26.2 us -> 24.7 us
    ppermute x34, starting transfers between devices: 62.3 us -> 68.3 us  [send(): return lax.ppermute(value, axis, moves)]
    ppermute x34, waiting for transfers between devices: 26.2 us -> 24.7 us  [send(): return lax.ppermute(value, axis, moves)]
  transfers between devices with their start and end apart: 34 -> 34, of which waited for: 12 -> 12; matrix products, arithmetic and copies ran while one was open for 4% -> 4% of each run, Pallas kernels for 21% -> 20%
where the time goes in v7:
time: 134 us; the launch traced here: 132 us
  starting transfers between devices  68.3 us (51%)
  Pallas kernels  30.6 us (23%)
  waiting for transfers between devices  24.7 us (18%)
  local copies, waits for them, and re-layouts  4.49 us (3%)
  other arithmetic  2.84 us (2%)
    ppermute x34, starting transfers between devices, send(): return lax.ppermute(value, axis, moves)  68.3 us
    pallas_call x17, Pallas kernels, call(): pl.pallas_call(kernel, out_shape=out_shape, in_specs=[SM] * n_smem + [VM]...  30.6 us
    ppermute x34, waiting for transfers between devices, send(): return lax.ppermute(value, axis, moves)  24.7 us
    unnamed x13, local copies, waits for them, and re-layouts  2.92 us
  transfers between devices with their start and end apart: 34, of which 12 were waited for; matrix products, arithmetic and copies ran while one was open for 4% of the time, Pallas kernels for 20%

profile of v7, /device:TPU:8, one launch (start us, length us, event | category | flops | bytes accessed | tf_op | source)
XLA Modules:
  0.0 131.8 jit_solution(14429722721043840889)
XLA Ops:
  1.7 7.3 %collective-permute-start.3 = (f32[6,32,256]{2,1,0:T(8,128)S(1)}, f32[6,32,256]{2,1,0:T(8,128)S(1)}, u32[]{:S(2)}, u32[]{:S(2)}) collective-permute-start(f32[6,32,256]{2,1,0:T(8,128)S(1)} %fusion.5.refs_1_), channel_id=1, source_target_pairs={{0,8},{1,9},{2,10},{3,11},{4,12},{5,13},{6,14},{7,15},{8,0},{9,1},... | collective-permute-start | bytes 589832 | tf_op jit(solution)/shard_map/ppermute | solution.py:350
  9.0 3.0 %collective-permute-start.2 = (f32[6,32,256]{2,1,0:T(8,128)S(1)}, f32[6,32,256]{2,1,0:T(8,128)S(1)}, u32[]{:S(2)}, u32[]{:S(2)}) collective-permute-start(f32[6,32,256]{2,1,0:T(8,128)S(1)} %fusion.5.refs_1_), channel_id=1, source_target_pairs={{0,4},{1,5},{2,6},{3,7},{4,0},{5,1},{6,2},{7,3},{8,12},{9,13},{10,... | collective-permute-start | bytes 589832 | tf_op jit(solution)/shard_map/ppermute | solution.py:350
  15.5 5.7 %collective-permute-done.1.refs_3_ = f32[6,32,256]{2,1,0:T(8,128)S(1)} collective-permute-done((f32[6,32,256]{2,1,0:T(8,128)S(1)}, f32[6,32,256]{2,1,0:T(8,128)S(1)}, u32[]{:S(2)}, u32[]{:S(2)}) %collective-permute-start.1) | collective-permute-done | bytes 196640 | tf_op jit(solution)/shard_map/ppermute | solution.py:350
  21.4 2.7 %collective-permute-start.6 = (f32[6,32,256]{2,1,0:T(8,128)S(1)}, f32[6,32,256]{2,1,0:T(8,128)S(1)}, u32[]{:S(2)}, u32[]{:S(2)}) collective-permute-start(f32[6,32,256]{2,1,0:T(8,128)S(1)} %collective-permute-done.3.refs_5_), channel_id=1, source_target_pairs={{0,4},{1,5},{2,6},{3,7},{4,0},{5,1},{6,2},{7,3},{8,12},{9,13},{10,... | collective-permute-start | bytes 589832 | tf_op jit(solution)/shard_map/ppermute | solution.py:350
  27.8 6.0 %collective-permute-done.4.refs_6_ = f32[6,32,256]{2,1,0:T(8,128)S(1)} collective-permute-done((f32[6,32,256]{2,1,0:T(8,128)S(1)}, f32[6,32,256]{2,1,0:T(8,128)S(1)}, u32[]{:S(2)}, u32[]{:S(2)}) %collective-permute-start.4) | collective-permute-done | bytes 196640 | tf_op jit(solution)/shard_map/ppermute | solution.py:350
  38.5 2.6 %second_outer.1 = (bf16[16,32,1536]{2,1,0:T(8,128)(2,1)S(1)}, bf16[16,32,1536]{2,1,0:T(8,128)(2,1)S(1)}, f32[3,32,256]{2,1,0:T(8,128)S(1)}, f32[3,32,256]{2,1,0:T(8,128)S(1)}) custom-call(s32[16]{0:T(128)S(1)} %fusion.6.refs_0_, f32[6,32,256]{2,1,0:T(8,128)S(1)} %fusion.5.refs_1_, f32[6,32,256]{2,1,0:T(8,128)S(1)} %collective-permute-done.refs_2_, ...), custom_call_target="tpu_custom_call" | custom-call | flops 452984832 | bytes 7798848 | tf_op jit(solution)/shard_map/second_outer/pallas_call | solution.py:29
  41.1 2.9 %collective-permute-start.9 = (f32[3,32,256]{2,1,0:T(8,128)S(1)}, f32[3,32,256]{2,1,0:T(8,128)S(1)}, u32[]{:S(2)}, u32[]{:S(2)}) collective-permute-start(f32[3,32,256]{2,1,0:T(8,128)S(1)} %get-tuple-element.84), channel_id=1, source_target_pairs={{0,16},{16,32},{32,48},{48,64},{64,80},{80,96},{96,112},{112,128},... | collective-permute-start | bytes 294920 | tf_op jit(solution)/shard_map/ppermute | solution.py:350
  44.1 5.6 %collective-permute-start.10 = (f32[3,32,256]{2,1,0:T(8,128)S(1)}, f32[3,32,256]{2,1,0:T(8,128)S(1)}, u32[]{:S(2)}, u32[]{:S(2)}) collective-permute-start(f32[3,32,256]{2,1,0:T(8,128)S(1)} %get-tuple-element.85), channel_id=1, source_target_pairs={{16,0},{32,16},{48,32},{64,48},{80,64},{96,80},{112,96},{128,112},... | collective-permute-start | bytes 294920 | tf_op jit(solution)/shard_map/ppermute | solution.py:350
  49.7 4.0 %second_inner.1.own = f32[6,32,256]{2,1,0:T(8,128)S(1)} custom-call(bf16[16,32,1536]{2,1,0:T(8,128)(2,1)S(1)} %get-tuple-element.80.g_hi.refs_0_, bf16[16,32,1536]{2,1,0:T(8,128)(2,1)S(1)} %get-tuple-element.81.g_lo.refs_1_, bf16[288,512]{1,0:T(8,128)(2,1)S(1)} %get-tuple-element.76.refs_12_.refs_0_, ...), custom_call_target="tpu_custom_call" | custom-call | flops 4076863488 | bytes 5111808 | tf_op jit(solution)/shard_map/second_inner/pallas_call | solution.py:29
  54.9 2.2 %collective-permute-start.13 = (f32[6,32,256]{2,1,0:T(8,128)S(1)}, f32[6,32,256]{2,1,0:T(8,128)S(1)}, u32[]{:S(2)}, u32[]{:S(2)}) collective-permute-start(f32[6,32,256]{2,1,0:T(8,128)S(1)} %first_grad.1.refs_1_), channel_id=1, source_target_pairs={{0,4},{1,5},{2,6},{3,7},{4,0},{5,1},{6,2},{7,3},{8,12},{9,13},{10,... | collective-permute-start | bytes 589832 | tf_op jit(solution)/shard_map/ppermute | solution.py:350
  60.7 4.3 %second_filter.1 = (f32[864,128]{1,0:T(8,128)S(1)}, f32[864,128]{1,0:T(8,128)S(1)}, f32[864,128]{1,0:T(8,128)S(1)}, f32[864,128]{1,0:T(8,128)S(1)}) custom-call(bf16[16,32,1536]{2,1,0:T(8,128)(2,1)S(1)} %get-tuple-element.80.g_hi.refs_0_, bf16[16,32,1536]{2,1,0:T(8,128)(2,1)S(1)} %get-tuple-element.81.g_lo.refs_1_, ...), custom_call_target="tpu_custom_call" | custom-call | flops 4076863488 | bytes 7274496 | tf_op jit(solution)/shard_map/second_filter/pallas_call | solution.py:29
  66.8 2.4 %collective-permute-start.19 = (f32[864,128]{1,0:T(8,128)S(1)}, f32[864,128]{1,0:T(8,128)S(1)}, u32[]{:S(2)}, u32[]{:S(2)}) collective-permute-start(f32[864,128]{1,0:T(8,128)S(1)} %get-tuple-element.94), channel_id=1, source_target_pairs={{0,128},{16,144},{32,160},{48,176},{64,192},{80,208},{96,224},{112... | collective-permute-start | bytes 1327112 | tf_op jit(solution)/shard_map/ppermute | solution.py:350
  69.2 2.1 %collective-permute-start.17 = (f32[6,32,256]{2,1,0:T(8,128)S(1)}, f32[6,32,256]{2,1,0:T(8,128)S(1)}, u32[]{:S(2)}, u32[]{:S(2)}) collective-permute-start(f32[6,32,256]{2,1,0:T(8,128)S(1)} %collective-permute-done.14.refs_5_), channel_id=1, source_target_pairs={{0,4},{1,5},{2,6},{3,7},{4,0},{5,1},{6,2},{7,3},{8,12},{9,13},{10,... | collective-permute-start | bytes 589832 | tf_op jit(solution)/shard_map/ppermute | solution.py:350
  75.9 2.4 %collective-permute-done.17.refs_8_ = f32[6,32,256]{2,1,0:T(8,128)S(1)} collective-permute-done((f32[6,32,256]{2,1,0:T(8,128)S(1)}, f32[6,32,256]{2,1,0:T(8,128)S(1)}, u32[]{:S(2)}, u32[]{:S(2)}) %collective-permute-start.17) | collective-permute-done | bytes 196640 | tf_op jit(solution)/shard_map/ppermute | solution.py:350
  81.0 2.0 %collective-permute-start.25 = (f32[864,128]{1,0:T(8,128)S(1)}, f32[864,128]{1,0:T(8,128)S(1)}, u32[]{:S(2)}, u32[]{:S(2)}) collective-permute-start(f32[864,128]{1,0:T(8,128)S(1)} %get-tuple-element.116), channel_id=1, source_target_pairs={{0,192},{16,208},{32,224},{48,240},{64,0},{80,16},{96,32},{112,48}... | collective-permute-start | bytes 1327112 | tf_op jit(solution)/shard_map/ppermute | solution.py:350
  83.2 3.1 %first_filter.1 = (bf16[16,32,1536]{2,1,0:T(8,128)(2,1)S(1)}, bf16[16,32,1536]{2,1,0:T(8,128)(2,1)S(1)}, f32[864,128]{1,0:T(8,128)S(1)}, f32[864,128]{1,0:T(8,128)S(1)}) custom-call(s32[16]{0:T(128)S(1)} %fusion.6.refs_0_, f32[6,32,256]{2,1,0:T(8,128)S(1)} %first_grad.1.refs_1_, f32[6,32,256]{2,1,0:T(8,128)S(1)} %collective-permute-done.11.refs_2_, ...), custom_call_target="tpu_custom_call" | custom-call | flops 2038431744 | bytes 9535552 | tf_op jit(solution)/shard_map/first_filter/pallas_call | solution.py:29
  86.5 4.4 %collective-permute-start.22 = (f32[864,128]{1,0:T(8,128)S(1)}, f32[864,128]{1,0:T(8,128)S(1)}, u32[]{:S(2)}, u32[]{:S(2)}) collective-permute-start(f32[864,128]{1,0:T(8,128)S(1)} %get-tuple-element.110), channel_id=1, source_target_pairs={{0,128},{16,144},{32,160},{48,176},{64,192},{80,208},{96,224},{112... | collective-permute-start | bytes 1327112 | tf_op jit(solution)/shard_map/ppermute | solution.py:350
  90.9 2.3 %first_filter_rest.1 = (f32[864,128]{1,0:T(8,128)S(1)}, f32[864,128]{1,0:T(8,128)S(1)}) custom-call(bf16[16,32,1536]{2,1,0:T(8,128)(2,1)S(1)} %get-tuple-element.130.refs_0_.g_hi, bf16[16,32,1536]{2,1,0:T(8,128)(2,1)S(1)} %get-tuple-element.107.refs_1_.g_lo, bf16[288,2048]{1,0:T(8,128)(2,1)S(1)} %get-tuple-element.96.refs_11_.refs_2_, ...), custom_call_target="tpu_custom_call" | custom-call | flops 2038431744 | bytes 6389760 | tf_op jit(solution)/shard_map/first_filter_rest/pallas_call | solution.py:29
  94.0 1.9 %collective-permute-start.26 = (f32[1,32,256]{2,1,0:T(8,128)S(1)}, f32[1,32,256]{2,1,0:T(8,128)S(1)}, u32[]{:S(2)}, u32[]{:S(2)}) collective-permute-start(f32[1,32,256]{2,1,0:T(8,128)S(1)} %get-tuple-element.118), channel_id=1, source_target_pairs={{0,16},{16,32},{32,48},{48,64},{64,80},{80,96},{96,112},{112,128},... | collective-permute-start | bytes 98312 | tf_op jit(solution)/shard_map/ppermute | solution.py:350
  96.0 13.1 %collective-permute-start.27 = (f32[1,32,256]{2,1,0:T(8,128)S(1)}, f32[1,32,256]{2,1,0:T(8,128)S(1)}, u32[]{:S(2)}, u32[]{:S(2)}) collective-permute-start(f32[1,32,256]{2,1,0:T(8,128)S(1)} %get-tuple-element.119), channel_id=1, source_target_pairs={{16,0},{32,16},{48,32},{64,48},{80,64},{96,80},{112,96},{128,112},... | collective-permute-start | bytes 98312 | tf_op jit(solution)/shard_map/ppermute | solution.py:350
  111.8 3.7 %collective-permute-start.33 = (f32[32,864]{1,0:T(8,128)S(1)}, f32[32,864]{1,0:T(8,128)S(1)}, u32[]{:S(2)}, u32[]{:S(2)}) collective-permute-start(f32[32,864]{1,0:T(8,128)S(1)} %get-tuple-element.136), channel_id=1, source_target_pairs={{0,48},{16,0},{32,16},{48,32},{64,112},{80,64},{96,80},{112,96},{1... | collective-permute-start | bytes 331784 | tf_op jit(solution)/shard_map/ppermute | solution.py:350
  118.6 2.8 %collective-permute-start.30 = (f32[32,864]{1,0:T(8,128)S(1)}, f32[32,864]{1,0:T(8,128)S(1)}, u32[]{:S(2)}, u32[]{:S(2)}) collective-permute-start(f32[32,864]{1,0:T(8,128)S(1)} %get-tuple-element.133), channel_id=1, source_target_pairs={{0,48},{16,0},{32,16},{48,32},{64,112},{80,64},{96,80},{112,96},{1... | collective-permute-start | bytes 331784 | tf_op jit(solution)/shard_map/ppermute | solution.py:350
  121.4 4.0 %first_inner.1.own = f32[6,32,256]{2,1,0:T(8,128)S(1)} custom-call(bf16[16,32,1536]{2,1,0:T(8,128)(2,1)S(1)} %get-tuple-element.130.refs_0_.g_hi, bf16[16,32,1536]{2,1,0:T(8,128)(2,1)S(1)} %get-tuple-element.107.refs_1_.g_lo, bf16[288,512]{1,0:T(8,128)(2,1)S(1)} %get-tuple-element.99.refs_0_, bf16[288,512]{1,0:T(8,128)(2,1)S(1)} %get-tuple-element.100.refs_1_, ...), custom_call_target="tpu_custom_call" | custom-call | flops 4076863488 | bytes 5111808 | tf_op jit(solution)/shard_map/first_inner/pallas_call | solution.py:29
  127.1 3.8 %collective-permute-done.29.refs_2_ = f32[32,864]{1,0:T(8,128)S(1)} collective-permute-done((f32[32,864]{1,0:T(8,128)S(1)}, f32[32,864]{1,0:T(8,128)S(1)}, u32[]{:S(2)}, u32[]{:S(2)}) %collective-permute-start.29) | collective-permute-done | bytes 110624 | tf_op jit(solution)/shard_map/ppermute | solution.py:350
  (85 shorter events, 36.4 us)
Async XLA Ops:
  1.7 13.7 %collective-permute-start.3 = (f32[6,32,256]{2,1,0:T(8,128)S(1)}, f32[6,32,256]{2,1,0:T(8,128)S(1)}, u32[]{:S(2)}, u32[]{:S(2)}) collective-permute-start(f32[6,32,256]{2,1,0:T(8,128)S(1)} %fusion.5.refs_1_), channel_id=1, source_target_pairs={{0,8},{1,9},{2,10},{3,11},{4,12},{5,13},{6,14},{7,15},{8,0},{9,1},... | collective-permute-start | bytes 589832 | tf_op jit(solution)/shard_map/ppermute | solution.py:350
  9.0 17.1 %collective-permute-start.2 = (f32[6,32,256]{2,1,0:T(8,128)S(1)}, f32[6,32,256]{2,1,0:T(8,128)S(1)}, u32[]{:S(2)}, u32[]{:S(2)}) collective-permute-start(f32[6,32,256]{2,1,0:T(8,128)S(1)} %fusion.5.refs_1_), channel_id=1, source_target_pairs={{0,4},{1,5},{2,6},{3,7},{4,0},{5,1},{6,2},{7,3},{8,12},{9,13},{10,... | collective-permute-start | bytes 589832 | tf_op jit(solution)/shard_map/ppermute | solution.py:350
  21.4 13.8 %collective-permute-start.6 = (f32[6,32,256]{2,1,0:T(8,128)S(1)}, f32[6,32,256]{2,1,0:T(8,128)S(1)}, u32[]{:S(2)}, u32[]{:S(2)}) collective-permute-start(f32[6,32,256]{2,1,0:T(8,128)S(1)} %collective-permute-done.3.refs_5_), channel_id=1, source_target_pairs={{0,4},{1,5},{2,6},{3,7},{4,0},{5,1},{6,2},{7,3},{8,12},{9,13},{10,... | collective-permute-start | bytes 589832 | tf_op jit(solution)/shard_map/ppermute | solution.py:350
  24.1 10.4 %collective-permute-start.5 = (f32[6,32,256]{2,1,0:T(8,128)S(1)}, f32[6,32,256]{2,1,0:T(8,128)S(1)}, u32[]{:S(2)}, u32[]{:S(2)}) collective-permute-start(f32[6,32,256]{2,1,0:T(8,128)S(1)} %collective-permute-done.3.refs_5_), channel_id=1, source_target_pairs={{0,6},{1,7},{2,0},{3,1},{4,2},{5,3},{6,4},{7,5},{8,14},{9,15},{10,... | collective-permute-start | bytes 589832 | tf_op jit(solution)/shard_map/ppermute | solution.py:350
  27.1 11.0 %collective-permute-start.7 = (f32[24,32,256]{2,1,0:T(8,128)}, f32[24,32,256]{2,1,0:T(8,128)}, u32[]{:S(2)}, u32[]{:S(2)}) collective-permute-start(f32[24,32,256]{2,1,0:T(8,128)} %pad_maximum_fusion), channel_id=1, source_target_pairs={{0,1},{1,0},{2,3},{3,2},{4,5},{5,4},{6,7},{7,6},{8,9},{9,8},{10,11... | collective-permute-start | bytes 2359304 | tf_op jit(solution)/shard_map/ppermute | solution.py:350
  41.1 12.6 %collective-permute-start.9 = (f32[3,32,256]{2,1,0:T(8,128)S(1)}, f32[3,32,256]{2,1,0:T(8,128)S(1)}, u32[]{:S(2)}, u32[]{:S(2)}) collective-permute-start(f32[3,32,256]{2,1,0:T(8,128)S(1)} %get-tuple-element.84), channel_id=1, source_target_pairs={{0,16},{16,32},{32,48},{48,64},{64,80},{80,96},{96,112},{112,128},... | collective-permute-start | bytes 294920 | tf_op jit(solution)/shard_map/ppermute | solution.py:350
  44.1 9.7 %collective-permute-start.10 = (f32[3,32,256]{2,1,0:T(8,128)S(1)}, f32[3,32,256]{2,1,0:T(8,128)S(1)}, u32[]{:S(2)}, u32[]{:S(2)}) collective-permute-start(f32[3,32,256]{2,1,0:T(8,128)S(1)} %get-tuple-element.85), channel_id=1, source_target_pairs={{16,0},{32,16},{48,32},{64,48},{80,64},{96,80},{112,96},{128,112},... | collective-permute-start | bytes 294920 | tf_op jit(solution)/shard_map/ppermute | solution.py:350
  53.8 15.4 %collective-permute-start.14 = (f32[6,32,256]{2,1,0:T(8,128)S(1)}, f32[6,32,256]{2,1,0:T(8,128)S(1)}, u32[]{:S(2)}, u32[]{:S(2)}) collective-permute-start(f32[6,32,256]{2,1,0:T(8,128)S(1)} %first_grad.1.refs_1_), channel_id=1, source_target_pairs={{0,8},{1,9},{2,10},{3,11},{4,12},{5,13},{6,14},{7,15},{8,0},{9,1},... | collective-permute-start | bytes 589832 | tf_op jit(solution)/shard_map/ppermute | solution.py:350
  54.9 10.1 %collective-permute-start.13 = (f32[6,32,256]{2,1,0:T(8,128)S(1)}, f32[6,32,256]{2,1,0:T(8,128)S(1)}, u32[]{:S(2)}, u32[]{:S(2)}) collective-permute-start(f32[6,32,256]{2,1,0:T(8,128)S(1)} %first_grad.1.refs_1_), channel_id=1, source_target_pairs={{0,4},{1,5},{2,6},{3,7},{4,0},{5,1},{6,2},{7,3},{8,12},{9,13},{10,... | collective-permute-start | bytes 589832 | tf_op jit(solution)/shard_map/ppermute | solution.py:350
  66.8 14.0 %collective-permute-start.19 = (f32[864,128]{1,0:T(8,128)S(1)}, f32[864,128]{1,0:T(8,128)S(1)}, u32[]{:S(2)}, u32[]{:S(2)}) collective-permute-start(f32[864,128]{1,0:T(8,128)S(1)} %get-tuple-element.94), channel_id=1, source_target_pairs={{0,128},{16,144},{32,160},{48,176},{64,192},{80,208},{96,224},{112... | collective-permute-start | bytes 1327112 | tf_op jit(solution)/shard_map/ppermute | solution.py:350
  69.2 9.2 %collective-permute-start.17 = (f32[6,32,256]{2,1,0:T(8,128)S(1)}, f32[6,32,256]{2,1,0:T(8,128)S(1)}, u32[]{:S(2)}, u32[]{:S(2)}) collective-permute-start(f32[6,32,256]{2,1,0:T(8,128)S(1)} %collective-permute-done.14.refs_5_), channel_id=1, source_target_pairs={{0,4},{1,5},{2,6},{3,7},{4,0},{5,1},{6,2},{7,3},{8,12},{9,13},{10,... | collective-permute-start | bytes 589832 | tf_op jit(solution)/shard_map/ppermute | solution.py:350
  73.4 9.7 %collective-permute-start.18 = (f32[24,32,256]{2,1,0:T(8,128)S(1)}, f32[24,32,256]{2,1,0:T(8,128)S(1)}, u32[]{:S(2)}, u32[]{:S(2)}) collective-permute-start(f32[24,32,256]{2,1,0:T(8,128)S(1)} %pad_maximum_fusion.1), channel_id=1, source_target_pairs={{0,1},{1,0},{2,3},{3,2},{4,5},{5,4},{6,7},{7,6},{8,9},{9,8},{10,11... | collective-permute-start | bytes 2359304 | tf_op jit(solution)/shard_map/ppermute | solution.py:350
  80.9 13.1 %collective-permute-start.24 = (f32[864,128]{1,0:T(8,128)S(1)}, f32[864,128]{1,0:T(8,128)S(1)}, u32[]{:S(2)}, u32[]{:S(2)}) collective-permute-start(f32[864,128]{1,0:T(8,128)S(1)} %get-tuple-element.114), channel_id=1, source_target_pairs={{0,64},{16,80},{32,96},{48,112},{64,128},{80,144},{96,160},{112,17... | collective-permute-start | bytes 1327112 | tf_op jit(solution)/shard_map/ppermute | solution.py:350
  81.0 14.9 %collective-permute-start.25 = (f32[864,128]{1,0:T(8,128)S(1)}, f32[864,128]{1,0:T(8,128)S(1)}, u32[]{:S(2)}, u32[]{:S(2)}) collective-permute-start(f32[864,128]{1,0:T(8,128)S(1)} %get-tuple-element.116), channel_id=1, source_target_pairs={{0,192},{16,208},{32,224},{48,240},{64,0},{80,16},{96,32},{112,48}... | collective-permute-start | bytes 1327112 | tf_op jit(solution)/shard_map/ppermute | solution.py:350
  86.3 25.5 %collective-permute-start.21 = (f32[864,128]{1,0:T(8,128)S(1)}, f32[864,128]{1,0:T(8,128)S(1)}, u32[]{:S(2)}, u32[]{:S(2)}) collective-permute-start(f32[864,128]{1,0:T(8,128)S(1)} %get-tuple-element.109), channel_id=1, source_target_pairs={{0,64},{16,80},{32,96},{48,112},{64,128},{80,144},{96,160},{112,17... | collective-permute-start | bytes 1327112 | tf_op jit(solution)/shard_map/ppermute | solution.py:350
  86.5 29.1 %collective-permute-start.22 = (f32[864,128]{1,0:T(8,128)S(1)}, f32[864,128]{1,0:T(8,128)S(1)}, u32[]{:S(2)}, u32[]{:S(2)}) collective-permute-start(f32[864,128]{1,0:T(8,128)S(1)} %get-tuple-element.110), channel_id=1, source_target_pairs={{0,128},{16,144},{32,160},{48,176},{64,192},{80,208},{96,224},{112... | collective-permute-start | bytes 1327112 | tf_op jit(solution)/shard_map/ppermute | solution.py:350
  93.1 22.4 %collective-permute-start.23 = (f32[864,128]{1,0:T(8,128)S(1)}, f32[864,128]{1,0:T(8,128)S(1)}, u32[]{:S(2)}, u32[]{:S(2)}) collective-permute-start(f32[864,128]{1,0:T(8,128)S(1)} %get-tuple-element.111), channel_id=1, source_target_pairs={{0,192},{16,208},{32,224},{48,240},{64,0},{80,16},{96,32},{112,48}... | collective-permute-start | bytes 1327112 | tf_op jit(solution)/shard_map/ppermute | solution.py:350
  94.0 15.1 %collective-permute-start.26 = (f32[1,32,256]{2,1,0:T(8,128)S(1)}, f32[1,32,256]{2,1,0:T(8,128)S(1)}, u32[]{:S(2)}, u32[]{:S(2)}) collective-permute-start(f32[1,32,256]{2,1,0:T(8,128)S(1)} %get-tuple-element.118), channel_id=1, source_target_pairs={{0,16},{16,32},{32,48},{48,64},{64,80},{80,96},{96,112},{112,128},... | collective-permute-start | bytes 98312 | tf_op jit(solution)/shard_map/ppermute | solution.py:350
  96.0 14.9 %collective-permute-start.27 = (f32[1,32,256]{2,1,0:T(8,128)S(1)}, f32[1,32,256]{2,1,0:T(8,128)S(1)}, u32[]{:S(2)}, u32[]{:S(2)}) collective-permute-start(f32[1,32,256]{2,1,0:T(8,128)S(1)} %get-tuple-element.119), channel_id=1, source_target_pairs={{16,0},{32,16},{48,32},{64,48},{80,64},{96,80},{112,96},{128,112},... | collective-permute-start | bytes 98312 | tf_op jit(solution)/shard_map/ppermute | solution.py:350
  111.7 13.7 %collective-permute-start.32 = (f32[32,864]{1,0:T(8,128)S(1)}, f32[32,864]{1,0:T(8,128)S(1)}, u32[]{:S(2)}, u32[]{:S(2)}) collective-permute-start(f32[32,864]{1,0:T(8,128)S(1)} %get-tuple-element.135), channel_id=1, source_target_pairs={{0,32},{16,48},{32,0},{48,16},{64,96},{80,112},{96,64},{112,80},{1... | collective-permute-start | bytes 331784 | tf_op jit(solution)/shard_map/ppermute | solution.py:350
  111.8 13.6 %collective-permute-start.33 = (f32[32,864]{1,0:T(8,128)S(1)}, f32[32,864]{1,0:T(8,128)S(1)}, u32[]{:S(2)}, u32[]{:S(2)}) collective-permute-start(f32[32,864]{1,0:T(8,128)S(1)} %get-tuple-element.136), channel_id=1, source_target_pairs={{0,48},{16,0},{32,16},{48,32},{64,112},{80,64},{96,80},{112,96},{1... | collective-permute-start | bytes 331784 | tf_op jit(solution)/shard_map/ppermute | solution.py:350
  116.4 10.7 %collective-permute-start.28 = (f32[32,864]{1,0:T(8,128)S(1)}, f32[32,864]{1,0:T(8,128)S(1)}, u32[]{:S(2)}, u32[]{:S(2)}) collective-permute-start(f32[32,864]{1,0:T(8,128)S(1)} %get-tuple-element.131), channel_id=1, source_target_pairs={{0,16},{16,32},{32,48},{48,0},{64,80},{80,96},{96,112},{112,64},{1... | collective-permute-start | bytes 331784 | tf_op jit(solution)/shard_map/ppermute | solution.py:350
  117.0 13.8 %collective-permute-start.29 = (f32[32,864]{1,0:T(8,128)S(1)}, f32[32,864]{1,0:T(8,128)S(1)}, u32[]{:S(2)}, u32[]{:S(2)}) collective-permute-start(f32[32,864]{1,0:T(8,128)S(1)} %get-tuple-element.132), channel_id=1, source_target_pairs={{0,32},{16,48},{32,0},{48,16},{64,96},{80,112},{96,64},{112,80},{1... | collective-permute-start | bytes 331784 | tf_op jit(solution)/shard_map/ppermute | solution.py:350
  118.6 12.3 %collective-permute-start.30 = (f32[32,864]{1,0:T(8,128)S(1)}, f32[32,864]{1,0:T(8,128)S(1)}, u32[]{:S(2)}, u32[]{:S(2)}) collective-permute-start(f32[32,864]{1,0:T(8,128)S(1)} %get-tuple-element.133), channel_id=1, source_target_pairs={{0,48},{16,0},{32,16},{48,32},{64,112},{80,64},{96,80},{112,96},{1... | collective-permute-start | bytes 331784 | tf_op jit(solution)/shard_map/ppermute | solution.py:350
  (15 other events, 135.1 us)
